TPU v7x, 32 devices: a whole 2x2x4 slice. The times are simulated.
32 devices in a mesh: dp: 8 (over y, x, core), tensor: 4 (over z).
Axes of the slice: x: 2, y: 2, z: 4, core: 2. Of those that a mesh axis runs over, the one named last changes fastest.
Arguments:
- tokens: bfloat16 [2048, 3072], P('dp', 'tensor'), may hold values from -6 to 6
- blocks: bfloat16 [3, 3072, 3072], P(None, 'tensor'), may hold values from -0.125 to 0.125
- left_factor: bfloat16 [3072, 256], P('tensor'), may hold values from -0.109375 to 0.109375
- right_factor: bfloat16 [256, 12288], P(None, 'tensor'), may hold values from -0.375 to 0.375
- upstream: bfloat16 [2048, 12288], P('dp', 'tensor'), may hold values from -6 to 6
Outputs:
- activated: bfloat16 [2048, 12288], P('dp', 'tensor')
- token_grad: bfloat16 [2048, 3072], P('dp', 'tensor')
- left_grad: bfloat16 [3072, 256], P('tensor')
- right_grad: bfloat16 [256, 12288], P(None, 'tensor')
All inputs are finite; a program needn't handle non-finite values.
Results may differ from a plain program's by a relative error of at most 0.0063.
Values may be sent and summed in bfloat16 or wider, within the bound.
No kernel may reach another device: no remote copies, remote signals or barrier semaphores. Data moves between devices by JAX's collectives and lax.ppermute only.
A program may use at most 128 MiB of HBM per device.

v0:
```python
import jax
import jax.numpy as jnp
from jax import lax
from jax.sharding import PartitionSpec as P


def partner_2(block, axis, distance):
    count = lax.axis_size(axis)
    route = []
    for low in range(count):
        high = low | 1 << distance
        if high != low and high < count:
            route += [(low, high), (high, low)]
    return lax.ppermute(block, axis, route)


def across(left, right, left_dim, right_dim):
    return lax.dot_general(
        left, right, (((left_dim,), (right_dim,)), ((), ())), preferred_element_type=jnp.float32
    )


def body(tokens, blocks, left_factor, right_factor, upstream):
    levels = blocks.shape[0] - 1
    row_count = tokens.shape[0]
    low_part = jnp.dot(tokens, left_factor, preferred_element_type=jnp.float32)
    low_rank = lax.psum(low_part, "tensor").astype(jnp.bfloat16)
    preact = jnp.dot(tokens, blocks[0], preferred_element_type=jnp.float32)
    preact = preact + jnp.dot(low_rank, right_factor, preferred_element_type=jnp.float32)
    for bit_index in range(levels):
        partner = partner_2(tokens, "tensor", bit_index)
        preact = preact + jnp.dot(
            partner, blocks[bit_index + 1], preferred_element_type=jnp.float32
        )
    gelu_out, pullback = jax.vjp(jax.nn.gelu, preact)
    activated = gelu_out.astype(jnp.bfloat16)
    slopes = pullback(upstream.astype(jnp.float32))[0].astype(jnp.bfloat16)
    mixed_part = across(slopes, right_factor, 1, 1)
    mixed_rows = lax.psum(mixed_part, "tensor").astype(jnp.bfloat16)
    norm_scale = 1.0 / jnp.sqrt(jnp.float32(row_count * lax.axis_size("dp")))
    left_part = across(tokens, mixed_rows, 0, 0) * norm_scale
    running = across(slopes, blocks[0], 1, 1) + across(mixed_rows, left_factor, 1, 1)
    for bit_index in range(levels):
        partial_value = across(slopes, blocks[bit_index + 1], 1, 1)
        running = running + partner_2(partial_value, "tensor", bit_index)
    token_grad = running.astype(jnp.bfloat16)
    right_part = across(low_rank, slopes, 0, 0) * norm_scale
    left_total, right_total = lax.psum((left_part, right_part), "dp")
    return (
        activated,
        token_grad,
        left_total.astype(jnp.bfloat16),
        right_total.astype(jnp.bfloat16),
    )


def solution(mesh):
    placed = (
        P("dp", "tensor"),
        P(None, "tensor", None),
        P("tensor", None),
        P(None, "tensor"),
        P("dp", "tensor"),
    )
    return jax.shard_map(
        body,
        mesh=mesh,
        in_specs=placed,
        out_specs=(P("dp", "tensor"), P("dp", "tensor"), P("tensor", None), P(None, "tensor")),
        check_vma=False,
    )
```

profile of v0, /device:TPU:0, one launch (start us, length us, event | category | flops | bytes accessed | tf_op | source)
XLA Modules:
  0.0 177.9 jit_solution(4787316324550358948)
XLA Ops:
  0.6 0.0 copy-start
  0.6 3.1 %collective-permute-start = (bf16[256,768]{1,0:T(8,128)(2,1)}, bf16[256,768]{1,0:T(8,128)(2,1)S(1)}, u32[]{:S(2)}, u32[]{:S(2)}) collective-permute-start(bf16[256,768]{1,0:T(8,128)(2,1)} %param.5), channel_id=1, source_target_pairs={{0,1},{1,0},{2,3},{3,2},{4,5},{5,4},{6,7},{7,6},{8,9},{9,8},{10,11... | collective-permute-start | bytes 1179656 | tf_op jit(solution)/shard_map/ppermute | solution.py:14
  3.8 2.6 %collective-permute-start.1 = (bf16[256,768]{1,0:T(8,128)(2,1)}, bf16[256,768]{1,0:T(8,128)(2,1)S(1)}, u32[]{:S(2)}, u32[]{:S(2)}) collective-permute-start(bf16[256,768]{1,0:T(8,128)(2,1)} %param.5), channel_id=1, source_target_pairs={{0,2},{2,0},{1,3},{3,1},{4,6},{6,4},{5,7},{7,5},{8,10},{10,8},{9,1... | collective-permute-start | bytes 1179656 | tf_op jit(solution)/shard_map/ppermute | solution.py:14
  6.4 1.4 fusion.42
  7.7 32.0 %all-reduce.4 = bf16[256,256]{1,0:T(8,128)(2,1)S(1)} all-reduce(f32[256,256]{1,0:T(8,128)S(1)} %fusion.42), channel_id=1, replica_groups=mesh['dp'=8,'tensor'=4] {'tensor'}, use_global_device_ids=true, to_apply=%region_0.0 | all-reduce | flops 65536 | bytes 393216 | tf_op jit(solution)/shard_map/psum | solution.py:27
  39.8 0.0 copy-start.3
  39.8 0.0 copy-start.6
  39.8 4.0 %fusion.10 = f32[256,3072]{1,0:T(8,128)S(1)} fusion(bf16[256,768]{1,0:T(8,128)(2,1)} %param.5, bf16[3,768,3072]{2,1,0:T(8,128)(2,1)} %param.6), kind=kOutput, calls=%fused_computation.10 | convolution fusion | flops 1207959552 | bytes 8257536 | tf_op jit(solution)/shard_map/dot_general | solution.py:28
  43.8 0.0 copy-done.3
  43.8 0.0 copy-done
  43.8 0.6 convolution_add_fusion
  44.4 0.0 copy-start.7
  44.5 0.0 collective-permute-done.1
  44.5 1.9 %copy-done.6 = bf16[3,768,3072]{2,1,0:T(8,128)(2,1)S(1)} copy-done((bf16[3,768,3072]{2,1,0:T(8,128)(2,1)S(1)}, bf16[3,768,3072]{2,1,0:T(8,128)(2,1)}, u32[]{:S(2)}) %copy-start.6) | copy-done | bytes 14155800
  46.4 1.5 fusion.2
  47.8 0.0 collective-permute-done
  47.8 0.0 copy-done.7
  47.8 4.9 %fusion.26 = (bf16[256,3072]{1,0:T(8,128)(2,1)S(1)}, bf16[256,3072]{1,0:T(8,128)(2,1)}) fusion(bf16[256,3072]{1,0:T(8,128)(2,1)S(1)} %copy-done.7, f32[256,3072]{1,0:T(8,128)S(1)} %fusion.2, f32[256,3072]{1,0:T(8,128)S(1)} %convolution_add_fusion, bf16[256,768]{1,0:T(8,128)(2,1)S(1)} %collective-permute-done, bf16[3,768,3072]{2,1,0:T(8,128)(2,1)S(1)} %copy-done.6), kind=kOutput, calls=%fused_computation.28 | convolution fusion | flops 1227620352 | bytes 16121856 | tf_op jit(solution)/shard_map/dot_general | solution.py:32
  52.7 1.3 fusion.43
  54.0 2.3 %fusion = f32[256,768]{1,0:T(8,128)} fusion(bf16[256,3072]{1,0:T(8,128)(2,1)S(1)} %get-tuple-element.10, bf16[3,768,3072]{2,1,0:T(8,128)(2,1)S(1)} %copy-done.6), kind=kOutput, calls=%fused_computation | convolution fusion | flops 1207959552 | bytes 7077888 | tf_op jit(solution)/shard_map/dot_general | solution.py:18
  56.3 0.0 copy-start.4
  56.4 2.3 %fusion.4 = f32[256,768]{1,0:T(8,128)} fusion(bf16[256,3072]{1,0:T(8,128)(2,1)S(1)} %get-tuple-element.10, bf16[3,768,3072]{2,1,0:T(8,128)(2,1)S(1)} %copy-done.6), kind=kOutput, calls=%fused_computation.4 | convolution fusion | flops 1207959552 | bytes 7077888 | tf_op jit(solution)/shard_map/dot_general | solution.py:18
  58.7 0.0 copy-done.4
  58.7 0.0 copy-start.2
  58.7 2.3 %convolution_multiply_fusion = f32[256,3072]{1,0:T(8,128)} fusion(bf16[256,3072]{1,0:T(8,128)(2,1)S(1)} %get-tuple-element.10, bf16[256,256]{1,0:T(8,128)(2,1)S(1)} %copy-done.4), kind=kOutput, calls=%fused_computation.20 | convolution fusion | flops 403439616 | bytes 4849664 | tf_op jit(solution)/shard_map/dot_general | solution.py:18
  60.9 23.4 %all-reduce.5 = bf16[256,256]{1,0:T(8,128)(2,1)} all-reduce(f32[256,256]{1,0:T(8,128)} %fusion.43), channel_id=1, replica_groups=mesh['dp'=8,'tensor'=4] {'tensor'}, use_global_device_ids=true, to_apply=%region_1.0 | all-reduce | flops 65536 | bytes 393216 | tf_op jit(solution)/shard_map/psum | solution.py:39
  84.4 0.0 copy-done.2
  84.4 2.1 %fusion.34 = f32[768,256]{0,1:T(8,128)} fusion(bf16[256,768]{1,0:T(8,128)(2,1)S(1)} %copy-done.2, bf16[256,256]{1,0:T(8,128)(2,1)} %all-reduce.5), kind=kOutput, calls=%fused_computation.38 | convolution fusion | flops 100859904 | bytes 1310720 | tf_op jit(solution)/shard_map/dot_general | solution.py:18
  86.4 0.0 collective-permute-start.2
  86.5 1.3 collective-permute-start.3
  87.7 83.0 %all-reduce.6 = (bf16[768,256]{0,1:T(8,128)(2,1)S(1)}, bf16[256,3072]{1,0:T(8,128)(2,1)}) all-reduce(f32[768,256]{0,1:T(8,128)} %fusion.34, f32[256,3072]{1,0:T(8,128)} %convolution_multiply_fusion), channel_id=1, replica_groups=mesh['dp'=8,'tensor'=4] {'dp'}, use_global_device_ids=true, to_apply=%region_2.0 | all-reduce | flops 983040 | bytes 5898240 | tf_op jit(solution)/shard_map/psum | solution.py:48
  170.7 0.9 copy.9
  171.6 0.0 copy-start.1
  171.6 0.0 copy-start.5
  171.6 3.8 %fusion.8 = f32[256,768]{1,0:T(8,128)S(1)} fusion(bf16[256,3072]{1,0:T(8,128)(2,1)S(1)} %get-tuple-element.10, bf16[3,768,3072]{2,1,0:T(8,128)(2,1)} %param.6), kind=kOutput, calls=%fused_computation.8 | convolution fusion | flops 1207959552 | bytes 7077888 | tf_op jit(solution)/shard_map/dot_general | solution.py:18
  175.5 0.0 collective-permute-done.2
  175.5 0.0 collective-permute-done.3
  175.5 0.0 copy-done.1
  175.5 0.0 copy-done.5
  175.5 2.4 %fusion.37 = bf16[256,768]{1,0:T(8,128)(2,1)} fusion(f32[256,768]{1,0:T(8,128)} %collective-permute-done.3, f32[256,768]{1,0:T(8,128)} %collective-permute-done.2, f32[256,768]{1,0:T(8,128)S(1)} %fusion.8, bf16[768,256]{1,0:T(8,128)(2,1)S(1)} %copy-done.1, bf16[256,256]{1,0:T(8,128)(2,1)S(1)} %copy-done.5), kind=kOutput, calls=%fused_computation.42 | convolution fusion | flops 101449728 | bytes 3276800 | tf_op jit(solution)/shard_map/dot_general | solution.py:18
Async XLA Ops:
  0.6 43.2 %copy-start = (bf16[256,3072]{1,0:T(8,128)(2,1)S(1)}, bf16[256,3072]{1,0:T(8,128)(2,1)}, u32[]{:S(2)}) copy-start(bf16[256,3072]{1,0:T(8,128)(2,1)} %param.8) | copy-start | bytes 4718596
  0.6 47.2 %collective-permute-start = (bf16[256,768]{1,0:T(8,128)(2,1)}, bf16[256,768]{1,0:T(8,128)(2,1)S(1)}, u32[]{:S(2)}, u32[]{:S(2)}) collective-permute-start(bf16[256,768]{1,0:T(8,128)(2,1)} %param.5), channel_id=1, source_target_pairs={{0,1},{1,0},{2,3},{3,2},{4,5},{5,4},{6,7},{7,6},{8,9},{9,8},{10,11... | collective-permute-start | bytes 1179656 | tf_op jit(solution)/shard_map/ppermute | solution.py:14
  3.8 40.7 %collective-permute-start.1 = (bf16[256,768]{1,0:T(8,128)(2,1)}, bf16[256,768]{1,0:T(8,128)(2,1)S(1)}, u32[]{:S(2)}, u32[]{:S(2)}) collective-permute-start(bf16[256,768]{1,0:T(8,128)(2,1)} %param.5), channel_id=1, source_target_pairs={{0,2},{2,0},{1,3},{3,1},{4,6},{6,4},{5,7},{7,5},{8,10},{10,8},{9,1... | collective-permute-start | bytes 1179656 | tf_op jit(solution)/shard_map/ppermute | solution.py:14
  39.8 4.0 %copy-start.3 = (bf16[256,256]{1,0:T(8,128)(2,1)}, bf16[256,256]{1,0:T(8,128)(2,1)S(1)}, u32[]{:S(2)}) copy-start(bf16[256,256]{1,0:T(8,128)(2,1)S(1)} %all-reduce.4) | copy-start | bytes 393220
  39.8 6.6 %copy-start.6 = (bf16[3,768,3072]{2,1,0:T(8,128)(2,1)S(1)}, bf16[3,768,3072]{2,1,0:T(8,128)(2,1)}, u32[]{:S(2)}) copy-start(bf16[3,768,3072]{2,1,0:T(8,128)(2,1)} %param.6) | copy-start | bytes 42467332
  44.4 3.4 %copy-start.7 = (bf16[256,3072]{1,0:T(8,128)(2,1)S(1)}, bf16[256,3072]{1,0:T(8,128)(2,1)}, u32[]{:S(2)}) copy-start(bf16[256,3072]{1,0:T(8,128)(2,1)} %param.9) | copy-start | bytes 4718596
  56.3 2.3 %copy-start.4 = (bf16[256,256]{1,0:T(8,128)(2,1)S(1)}, bf16[256,256]{1,0:T(8,128)(2,1)}, u32[]{:S(2)}) copy-start(bf16[256,256]{1,0:T(8,128)(2,1)} %copy-done.3) | copy-start | bytes 393220
  58.7 25.7 %copy-start.2 = (bf16[256,768]{1,0:T(8,128)(2,1)S(1)}, bf16[256,768]{1,0:T(8,128)(2,1)}, u32[]{:S(2)}) copy-start(bf16[256,768]{1,0:T(8,128)(2,1)} %param.5) | copy-start | bytes 1179652
  86.4 89.0 %collective-permute-start.2 = (f32[256,768]{1,0:T(8,128)}, f32[256,768]{1,0:T(8,128)}, u32[]{:S(2)}, u32[]{:S(2)}) collective-permute-start(f32[256,768]{1,0:T(8,128)} %fusion.4), channel_id=1, source_target_pairs={{0,1},{1,0},{2,3},{3,2},{4,5},{5,4},{6,7},{7,6},{8,9},{9,8},{10,11... | collective-permute-start | bytes 2359304 | tf_op jit(solution)/shard_map/ppermute | solution.py:14
  86.5 89.0 %collective-permute-start.3 = (f32[256,768]{1,0:T(8,128)}, f32[256,768]{1,0:T(8,128)}, u32[]{:S(2)}, u32[]{:S(2)}) collective-permute-start(f32[256,768]{1,0:T(8,128)} %fusion), channel_id=1, source_target_pairs={{0,2},{2,0},{1,3},{3,1},{4,6},{6,4},{5,7},{7,5},{8,10},{10,8},{9,1... | collective-permute-start | bytes 2359304 | tf_op jit(solution)/shard_map/ppermute | solution.py:14
  171.6 3.8 %copy-start.1 = (bf16[768,256]{1,0:T(8,128)(2,1)S(1)}, bf16[768,256]{1,0:T(8,128)(2,1)}, u32[]{:S(2)}) copy-start(bf16[768,256]{1,0:T(8,128)(2,1)} %param.7) | copy-start | bytes 1179652
  171.6 3.9 %copy-start.5 = (bf16[256,256]{1,0:T(8,128)(2,1)S(1)}, bf16[256,256]{1,0:T(8,128)(2,1)}, u32[]{:S(2)}) copy-start(bf16[256,256]{1,0:T(8,128)(2,1)} %all-reduce.5) | copy-start | bytes 393220
where the time goes:
time: 178 us
  blocking collectives  138 us (78%)
  matrix products  28.9 us (16%)
  starting transfers between devices  6.97 us (4%)
  local copies, waits for them, and re-layouts  2.86 us (2%)
    psum x1, blocking collectives, body(): left_total, right_total = lax.psum((left_part, right_part), 'dp')  83 us
    psum x1, blocking collectives, body(): low_rank = lax.psum(low_part, 'tensor').astype(jnp.bfloat16)  32 us
    psum x1, blocking collectives, body(): mixed_rows = lax.psum(mixed_part, 'tensor').astype(jnp.bfloat16)  23.4 us
    dot_general x7, matrix products, across(): lax.dot_general(left, right, (((left_dim,), (right_dim,)), ((), ())), pre...  16.5 us
    ppermute x4, starting transfers between devices, partner_2(): return lax.ppermute(block, axis, route)  6.97 us
    dot_general x2, matrix products, body(): jnp.dot(partner, blocks[bit_index + 1], preferred_element_type=jnp.float32)  6.33 us
    dot_general x1, matrix products, body(): preact = jnp.dot(tokens, blocks[0], preferred_element_type=jnp.float32)  3.99 us
  transfers between devices with their start and end apart: 4, of which 0 were waited for; matrix products, arithmetic and copies ran while one was open for 7% of the time, Pallas kernels for 0%

commit v1 on v0

v1 whole, which is shorter than its diff:
```python
import functools

import jax
import jax.numpy as jnp
from jax import lax
from jax.experimental import pallas as pl
from jax.experimental.pallas import tpu as pltpu
from jax.sharding import PartitionSpec as P


VMEM = pl.BlockSpec(memory_space=pltpu.VMEM)
SMEM = pl.BlockSpec(memory_space=pltpu.SMEM)
HBM = pl.BlockSpec(memory_space=pltpu.HBM)
MIB = 1 << 20


def swap(block, axes, partner):
    dp, tensor = lax.axis_size("dp"), lax.axis_size("tensor")
    if axes == "dp":
        route = [(i, partner(i, 0)) for i in range(dp)]
    else:
        axes = ("dp", "tensor")
        route = [(i * tensor + j, i * tensor + partner(i, j)) for i in range(dp) for j in range(tensor)]
    return lax.ppermute(block, axes, route)


def swap_tensor(block, step, levels):
    return swap(block, "tensor", lambda i, j: j ^ (1 << (levels - 1 - step if i & 1 else step)))


def swap_chips(block, step, count):
    return swap(block, "dp", lambda i, j: i ^ (2 << (count - 1 - step if i & 1 else step)))


def swap_core(block):
    return swap(block, "dp", lambda i, j: i ^ 1)


def dot(left, right, left_dim, right_dim):
    return lax.dot_general(
        left, right, (((left_dim,), (right_dim,)), ((), ())), preferred_element_type=jnp.float32
    )


def tiles(extent, width):
    return [slice(at, min(at + width, extent)) for at in range(0, extent, width)]


def call(kernel, outs, args, flops, mib, scratch=(), in_specs=None, out_specs=None):
    nbytes = sum(a.size * a.dtype.itemsize for a in (*args, *outs))
    return pl.pallas_call(
        kernel,
        out_shape=outs,
        in_specs=in_specs or [VMEM] * len(args),
        out_specs=out_specs or [VMEM] * len(outs),
        scratch_shapes=list(scratch),
        compiler_params=pltpu.CompilerParams(vmem_limit_bytes=mib * MIB),
        cost_estimate=pl.CostEstimate(flops=flops, bytes_accessed=nbytes // 8, transcendentals=0),
    )(*args)


def chip_at(device, side, chips, position):
    steps = chips.bit_length() - 1
    core = (device & 1) ^ side
    up = down = 0
    for step in range(steps):
        if position >> (steps - 1 - step) & 1:
            up |= 1 << step
            down |= 1 << (steps - 1 - step)
    return (device >> 1) ^ (up + core * (down - up))


def section_at(device, step, levels):
    return step + 1 + (device & 1) * (levels - 1 - 2 * step)


def low_kernel(device_ref, x_ref, left_ref, total_ref, sent_ref):
    value = dot(x_ref[...], left_ref[...], 1, 0)
    total_ref[...] = value
    sent_ref[...] = value.astype(jnp.bfloat16)


def low_partial(device, tokens, left_factor):
    shape = (tokens.shape[0], left_factor.shape[1])
    outs = [jax.ShapeDtypeStruct(shape, jnp.float32), jax.ShapeDtypeStruct(shape, jnp.bfloat16)]
    flops = 2 * tokens.size * shape[1]
    specs = [SMEM, VMEM, VMEM]
    return call(low_kernel, outs, (device, tokens, left_factor), flops, 4, (), specs)


def add_kernel(value_ref, got_ref, total_ref, sent_ref):
    value = value_ref[...] + got_ref[...].astype(jnp.float32)
    total_ref[...] = value
    sent_ref[...] = value.astype(jnp.bfloat16)


def add(value, got):
    outs = [
        jax.ShapeDtypeStruct(value.shape, jnp.float32),
        jax.ShapeDtypeStruct(value.shape, jnp.bfloat16),
    ]
    return call(add_kernel, outs, (value, got), 0, 2)


def first_kernel(device_ref, x_ref, b_ref, out_ref, held_ref, sem):
    copies = []
    columns = tiles(out_ref.shape[1], 512)
    for index, at in enumerate(columns):
        copies.append(
            pltpu.make_async_copy(b_ref.at[0, :, at], held_ref.at[0, :, at], sem.at[index])
        )
    for section in range(1, b_ref.shape[0]):
        copies.append(
            pltpu.make_async_copy(
                b_ref.at[section], held_ref.at[section], sem.at[len(columns) + section - 1]
            )
        )
    for copy in copies:
        copy.start()
    x = x_ref[...]
    for copy, at in zip(copies, columns):
        copy.wait()
        out_ref[:, at] = dot(x, held_ref[0, :, at], 1, 0)
    for copy in copies[len(columns) :]:
        copy.wait()


def first(device, tokens, blocks):
    outs = [
        jax.ShapeDtypeStruct((tokens.shape[0], blocks.shape[2]), jnp.float32),
        jax.ShapeDtypeStruct(blocks.shape, blocks.dtype),
    ]
    count = len(tiles(blocks.shape[2], 512)) + blocks.shape[0] - 1
    scratch = [pltpu.SemaphoreType.DMA((count,))]
    flops = 2 * tokens.size * blocks.shape[2]
    return call(first_kernel, outs, (device, tokens, blocks), flops, 34, scratch, [SMEM, VMEM, HBM])


def forward_kernel(step, device_ref, x_ref, b_ref, running_ref, out_ref):
    section = section_at(device_ref[0], step, b_ref.shape[0] - 1)
    x = x_ref[...]
    for at in tiles(out_ref.shape[1], 512):
        out_ref[:, at] = running_ref[:, at] + dot(x, b_ref[section, :, at], 1, 0)


def forward(device, step, x, blocks, running):
    out = jax.ShapeDtypeStruct(running.shape, jnp.float32)
    flops = 2 * x.size * blocks.shape[2]
    kernel = functools.partial(forward_kernel, step)
    specs = [SMEM, VMEM, VMEM, VMEM]
    return call(kernel, [out], (device, x, blocks, running), flops, 4, (), specs)[0]


def backward_kernel(step, device_ref, s_ref, b_ref, out_ref):
    section = 0 if step is None else section_at(device_ref[0], step, b_ref.shape[0] - 1)
    slopes = s_ref[...]
    for at in tiles(out_ref.shape[1], 256):
        out_ref[:, at] = dot(slopes, b_ref[section, at, :], 1, 1).astype(out_ref.dtype)


def backward(device, step, slopes, blocks, dtype):
    out = jax.ShapeDtypeStruct((slopes.shape[0], blocks.shape[1]), dtype)
    flops = 2 * slopes.size * blocks.shape[1]
    kernel = functools.partial(backward_kernel, step)
    return call(kernel, [out], (device, slopes, blocks), flops, 6, (), [SMEM, VMEM, VMEM])[0]


def gelu_and_slope(value, upstream):
    base = 0.7978845608028654
    cubic = 0.044715
    square = value * value
    s = 0.5 + 0.5 * jnp.tanh(value * (base + (base * cubic) * square))
    act = value * s
    slope = s + (act - act * s) * (2 * base + (6 * base * cubic) * square)
    return act, upstream * slope


def middle_kernel(
    step, chips, device_ref, pre_ref, x_ref, b_ref, low_ref, got_ref, right_ref, up_ref,
    act_ref, slope_ref, mixed_ref, mixed_sent_ref, keep_ref, send_ref, turned_ref, order_ref,
):
    rank = low_ref.shape[1]
    half = rank // 2
    piece = half // chips
    device = device_ref[0]
    total = low_ref[...] + got_ref[...].astype(jnp.float32)
    low = total.astype(jnp.bfloat16)
    turned_ref[...] = low.astype(jnp.float32).T
    for side in range(2):
        for other in range(chips):
            source = ((device & 1) ^ side) * half + chip_at(device, side, chips, other) * piece
            target = side * half + other * piece
            order_ref[target : target + piece, :] = turned_ref[
                pl.ds(pl.multiple_of(source, piece), piece), :
            ].astype(jnp.bfloat16)
    section = section_at(device, step, b_ref.shape[0] - 1)
    x = x_ref[...]
    order = order_ref[...]
    mixed = None
    for at in tiles(up_ref.shape[1], 1024):
        right = right_ref[:, at]
        value = pre_ref[:, at] + dot(x, b_ref[section, :, at], 1, 0) + dot(low, right, 1, 0)
        act, slope = gelu_and_slope(value, up_ref[:, at].astype(jnp.float32))
        act_ref[:, at] = act.astype(jnp.bfloat16)
        slope = slope.astype(jnp.bfloat16)
        slope_ref[:, at] = slope
        part = dot(slope, right, 1, 1)
        mixed = part if mixed is None else mixed + part
        product = dot(order, slope, 1, 0)
        keep_ref[:, at] = product[:half]
        send_ref[:, at] = product[half:].astype(jnp.bfloat16)
    mixed_ref[...] = mixed
    mixed_sent_ref[...] = mixed.astype(jnp.bfloat16)


def middle(device, step, chips, running, x, blocks, low, got, right_factor, upstream):
    rows, cols = upstream.shape
    rank = low.shape[1]
    bf16, f32 = jnp.bfloat16, jnp.float32
    outs = [
        jax.ShapeDtypeStruct((rows, cols), bf16),
        jax.ShapeDtypeStruct((rows, cols), bf16),
        jax.ShapeDtypeStruct((rows, rank), f32),
        jax.ShapeDtypeStruct((rows, rank), bf16),
        jax.ShapeDtypeStruct((rank // 2, cols), f32),
        jax.ShapeDtypeStruct((rank // 2, cols), bf16),
    ]
    args = (device, running, x, blocks, low, got, right_factor, upstream)
    flops = 2 * rows * cols * (x.shape[1] + 3 * rank)
    scratch = [pltpu.VMEM((rank, rows), f32), pltpu.VMEM((rank, rows), bf16)]
    kernel = functools.partial(middle_kernel, step, chips)
    specs = [SMEM] + [VMEM] * (len(args) - 1)
    return call(kernel, outs, args, flops, 16, scratch, specs)


def turn_kernel(*refs):
    out_ref = refs[-1]
    column = 0
    for ref in refs[:-1]:
        rows = ref.shape[0]
        out_ref[:, column : column + rows] = ref[...].astype(jnp.float32).T.astype(jnp.bfloat16)
        column += rows


def turn(parts):
    rows = sum(part.shape[0] for part in parts)
    out = jax.ShapeDtypeStruct((parts[0].shape[1], rows), jnp.bfloat16)
    return call(turn_kernel, [out], parts, 0, 8)[0]


def left_kernel(scale, turned_ref, *refs):
    total_ref, sent_ref = refs[-2:]
    total = None
    column = 0
    for ref in refs[:-2]:
        rows = ref.shape[0]
        part = dot(turned_ref[:, column : column + rows], ref[...], 1, 0)
        total = part if total is None else total + part
        column += rows
    total = total * scale
    total_ref[...] = total
    sent_ref[...] = total.astype(jnp.bfloat16)


def left_partial(turned, mixed, scale):
    shape = (turned.shape[0], mixed[0].shape[1])
    outs = [jax.ShapeDtypeStruct(shape, jnp.float32), jax.ShapeDtypeStruct(shape, jnp.bfloat16)]
    flops = 2 * turned.size * shape[1]
    return call(functools.partial(left_kernel, scale), outs, (turned, *mixed), flops, 6)


def join_kernel(chips, device_ref, *refs):
    parts, out_ref, sem = refs[:-2], refs[-2], refs[-1]
    height = out_ref.shape[0] // (2 * chips)
    device = device_ref[0]
    copies = []
    for side in range(2):
        other = 0
        for ref in parts[side * len(parts) // 2 : (side + 1) * len(parts) // 2]:
            for at in tiles(ref.shape[0], height):
                row = ((device & 1) ^ side) * chips + chip_at(device, side, chips, other)
                target = out_ref.at[pl.ds(pl.multiple_of(row * height, height), height), :]
                copies.append(pltpu.make_async_copy(ref.at[at, :], target, sem.at[len(copies)]))
                other += 1
    for copy in copies:
        copy.start()
    for copy in copies:
        copy.wait()


def join(device, chips, parts):
    out = jax.ShapeDtypeStruct(
        (sum(part.shape[0] for part in parts), parts[0].shape[1]), jnp.bfloat16
    )
    specs = [SMEM] + [VMEM] * len(parts)
    scratch = [pltpu.SemaphoreType.DMA((2 * chips,))]
    kernel = functools.partial(join_kernel, chips)
    return call(kernel, [out], (device, *parts), 0, 2, scratch, specs, [HBM])[0]


def body(tokens, blocks, left_factor, right_factor, upstream):
    bf16, f32 = jnp.bfloat16, jnp.float32
    levels = blocks.shape[0] - 1
    group = lax.axis_size("dp")
    chips = group // 2
    steps = chips.bit_length() - 1
    norm_scale = 1.0 / float(tokens.shape[0] * group) ** 0.5
    device = lax.axis_index("dp").astype(jnp.int32).reshape(1)

    low, low_sent = low_partial(device, tokens, left_factor)
    partners = []
    for step in range(levels):
        got = swap_tensor(low_sent, step, levels)
        partners.append(swap_tensor(tokens, step, levels))
        if step < levels - 1:
            low, low_sent = add(low, got)
    running, held = first(device, tokens, blocks)
    token_parts = [tokens]
    for step in reversed(range(steps)):
        sent = jnp.concatenate(token_parts) if len(token_parts) > 1 else tokens
        token_parts.append(swap_chips(sent, step, steps))
    for step in range(levels - 1):
        running = forward(device, step, partners[step], held, running)
    activated, slopes, mixed, mixed_sent, keep, send = middle(
        device, levels - 1, chips, running, partners[-1], held, low, got, right_factor, upstream
    )
    turned = turn(token_parts)

    mine = keep + swap_core(send).astype(f32)
    for step in range(steps):
        half = mine.shape[0] // 2
        got = swap_chips(mine[half:].astype(bf16), step, steps)
        mine = mine[:half] + got.astype(f32)
    pieces = [(mine * norm_scale).astype(bf16)]

    returned = []
    for step in range(levels):
        got = swap_tensor(mixed_sent, step, levels)
        mixed, mixed_sent = add(mixed, got)
        part = backward(device, step, slopes, held, bf16)
        returned.append(swap_tensor(part, step, levels))
    token_sum = backward(device, None, slopes, held, f32)

    rows_parts = [mixed_sent]
    for step in reversed(range(steps)):
        sent = jnp.concatenate(pieces) if len(pieces) > 1 else pieces[0]
        pieces.append(swap_chips(sent, step, steps))
        sent = jnp.concatenate(rows_parts) if len(rows_parts) > 1 else mixed_sent
        rows_parts.append(swap_chips(sent, step, steps))
    left_total, left_sent = left_partial(turned, rows_parts, norm_scale)
    left_grad = (left_total + swap_core(left_sent).astype(f32)).astype(bf16)
    pieces += [swap_core(part) for part in pieces]
    right_grad = join(device, chips, pieces)

    token_sum = token_sum + dot(mixed_sent, left_factor, 1, 1)
    for part in returned:
        token_sum = token_sum + part.astype(f32)
    return activated, token_sum.astype(bf16), left_grad, right_grad


def solution(mesh):
    placed = (
        P("dp", "tensor"),
        P(None, "tensor", None),
        P("tensor", None),
        P(None, "tensor"),
        P("dp", "tensor"),
    )

    return jax.shard_map(
        body,
        mesh=mesh,
        in_specs=placed,
        out_specs=(P("dp", "tensor"), P("dp", "tensor"), P("tensor", None), P(None, "tensor")),
        check_vma=False,
    )
```

time: 178 us -> 82.9 us (0.47)
  blocking collectives: 138 us -> 0 us
  waiting for transfers between devices: 0.01 us -> 30.3 us
  matrix products: 28.9 us -> 0.3 us
  Pallas kernels: 0 us -> 19.4 us
  starting transfers between devices: 6.97 us -> 26.2 us
  other arithmetic: 0 us -> 2.17 us
    psum x3 -> x0, blocking collectives: 138 us -> none  [the longest x1 83 us: body(): left_total, right_total = lax.psum((left_part, right_part), 'dp')]
    ppermute x4 -> x21, waiting for transfers between devices: 0.01 us -> 30.3 us  [swap(): return lax.ppermute(block, axes, route)]
    dot_general x12 -> x1, matrix products: 28.9 us -> 0.3 us  [dot(): lax.dot_general(left, right, (((left_dim,), (right_dim,)), ((), ())), pre...]
    pallas_call x0 -> x13, Pallas kernels: none -> 19.4 us  [call(): pl.pallas_call(kernel, out_shape=outs, in_specs=in_specs or [VMEM] * len(...]
    ppermute x4 -> x21, starting transfers between devices: 6.97 us -> 26.2 us  [swap(): return lax.ppermute(block, axes, route)]
    convert_element_type x0 -> x3, other arithmetic: none -> 1.8 us  [the longest x1 0.91 us: body(): return (activated, token_sum.astype(bf16), left_grad, right_grad)]
  transfers between devices with their start and end apart: 4 -> 21, of which waited for: 0 -> 10; matrix products, arithmetic and copies ran while one was open for 7% -> 3% of each run, Pallas kernels for 0% -> 16%
where the time goes in v1:
time: 82.9 us; the launch traced here: 82.7 us
  waiting for transfers between devices  30.3 us (37%)
  starting transfers between devices  26.2 us (32%)
  Pallas kernels  19.4 us (23%)
  local copies, waits for them, and re-layouts  3.49 us (4%)
  other arithmetic  2.17 us (3%)
  between operations  0.84 us (1%)
    ppermute x21, waiting for transfers between devices, swap(): return lax.ppermute(block, axes, route)  30.3 us
    ppermute x21, starting transfers between devices, swap(): return lax.ppermute(block, axes, route)  26.2 us
    pallas_call x13, Pallas kernels, call(): pl.pallas_call(kernel, out_shape=outs, in_specs=in_specs or [VMEM] * len(...  19.4 us
    unnamed x14, local copies, waits for them, and re-layouts  3.42 us
  transfers between devices with their start and end apart: 21, of which 10 were waited for; matrix products, arithmetic and copies ran while one was open for 3% of the time, Pallas kernels for 16%

profile of v1, /device:TPU:0, one launch (start us, length us, event | category | flops | bytes accessed | tf_op | source)
XLA Modules:
  0.0 82.7 jit_solution(14687299858735757613)
XLA Ops:
  0.6 3.1 %collective-permute-start = (bf16[256,768]{1,0:T(8,128)(2,1)}, bf16[256,768]{1,0:T(8,128)(2,1)S(1)}, u32[]{:S(2)}, u32[]{:S(2)}) collective-permute-start(bf16[256,768]{1,0:T(8,128)(2,1)} %refs_0_.1), channel_id=1, source_target_pairs={{0,1},{1,0},{2,3},{3,2},{4,6},{5,7},{6,4},{7,5},{8,9},{9,8},{10,11... | collective-permute-start | bytes 1179656 | tf_op jit(solution)/shard_map/ppermute | solution.py:24
  3.7 2.6 %collective-permute-start.1 = (bf16[256,768]{1,0:T(8,128)(2,1)}, bf16[256,768]{1,0:T(8,128)(2,1)S(1)}, u32[]{:S(2)}, u32[]{:S(2)}) collective-permute-start(bf16[256,768]{1,0:T(8,128)(2,1)} %refs_0_.1), channel_id=1, source_target_pairs={{0,2},{1,3},{2,0},{3,1},{4,5},{5,4},{6,7},{7,6},{8,10},{9,11},{10,... | collective-permute-start | bytes 1179656 | tf_op jit(solution)/shard_map/ppermute | solution.py:24
  6.3 1.0 %copy-done = bf16[256,768]{1,0:T(8,128)(2,1)S(1)} copy-done((bf16[256,768]{1,0:T(8,128)(2,1)S(1)}, bf16[256,768]{1,0:T(8,128)(2,1)}, u32[]{:S(2)}) %copy-start) | copy-done | bytes 393240
  7.4 1.0 %copy-done.5 = bf16[768,256]{1,0:T(8,128)(2,1)S(1)} copy-done((bf16[768,256]{1,0:T(8,128)(2,1)S(1)}, bf16[768,256]{1,0:T(8,128)(2,1)}, u32[]{:S(2)}) %copy-start.5) | copy-done | bytes 393240
  8.4 0.3 shard_map.86
  8.6 0.5 collective-permute-start.2
  9.2 15.7 %collective-permute-done.2.got_ref = bf16[256,256]{1,0:T(8,128)(2,1)S(1)} collective-permute-done((bf16[256,256]{1,0:T(8,128)(2,1)S(1)}, bf16[256,256]{1,0:T(8,128)(2,1)S(1)}, u32[]{:S(2)}, u32[]{:S(2)}) %collective-permute-start.2) | collective-permute-done | bytes 131104 | tf_op jit(solution)/shard_map/ppermute | solution.py:24
  24.9 2.2 %collective-permute-start.3 = (bf16[256,256]{1,0:T(8,128)(2,1)S(1)}, bf16[256,256]{1,0:T(8,128)(2,1)S(1)}, u32[]{:S(2)}, u32[]{:S(2)}) collective-permute-start(bf16[256,256]{1,0:T(8,128)(2,1)S(1)} %get-tuple-element.26), channel_id=1, source_target_pairs={{0,2},{1,3},{2,0},{3,1},{4,5},{5,4},{6,7},{7,6},{8,10},{9,11},{10,... | collective-permute-start | bytes 393224 | tf_op jit(solution)/shard_map/ppermute | solution.py:24
  27.2 1.0 %copy-done.1 = bf16[256,768]{1,0:T(8,128)(2,1)S(1)} copy-done((bf16[256,768]{1,0:T(8,128)(2,1)S(1)}, bf16[256,768]{1,0:T(8,128)(2,1)}, u32[]{:S(2)}) %copy-start.1) | copy-done | bytes 393240
  28.1 5.2 %shard_map.84 = (f32[256,3072]{1,0:T(8,128)S(1)}, bf16[3,768,3072]{2,1,0:T(8,128)(2,1)S(1)}) custom-call(s32[1]{0:T(128)} %bitcast.device_ref, bf16[256,768]{1,0:T(8,128)(2,1)S(1)} %copy-done.1, bf16[3,768,3072]{2,1,0:T(8,128)(2,1)} %b_ref.1), custom_call_target="tpu_custom_call" | custom-call | flops 1207959552 | bytes 3981312 | tf_op jit(solution)/shard_map/pallas_call | solution.py:51
  33.4 1.4 %shard_map.85.pre_ref = f32[256,3072]{1,0:T(8,128)S(1)} custom-call(s32[1]{0:T(128)} %bitcast.device_ref, bf16[256,768]{1,0:T(8,128)(2,1)S(1)} %collective-permute-done.x_ref, bf16[3,768,3072]{2,1,0:T(8,128)(2,1)S(1)} %get-tuple-element.21.b_ref, f32[256,3072]{1,0:T(8,128)S(1)} %get-tuple-element.22.running_ref), custom_call_target="tpu_custom_call" | custom-call | flops 1207959552 | bytes 2605056 | tf_op jit(solution)/shard_map/pallas_call | solution.py:51
  34.9 0.4 copy-done.4
  35.3 5.1 %shard_map.88 = (bf16[256,3072]{1,0:T(8,128)(2,1)}, bf16[256,3072]{1,0:T(8,128)(2,1)S(1)}, f32[256,256]{1,0:T(8,128)S(1)}, bf16[256,256]{1,0:T(8,128)(2,1)S(1)},...) custom-call(s32[1]{0:T(128)} %bitcast.device_ref, f32[256,3072]{1,0:T(8,128)S(1)} %shard_map.85.pre_ref, ...), custom_call_target="tpu_custom_call" | custom-call | flops 2415919104 | bytes 3391488 | tf_op jit(solution)/shard_map/pallas_call | solution.py:51
  40.4 2.3 %collective-permute-done.13 = bf16[128,3072]{1,0:T(8,128)(2,1)S(1)} collective-permute-done((bf16[128,3072]{1,0:T(8,128)(2,1)S(1)}, bf16[128,3072]{1,0:T(8,128)(2,1)S(1)}, u32[]{:S(2)}, u32[]{:S(2)}) %collective-permute-start.13) | collective-permute-done | bytes 786464 | tf_op jit(solution)/shard_map/ppermute | solution.py:24
  42.7 0.2 convert_add_fusion
  42.9 1.6 %collective-permute-start.14 = (bf16[64,3072]{1,0:T(8,128)(2,1)S(1)}, bf16[64,3072]{1,0:T(8,128)(2,1)S(1)}, u32[]{:S(2)}, u32[]{:S(2)}) collective-permute-start(bf16[64,3072]{1,0:T(8,128)(2,1)S(1)} %slice.30), channel_id=1, source_target_pairs={{0,8},{4,20},{8,0},{12,28},{16,24},{20,4},{24,16},{28,12},{1,9},{5... | collective-permute-start | bytes 1179656 | tf_op jit(solution)/shard_map/ppermute | solution.py:24
  44.5 0.8 %collective-permute-start.4 = (bf16[256,256]{1,0:T(8,128)(2,1)S(1)}, bf16[256,256]{1,0:T(8,128)(2,1)S(1)}, u32[]{:S(2)}, u32[]{:S(2)}) collective-permute-start(bf16[256,256]{1,0:T(8,128)(2,1)S(1)} %get-tuple-element.30), channel_id=1, source_target_pairs={{0,1},{1,0},{2,3},{3,2},{4,6},{5,7},{6,4},{7,5},{8,9},{9,8},{10,11... | collective-permute-start | bytes 393224 | tf_op jit(solution)/shard_map/ppermute | solution.py:24
  45.3 1.5 %collective-permute-start.8 = (bf16[256,768]{1,0:T(8,128)(2,1)S(1)}, bf16[256,768]{1,0:T(8,128)(2,1)S(1)}, u32[]{:S(2)}, u32[]{:S(2)}) collective-permute-start(bf16[256,768]{1,0:T(8,128)(2,1)S(1)} %copy-done.2), channel_id=1, source_target_pairs={{0,16},{4,12},{8,24},{12,4},{16,0},{20,28},{24,8},{28,20},{1,17},{... | collective-permute-start | bytes 1179656 | tf_op jit(solution)/shard_map/ppermute | solution.py:24
  46.8 3.2 %collective-permute-done.4.got_ref = bf16[256,256]{1,0:T(8,128)(2,1)S(1)} collective-permute-done((bf16[256,256]{1,0:T(8,128)(2,1)S(1)}, bf16[256,256]{1,0:T(8,128)(2,1)S(1)}, u32[]{:S(2)}, u32[]{:S(2)}) %collective-permute-start.4) | collective-permute-done | bytes 131104 | tf_op jit(solution)/shard_map/ppermute | solution.py:24
  50.1 1.5 %collective-permute-start.5 = (bf16[256,256]{1,0:T(8,128)(2,1)S(1)}, bf16[256,256]{1,0:T(8,128)(2,1)S(1)}, u32[]{:S(2)}, u32[]{:S(2)}) collective-permute-start(bf16[256,256]{1,0:T(8,128)(2,1)S(1)} %get-tuple-element.32), channel_id=1, source_target_pairs={{0,2},{1,3},{2,0},{3,1},{4,5},{5,4},{6,7},{7,6},{8,10},{9,11},{10,... | collective-permute-start | bytes 393224 | tf_op jit(solution)/shard_map/ppermute | solution.py:24
  51.6 1.4 %collective-permute-done.14 = bf16[64,3072]{1,0:T(8,128)(2,1)S(1)} collective-permute-done((bf16[64,3072]{1,0:T(8,128)(2,1)S(1)}, bf16[64,3072]{1,0:T(8,128)(2,1)S(1)}, u32[]{:S(2)}, u32[]{:S(2)}) %collective-permute-start.14) | collective-permute-done | bytes 393248 | tf_op jit(solution)/shard_map/ppermute | solution.py:24
  53.0 0.1 slice_add_fusion
  53.2 2.6 %collective-permute-start.15 = (bf16[32,3072]{1,0:T(8,128)(2,1)S(1)}, bf16[32,3072]{1,0:T(8,128)(2,1)S(1)}, u32[]{:S(2)}, u32[]{:S(2)}) collective-permute-start(bf16[32,3072]{1,0:T(8,128)(2,1)S(1)} %slice.31), channel_id=1, source_target_pairs={{0,16},{4,12},{8,24},{12,4},{16,0},{20,28},{24,8},{28,20},{1,17},{... | collective-permute-start | bytes 589832 | tf_op jit(solution)/shard_map/ppermute | solution.py:24
  55.8 1.5 %collective-permute-start.9 = (bf16[512,768]{1,0:T(8,128)(2,1)S(1)}, bf16[512,768]{1,0:T(8,128)(2,1)S(1)}, u32[]{:S(2)}, u32[]{:S(2)}) collective-permute-start(bf16[512,768]{1,0:T(8,128)(2,1)S(1)} %pad_maximum_fusion), channel_id=1, source_target_pairs={{0,8},{4,20},{8,0},{12,28},{16,24},{20,4},{24,16},{28,12},{1,9},{5... | collective-permute-start | bytes 2359304 | tf_op jit(solution)/shard_map/ppermute | solution.py:24
  57.4 1.4 %shard_map.92 = bf16[256,768]{1,0:T(8,128)(2,1)S(1)} custom-call(s32[1]{0:T(128)} %bitcast.device_ref, bf16[256,3072]{1,0:T(8,128)(2,1)S(1)} %get-tuple-element.28.s_ref, bf16[3,768,3072]{2,1,0:T(8,128)(2,1)S(1)} %get-tuple-element.21.b_ref), custom_call_target="tpu_custom_call" | custom-call | flops 1207959552 | bytes 2015232 | tf_op jit(solution)/shard_map/pallas_call | solution.py:51
  58.8 0.6 collective-permute-start.6
  59.4 0.7 shard_map.91
  60.2 0.2 collective-permute-start.10
  60.3 0.7 collective-permute-done.15
  61.1 2.5 %collective-permute-start.16 = (bf16[32,3072]{1,0:T(8,128)(2,1)S(1)}, bf16[32,3072]{1,0:T(8,128)(2,1)S(1)}, u32[]{:S(2)}, u32[]{:S(2)}) collective-permute-start(bf16[32,3072]{1,0:T(8,128)(2,1)S(1)} %fusion.1.refs_0_), channel_id=1, source_target_pairs={{0,16},{4,12},{8,24},{12,4},{16,0},{20,28},{24,8},{28,20},{1,17},{... | collective-permute-start | bytes 589832 | tf_op jit(solution)/shard_map/ppermute | solution.py:24
  63.7 1.4 %shard_map.93 = bf16[256,768]{1,0:T(8,128)(2,1)S(1)} custom-call(s32[1]{0:T(128)} %bitcast.device_ref, bf16[256,3072]{1,0:T(8,128)(2,1)S(1)} %get-tuple-element.28.s_ref, bf16[3,768,3072]{2,1,0:T(8,128)(2,1)S(1)} %get-tuple-element.21.b_ref), custom_call_target="tpu_custom_call" | custom-call | flops 1207959552 | bytes 2015232 | tf_op jit(solution)/shard_map/pallas_call | solution.py:51
  65.1 2.0 %collective-permute-start.7 = (bf16[256,768]{1,0:T(8,128)(2,1)S(1)}, bf16[256,768]{1,0:T(8,128)(2,1)S(1)}, u32[]{:S(2)}, u32[]{:S(2)}) collective-permute-start(bf16[256,768]{1,0:T(8,128)(2,1)S(1)} %shard_map.93), channel_id=1, source_target_pairs={{0,2},{1,3},{2,0},{3,1},{4,5},{5,4},{6,7},{7,6},{8,10},{9,11},{10,... | collective-permute-start | bytes 1179656 | tf_op jit(solution)/shard_map/ppermute | solution.py:24
  67.2 1.6 %collective-permute-start.11 = (bf16[512,256]{1,0:T(8,128)(2,1)S(1)}, bf16[512,256]{1,0:T(8,128)(2,1)S(1)}, u32[]{:S(2)}, u32[]{:S(2)}) collective-permute-start(bf16[512,256]{1,0:T(8,128)(2,1)S(1)} %pad_maximum_fusion.2), channel_id=1, source_target_pairs={{0,8},{4,20},{8,0},{12,28},{16,24},{20,4},{24,16},{28,12},{1,9},{5... | collective-permute-start | bytes 786440 | tf_op jit(solution)/shard_map/ppermute | solution.py:24
  68.7 2.0 %collective-permute-done.16.refs_1_ = bf16[32,3072]{1,0:T(8,128)(2,1)S(1)} collective-permute-done((bf16[32,3072]{1,0:T(8,128)(2,1)S(1)}, bf16[32,3072]{1,0:T(8,128)(2,1)S(1)}, u32[]{:S(2)}, u32[]{:S(2)}) %collective-permute-start.16) | collective-permute-done | bytes 196640 | tf_op jit(solution)/shard_map/ppermute | solution.py:24
  70.8 0.6 collective-permute-start.17
  71.4 1.4 %shard_map.89 = f32[256,768]{1,0:T(8,128)S(1)} custom-call(s32[1]{0:T(128)} %bitcast.device_ref, bf16[256,3072]{1,0:T(8,128)(2,1)S(1)} %get-tuple-element.28.s_ref, bf16[3,768,3072]{2,1,0:T(8,128)(2,1)S(1)} %get-tuple-element.21.b_ref), custom_call_target="tpu_custom_call" | custom-call | flops 1207959552 | bytes 2064384 | tf_op jit(solution)/shard_map/pallas_call | solution.py:51
  72.8 0.5 shard_map.94.turned_ref
  73.3 0.9 %collective-permute-done.11.refs_2_ = bf16[512,256]{1,0:T(8,128)(2,1)S(1)} collective-permute-done((bf16[512,256]{1,0:T(8,128)(2,1)S(1)}, bf16[512,256]{1,0:T(8,128)(2,1)S(1)}, u32[]{:S(2)}, u32[]{:S(2)}) %collective-permute-start.11) | collective-permute-done | bytes 262176 | tf_op jit(solution)/shard_map/ppermute | solution.py:24
  74.2 0.6 shard_map.95
  74.8 0.1 collective-permute-start.12
  74.9 0.3 fusion.2
  75.2 3.4 %collective-permute-done.17.refs_2_ = bf16[64,3072]{1,0:T(8,128)(2,1)S(1)} collective-permute-done((bf16[64,3072]{1,0:T(8,128)(2,1)S(1)}, bf16[64,3072]{1,0:T(8,128)(2,1)S(1)}, u32[]{:S(2)}, u32[]{:S(2)}) %collective-permute-start.17) | collective-permute-done | bytes 393248 | tf_op jit(solution)/shard_map/ppermute | solution.py:24
  78.6 0.9 %add_convert_fusion.1 = bf16[256,768]{1,0:T(8,128)(2,1)} fusion(bf16[256,768]{1,0:T(8,128)(2,1)S(1)} %collective-permute-done.7, bf16[256,768]{1,0:T(8,128)(2,1)S(1)} %collective-permute-done.6, f32[256,768]{1,0:T(8,128)S(1)} %shard_map.89, f32[256,768]{1,0:T(8,128)S(1)} %fusion.2), kind=kLoop, calls=%fused_computation.5 | loop fusion | flops 1179648 | bytes 2752512 | tf_op jit(solution)/shard_map/convert_element_type | solution.py:358
  79.5 0.5 collective-permute-start.18
  80.1 0.8 %add_convert_fusion = bf16[768,256]{1,0:T(8,128)(2,1)} fusion(f32[768,256]{1,0:T(8,128)S(1)} %get-tuple-element.34, bf16[768,256]{1,0:T(8,128)(2,1)S(1)} %collective-permute-done.12), kind=kLoop, calls=%fused_computation.4 | loop fusion | flops 589824 | bytes 1572864 | tf_op jit(solution)/shard_map/convert_element_type | solution.py:351
  80.9 0.2 collective-permute-done.18.refs_3_
  81.1 0.4 collective-permute-done.19.refs_4_
  81.5 1.2 %shard_map.96 = bf16[256,3072]{1,0:T(8,128)(2,1)} custom-call(s32[1]{0:T(128)} %bitcast.device_ref, bf16[32,3072]{1,0:T(8,128)(2,1)S(1)} %fusion.1.refs_0_, bf16[32,3072]{1,0:T(8,128)(2,1)S(1)} %collective-permute-done.16.refs_1_, bf16[64,3072]{1,0:T(8,128)(2,1)S(1)} %collective-permute-done.17.refs_2_, ...), custom_call_target="tpu_custom_call" | custom-call | bytes 393216 | tf_op jit(solution)/shard_map/pallas_call | solution.py:51
  (32 shorter events, 0.4 us)
Async XLA Ops:
  0.6 32.8 %collective-permute-start = (bf16[256,768]{1,0:T(8,128)(2,1)}, bf16[256,768]{1,0:T(8,128)(2,1)S(1)}, u32[]{:S(2)}, u32[]{:S(2)}) collective-permute-start(bf16[256,768]{1,0:T(8,128)(2,1)} %refs_0_.1), channel_id=1, source_target_pairs={{0,1},{1,0},{2,3},{3,2},{4,6},{5,7},{6,4},{7,5},{8,9},{9,8},{10,11... | collective-permute-start | bytes 1179656 | tf_op jit(solution)/shard_map/ppermute | solution.py:24
  3.7 31.1 %collective-permute-start.1 = (bf16[256,768]{1,0:T(8,128)(2,1)}, bf16[256,768]{1,0:T(8,128)(2,1)S(1)}, u32[]{:S(2)}, u32[]{:S(2)}) collective-permute-start(bf16[256,768]{1,0:T(8,128)(2,1)} %refs_0_.1), channel_id=1, source_target_pairs={{0,2},{1,3},{2,0},{3,1},{4,5},{5,4},{6,7},{7,6},{8,10},{9,11},{10,... | collective-permute-start | bytes 1179656 | tf_op jit(solution)/shard_map/ppermute | solution.py:24
  6.3 1.0 %copy-start = (bf16[256,768]{1,0:T(8,128)(2,1)S(1)}, bf16[256,768]{1,0:T(8,128)(2,1)}, u32[]{:S(2)}) copy-start(bf16[256,768]{1,0:T(8,128)(2,1)} %refs_0_.1) | copy-start | bytes 1179652
  7.4 1.0 %copy-start.5 = (bf16[768,256]{1,0:T(8,128)(2,1)S(1)}, bf16[768,256]{1,0:T(8,128)(2,1)}, u32[]{:S(2)}) copy-start(bf16[768,256]{1,0:T(8,128)(2,1)} %left_ref.1) | copy-start | bytes 1179652
  8.6 16.2 %collective-permute-start.2 = (bf16[256,256]{1,0:T(8,128)(2,1)S(1)}, bf16[256,256]{1,0:T(8,128)(2,1)S(1)}, u32[]{:S(2)}, u32[]{:S(2)}) collective-permute-start(bf16[256,256]{1,0:T(8,128)(2,1)S(1)} %get-tuple-element.24), channel_id=1, source_target_pairs={{0,1},{1,0},{2,3},{3,2},{4,6},{5,7},{6,4},{7,5},{8,9},{9,8},{10,11... | collective-permute-start | bytes 393224 | tf_op jit(solution)/shard_map/ppermute | solution.py:24
  24.9 9.9 %collective-permute-start.3 = (bf16[256,256]{1,0:T(8,128)(2,1)S(1)}, bf16[256,256]{1,0:T(8,128)(2,1)S(1)}, u32[]{:S(2)}, u32[]{:S(2)}) collective-permute-start(bf16[256,256]{1,0:T(8,128)(2,1)S(1)} %get-tuple-element.26), channel_id=1, source_target_pairs={{0,2},{1,3},{2,0},{3,1},{4,5},{5,4},{6,7},{7,6},{8,10},{9,11},{10,... | collective-permute-start | bytes 393224 | tf_op jit(solution)/shard_map/ppermute | solution.py:24
  27.1 1.0 %copy-start.1 = (bf16[256,768]{1,0:T(8,128)(2,1)S(1)}, bf16[256,768]{1,0:T(8,128)(2,1)}, u32[]{:S(2)}) copy-start(bf16[256,768]{1,0:T(8,128)(2,1)} %refs_0_.1) | copy-start | bytes 1179652
  33.4 1.5 %copy-start.3 = (bf16[256,3072]{1,0:T(8,128)(2,1)S(1)}, bf16[256,3072]{1,0:T(8,128)(2,1)}, u32[]{:S(2)}) copy-start(bf16[256,3072]{1,0:T(8,128)(2,1)} %right_ref.1) | copy-start | bytes 4718596
  33.4 1.9 %copy-start.4 = (bf16[256,3072]{1,0:T(8,128)(2,1)S(1)}, bf16[256,3072]{1,0:T(8,128)(2,1)}, u32[]{:S(2)}) copy-start(bf16[256,3072]{1,0:T(8,128)(2,1)} %up_ref.1) | copy-start | bytes 4718596
  40.4 2.3 %collective-permute-start.13 = (bf16[128,3072]{1,0:T(8,128)(2,1)S(1)}, bf16[128,3072]{1,0:T(8,128)(2,1)S(1)}, u32[]{:S(2)}, u32[]{:S(2)}) collective-permute-start(bf16[128,3072]{1,0:T(8,128)(2,1)S(1)} %get-tuple-element.37), channel_id=1, source_target_pairs={{0,4},{4,0},{8,12},{12,8},{16,20},{20,16},{24,28},{28,24},{1,5},{5... | collective-permute-start | bytes 2359304 | tf_op jit(solution)/shard_map/ppermute | solution.py:24
  42.7 2.7 %copy-start.2 = (bf16[256,768]{1,0:T(8,128)(2,1)S(1)}, bf16[256,768]{1,0:T(8,128)(2,1)}, u32[]{:S(2)}) copy-start(bf16[256,768]{1,0:T(8,128)(2,1)} %refs_0_.1) | copy-start | bytes 1179652
  42.9 10.1 %collective-permute-start.14 = (bf16[64,3072]{1,0:T(8,128)(2,1)S(1)}, bf16[64,3072]{1,0:T(8,128)(2,1)S(1)}, u32[]{:S(2)}, u32[]{:S(2)}) collective-permute-start(bf16[64,3072]{1,0:T(8,128)(2,1)S(1)} %slice.30), channel_id=1, source_target_pairs={{0,8},{4,20},{8,0},{12,28},{16,24},{20,4},{24,16},{28,12},{1,9},{5... | collective-permute-start | bytes 1179656 | tf_op jit(solution)/shard_map/ppermute | solution.py:24
  44.5 5.6 %collective-permute-start.4 = (bf16[256,256]{1,0:T(8,128)(2,1)S(1)}, bf16[256,256]{1,0:T(8,128)(2,1)S(1)}, u32[]{:S(2)}, u32[]{:S(2)}) collective-permute-start(bf16[256,256]{1,0:T(8,128)(2,1)S(1)} %get-tuple-element.30), channel_id=1, source_target_pairs={{0,1},{1,0},{2,3},{3,2},{4,6},{5,7},{6,4},{7,5},{8,9},{9,8},{10,11... | collective-permute-start | bytes 393224 | tf_op jit(solution)/shard_map/ppermute | solution.py:24
  45.3 10.4 %collective-permute-start.8 = (bf16[256,768]{1,0:T(8,128)(2,1)S(1)}, bf16[256,768]{1,0:T(8,128)(2,1)S(1)}, u32[]{:S(2)}, u32[]{:S(2)}) collective-permute-start(bf16[256,768]{1,0:T(8,128)(2,1)S(1)} %copy-done.2), channel_id=1, source_target_pairs={{0,16},{4,12},{8,24},{12,4},{16,0},{20,28},{24,8},{28,20},{1,17},{... | collective-permute-start | bytes 1179656 | tf_op jit(solution)/shard_map/ppermute | solution.py:24
  50.1 9.3 %collective-permute-start.5 = (bf16[256,256]{1,0:T(8,128)(2,1)S(1)}, bf16[256,256]{1,0:T(8,128)(2,1)S(1)}, u32[]{:S(2)}, u32[]{:S(2)}) collective-permute-start(bf16[256,256]{1,0:T(8,128)(2,1)S(1)} %get-tuple-element.32), channel_id=1, source_target_pairs={{0,2},{1,3},{2,0},{3,1},{4,5},{5,4},{6,7},{7,6},{8,10},{9,11},{10,... | collective-permute-start | bytes 393224 | tf_op jit(solution)/shard_map/ppermute | solution.py:24
  53.2 7.9 %collective-permute-start.15 = (bf16[32,3072]{1,0:T(8,128)(2,1)S(1)}, bf16[32,3072]{1,0:T(8,128)(2,1)S(1)}, u32[]{:S(2)}, u32[]{:S(2)}) collective-permute-start(bf16[32,3072]{1,0:T(8,128)(2,1)S(1)} %slice.31), channel_id=1, source_target_pairs={{0,16},{4,12},{8,24},{12,4},{16,0},{20,28},{24,8},{28,20},{1,17},{... | collective-permute-start | bytes 589832 | tf_op jit(solution)/shard_map/ppermute | solution.py:24
  55.8 17.0 %collective-permute-start.9 = (bf16[512,768]{1,0:T(8,128)(2,1)S(1)}, bf16[512,768]{1,0:T(8,128)(2,1)S(1)}, u32[]{:S(2)}, u32[]{:S(2)}) collective-permute-start(bf16[512,768]{1,0:T(8,128)(2,1)S(1)} %pad_maximum_fusion), channel_id=1, source_target_pairs={{0,8},{4,20},{8,0},{12,28},{16,24},{20,4},{24,16},{28,12},{1,9},{5... | collective-permute-start | bytes 2359304 | tf_op jit(solution)/shard_map/ppermute | solution.py:24
  58.8 19.8 %collective-permute-start.6 = (bf16[256,768]{1,0:T(8,128)(2,1)S(1)}, bf16[256,768]{1,0:T(8,128)(2,1)S(1)}, u32[]{:S(2)}, u32[]{:S(2)}) collective-permute-start(bf16[256,768]{1,0:T(8,128)(2,1)S(1)} %shard_map.92), channel_id=1, source_target_pairs={{0,1},{1,0},{2,3},{3,2},{4,6},{5,7},{6,4},{7,5},{8,9},{9,8},{10,11... | collective-permute-start | bytes 1179656 | tf_op jit(solution)/shard_map/ppermute | solution.py:24
  60.2 7.0 %collective-permute-start.10 = (bf16[256,256]{1,0:T(8,128)(2,1)S(1)}, bf16[256,256]{1,0:T(8,128)(2,1)S(1)}, u32[]{:S(2)}, u32[]{:S(2)}) collective-permute-start(bf16[256,256]{1,0:T(8,128)(2,1)S(1)} %get-tuple-element.33.refs_0_), channel_id=1, source_target_pairs={{0,16},{4,12},{8,24},{12,4},{16,0},{20,28},{24,8},{28,20},{1,17},{... | collective-permute-start | bytes 393224 | tf_op jit(solution)/shard_map/ppermute | solution.py:24
  61.1 9.6 %collective-permute-start.16 = (bf16[32,3072]{1,0:T(8,128)(2,1)S(1)}, bf16[32,3072]{1,0:T(8,128)(2,1)S(1)}, u32[]{:S(2)}, u32[]{:S(2)}) collective-permute-start(bf16[32,3072]{1,0:T(8,128)(2,1)S(1)} %fusion.1.refs_0_), channel_id=1, source_target_pairs={{0,16},{4,12},{8,24},{12,4},{16,0},{20,28},{24,8},{28,20},{1,17},{... | collective-permute-start | bytes 589832 | tf_op jit(solution)/shard_map/ppermute | solution.py:24
  65.1 13.5 %collective-permute-start.7 = (bf16[256,768]{1,0:T(8,128)(2,1)S(1)}, bf16[256,768]{1,0:T(8,128)(2,1)S(1)}, u32[]{:S(2)}, u32[]{:S(2)}) collective-permute-start(bf16[256,768]{1,0:T(8,128)(2,1)S(1)} %shard_map.93), channel_id=1, source_target_pairs={{0,2},{1,3},{2,0},{3,1},{4,5},{5,4},{6,7},{7,6},{8,10},{9,11},{10,... | collective-permute-start | bytes 1179656 | tf_op jit(solution)/shard_map/ppermute | solution.py:24
  67.2 7.0 %collective-permute-start.11 = (bf16[512,256]{1,0:T(8,128)(2,1)S(1)}, bf16[512,256]{1,0:T(8,128)(2,1)S(1)}, u32[]{:S(2)}, u32[]{:S(2)}) collective-permute-start(bf16[512,256]{1,0:T(8,128)(2,1)S(1)} %pad_maximum_fusion.2), channel_id=1, source_target_pairs={{0,8},{4,20},{8,0},{12,28},{16,24},{20,4},{24,16},{28,12},{1,9},{5... | collective-permute-start | bytes 786440 | tf_op jit(solution)/shard_map/ppermute | solution.py:24
  70.8 7.8 %collective-permute-start.17 = (bf16[64,3072]{1,0:T(8,128)(2,1)S(1)}, bf16[64,3072]{1,0:T(8,128)(2,1)S(1)}, u32[]{:S(2)}, u32[]{:S(2)}) collective-permute-start(bf16[64,3072]{1,0:T(8,128)(2,1)S(1)} %pad_maximum_fusion.1), channel_id=1, source_target_pairs={{0,8},{4,20},{8,0},{12,28},{16,24},{20,4},{24,16},{28,12},{1,9},{5... | collective-permute-start | bytes 1179656 | tf_op jit(solution)/shard_map/ppermute | solution.py:24
  73.3 1.6 %copy-start.6 = (bf16[768,256]{1,0:T(8,128)(2,1)S(1)}, bf16[768,256]{1,0:T(8,128)(2,1)}, u32[]{:S(2)}) copy-start(bf16[768,256]{1,0:T(8,128)(2,1)} %left_ref.1) | copy-start | bytes 1179652
  74.8 5.3 %collective-permute-start.12 = (bf16[768,256]{1,0:T(8,128)(2,1)S(1)}, bf16[768,256]{1,0:T(8,128)(2,1)S(1)}, u32[]{:S(2)}, u32[]{:S(2)}) collective-permute-start(bf16[768,256]{1,0:T(8,128)(2,1)S(1)} %get-tuple-element.35), channel_id=1, source_target_pairs={{0,4},{4,0},{8,12},{12,8},{16,20},{20,16},{24,28},{28,24},{1,5},{5... | collective-permute-start | bytes 1179656 | tf_op jit(solution)/shard_map/ppermute | solution.py:24
  78.6 2.9 %collective-permute-start.20 = (bf16[64,3072]{1,0:T(8,128)(2,1)S(1)}, bf16[64,3072]{1,0:T(8,128)(2,1)S(1)}, u32[]{:S(2)}, u32[]{:S(2)}) collective-permute-start(bf16[64,3072]{1,0:T(8,128)(2,1)S(1)} %collective-permute-done.17.refs_2_), channel_id=1, source_target_pairs={{0,4},{4,0},{8,12},{12,8},{16,20},{20,16},{24,28},{28,24},{1,5},{5... | collective-permute-start | bytes 1179656 | tf_op jit(solution)/shard_map/ppermute | solution.py:24
  79.5 1.6 %collective-permute-start.18 = (bf16[32,3072]{1,0:T(8,128)(2,1)S(1)}, bf16[32,3072]{1,0:T(8,128)(2,1)S(1)}, u32[]{:S(2)}, u32[]{:S(2)}) collective-permute-start(bf16[32,3072]{1,0:T(8,128)(2,1)S(1)} %fusion.1.refs_0_), channel_id=1, source_target_pairs={{0,4},{4,0},{8,12},{12,8},{16,20},{20,16},{24,28},{28,24},{1,5},{5... | collective-permute-start | bytes 589832 | tf_op jit(solution)/shard_map/ppermute | solution.py:24
  80.0 1.4 %collective-permute-start.19 = (bf16[32,3072]{1,0:T(8,128)(2,1)S(1)}, bf16[32,3072]{1,0:T(8,128)(2,1)S(1)}, u32[]{:S(2)}, u32[]{:S(2)}) collective-permute-start(bf16[32,3072]{1,0:T(8,128)(2,1)S(1)} %collective-permute-done.16.refs_1_), channel_id=1, source_target_pairs={{0,4},{4,0},{8,12},{12,8},{16,20},{20,16},{24,28},{28,24},{1,5},{5... | collective-permute-start | bytes 589832 | tf_op jit(solution)/shard_map/ppermute | solution.py:24

commit v2 on v1

--- a/solution.py
+++ b/solution.py
@@ -74,6 +74,13 @@
     return step + 1 + (device & 1) * (levels - 1 - 2 * step)
 
 
+def gather_chips(part, count):
+    parts = [part]
+    for step in reversed(range(count)):
+        parts += [swap_chips(held, step, count) for held in parts]
+    return parts
+
+
 def low_kernel(device_ref, x_ref, left_ref, total_ref, sent_ref):
     value = dot(x_ref[...], left_ref[...], 1, 0)
     total_ref[...] = value
@@ -88,17 +95,14 @@
     return call(low_kernel, outs, (device, tokens, left_factor), flops, 4, (), specs)
 
 
-def add_kernel(value_ref, got_ref, total_ref, sent_ref):
+def add_kernel(value_ref, got_ref, *outs):
     value = value_ref[...] + got_ref[...].astype(jnp.float32)
-    total_ref[...] = value
-    sent_ref[...] = value.astype(jnp.bfloat16)
-
-
-def add(value, got):
-    outs = [
-        jax.ShapeDtypeStruct(value.shape, jnp.float32),
-        jax.ShapeDtypeStruct(value.shape, jnp.bfloat16),
-    ]
+    for out_ref in outs:
+        out_ref[...] = value.astype(out_ref.dtype)
+
+
+def add(value, got, dtypes=(jnp.float32, jnp.bfloat16)):
+    outs = [jax.ShapeDtypeStruct(value.shape, dtype) for dtype in dtypes]
     return call(add_kernel, outs, (value, got), 0, 2)
 
 
@@ -136,33 +140,44 @@
     return call(first_kernel, outs, (device, tokens, blocks), flops, 34, scratch, [SMEM, VMEM, HBM])
 
 
-def forward_kernel(step, device_ref, x_ref, b_ref, running_ref, out_ref):
+def forward_kernel(step, device_ref, b_ref, running_ref, *refs):
+    out_ref = refs[-1]
     section = section_at(device_ref[0], step, b_ref.shape[0] - 1)
-    x = x_ref[...]
+    x = rows_joined(refs[:-1])
     for at in tiles(out_ref.shape[1], 512):
         out_ref[:, at] = running_ref[:, at] + dot(x, b_ref[section, :, at], 1, 0)
 
 
-def forward(device, step, x, blocks, running):
+def rows_joined(refs):
+    return refs[0][...] if len(refs) == 1 else jnp.concatenate([ref[...] for ref in refs])
+
+
+def forward(device, step, parts, blocks, running):
     out = jax.ShapeDtypeStruct(running.shape, jnp.float32)
-    flops = 2 * x.size * blocks.shape[2]
+    flops = 2 * running.size * blocks.shape[1]
     kernel = functools.partial(forward_kernel, step)
-    specs = [SMEM, VMEM, VMEM, VMEM]
-    return call(kernel, [out], (device, x, blocks, running), flops, 4, (), specs)[0]
-
-
-def backward_kernel(step, device_ref, s_ref, b_ref, out_ref):
+    args = (device, blocks, running, *parts)
+    specs = [SMEM] + [VMEM] * (len(args) - 1)
+    return call(kernel, [out], args, flops, 4, (), specs)[0]
+
+
+def backward_kernel(step, device_ref, s_ref, b_ref, *outs):
     section = 0 if step is None else section_at(device_ref[0], step, b_ref.shape[0] - 1)
     slopes = s_ref[...]
-    for at in tiles(out_ref.shape[1], 256):
-        out_ref[:, at] = dot(slopes, b_ref[section, at, :], 1, 1).astype(out_ref.dtype)
-
-
-def backward(device, step, slopes, blocks, dtype):
-    out = jax.ShapeDtypeStruct((slopes.shape[0], blocks.shape[1]), dtype)
+    height = outs[0].shape[0]
+    for at in tiles(b_ref.shape[1], 256):
+        value = dot(slopes, b_ref[section, at, :], 1, 1)
+        for index, out_ref in enumerate(outs):
+            rows = value[index * height : (index + 1) * height]
+            out_ref[:, at] = rows.astype(out_ref.dtype)
+
+
+def backward(device, step, slopes, blocks, dtype, count):
+    shape = (slopes.shape[0] // count, blocks.shape[1])
+    outs = [jax.ShapeDtypeStruct(shape, dtype)] * count
     flops = 2 * slopes.size * blocks.shape[1]
     kernel = functools.partial(backward_kernel, step)
-    return call(kernel, [out], (device, slopes, blocks), flops, 6, (), [SMEM, VMEM, VMEM])[0]
+    return call(kernel, outs, (device, slopes, blocks), flops, 6, (), [SMEM, VMEM, VMEM])
 
 
 def gelu_and_slope(value, upstream):
@@ -248,13 +263,17 @@
     return call(turn_kernel, [out], parts, 0, 8)[0]
 
 
-def left_kernel(scale, turned_ref, *refs):
+def left_kernel(scale, early_ref, late_ref, *refs):
     total_ref, sent_ref = refs[-2:]
     total = None
     column = 0
     for ref in refs[:-2]:
         rows = ref.shape[0]
-        part = dot(turned_ref[:, column : column + rows], ref[...], 1, 0)
+        if column < early_ref.shape[1]:
+            turned = early_ref[:, column : column + rows]
+        else:
+            turned = late_ref[...]
+        part = dot(turned, ref[...], 1, 0)
         total = part if total is None else total + part
         column += rows
     total = total * scale
@@ -262,16 +281,37 @@
     sent_ref[...] = total.astype(jnp.bfloat16)
 
 
-def left_partial(turned, mixed, scale):
-    shape = (turned.shape[0], mixed[0].shape[1])
+def left_partial(early, late, mixed, scale):
+    shape = (early.shape[0], mixed[0].shape[1])
     outs = [jax.ShapeDtypeStruct(shape, jnp.float32), jax.ShapeDtypeStruct(shape, jnp.bfloat16)]
-    flops = 2 * turned.size * shape[1]
-    return call(functools.partial(left_kernel, scale), outs, (turned, *mixed), flops, 6)
-
-
-def join_kernel(chips, device_ref, *refs):
-    parts, out_ref, sem = refs[:-2], refs[-2], refs[-1]
-    height = out_ref.shape[0] // (2 * chips)
+    flops = 2 * (early.size + late.size) * shape[1]
+    kernel = functools.partial(left_kernel, scale)
+    return call(kernel, outs, (early, late, *mixed), flops, 6)
+
+
+def token_kernel(own_ref, mixed_ref, left_ref, *refs):
+    returned, out_ref, held_ref, sem = refs[:-3], refs[-3], refs[-2], refs[-1]
+    total = own_ref[...] + dot(mixed_ref[...], left_ref[...], 1, 1)
+    for index in range(0, len(returned), 2):
+        total = total + rows_joined(returned[index : index + 2]).astype(jnp.float32)
+    held_ref[...] = total.astype(jnp.bfloat16)
+    copy = pltpu.make_async_copy(held_ref, out_ref, sem)
+    copy.start()
+    copy.wait()
+
+
+def token_total(own, mixed, left_factor, returned):
+    out = jax.ShapeDtypeStruct(own.shape, jnp.bfloat16)
+    args = (own, mixed, left_factor, *returned)
+    scratch = [pltpu.VMEM(own.shape, jnp.bfloat16), pltpu.SemaphoreType.DMA]
+    flops = 2 * own.size * mixed.shape[1]
+    return call(token_kernel, [out], args, flops, 4, scratch, None, [HBM])[0]
+
+
+def finish_kernel(chips, device_ref, total_ref, got_ref, *refs):
+    parts = refs[:-4]
+    right_ref, left_ref, held_ref, sem = refs[-4:]
+    height = right_ref.shape[0] // (2 * chips)
     device = device_ref[0]
     copies = []
     for side in range(2):
@@ -279,23 +319,32 @@
         for ref in parts[side * len(parts) // 2 : (side + 1) * len(parts) // 2]:
             for at in tiles(ref.shape[0], height):
                 row = ((device & 1) ^ side) * chips + chip_at(device, side, chips, other)
-                target = out_ref.at[pl.ds(pl.multiple_of(row * height, height), height), :]
+                target = right_ref.at[pl.ds(pl.multiple_of(row * height, height), height), :]
                 copies.append(pltpu.make_async_copy(ref.at[at, :], target, sem.at[len(copies)]))
                 other += 1
     for copy in copies:
         copy.start()
+    held_ref[...] = (total_ref[...] + got_ref[...].astype(jnp.float32)).astype(jnp.bfloat16)
+    copies.append(pltpu.make_async_copy(held_ref, left_ref, sem.at[len(copies)]))
+    copies[-1].start()
     for copy in copies:
         copy.wait()
 
 
-def join(device, chips, parts):
-    out = jax.ShapeDtypeStruct(
-        (sum(part.shape[0] for part in parts), parts[0].shape[1]), jnp.bfloat16
-    )
-    specs = [SMEM] + [VMEM] * len(parts)
-    scratch = [pltpu.SemaphoreType.DMA((2 * chips,))]
-    kernel = functools.partial(join_kernel, chips)
-    return call(kernel, [out], (device, *parts), 0, 2, scratch, specs, [HBM])[0]
+def finish(device, chips, left_total, left_got, parts):
+    rows = sum(part.shape[0] for part in parts)
+    outs = [
+        jax.ShapeDtypeStruct((rows, parts[0].shape[1]), jnp.bfloat16),
+        jax.ShapeDtypeStruct(left_total.shape, jnp.bfloat16),
+    ]
+    specs = [SMEM] + [VMEM] * (len(parts) + 2)
+    scratch = [
+        pltpu.VMEM(left_total.shape, jnp.bfloat16),
+        pltpu.SemaphoreType.DMA((2 * chips + 1,)),
+    ]
+    kernel = functools.partial(finish_kernel, chips)
+    args = (device, left_total, left_got, *parts)
+    return call(kernel, outs, args, 0, 2, scratch, specs, [HBM, HBM])
 
 
 def body(tokens, blocks, left_factor, right_factor, upstream):
@@ -307,55 +356,47 @@
     norm_scale = 1.0 / float(tokens.shape[0] * group) ** 0.5
     device = lax.axis_index("dp").astype(jnp.int32).reshape(1)
 
+    partners = [swap_tensor(tokens, step, levels) for step in range(levels)]
     low, low_sent = low_partial(device, tokens, left_factor)
-    partners = []
     for step in range(levels):
         got = swap_tensor(low_sent, step, levels)
-        partners.append(swap_tensor(tokens, step, levels))
         if step < levels - 1:
             low, low_sent = add(low, got)
     running, held = first(device, tokens, blocks)
-    token_parts = [tokens]
-    for step in reversed(range(steps)):
-        sent = jnp.concatenate(token_parts) if len(token_parts) > 1 else tokens
-        token_parts.append(swap_chips(sent, step, steps))
+    token_parts = gather_chips(tokens, steps)
     for step in range(levels - 1):
-        running = forward(device, step, partners[step], held, running)
+        running = forward(device, step, [partners[step]], held, running)
     activated, slopes, mixed, mixed_sent, keep, send = middle(
         device, levels - 1, chips, running, partners[-1], held, low, got, right_factor, upstream
     )
-    turned = turn(token_parts)
+    early, late = turn(token_parts[:-1]), turn(token_parts[-1:])
 
     mine = keep + swap_core(send).astype(f32)
     for step in range(steps):
         half = mine.shape[0] // 2
         got = swap_chips(mine[half:].astype(bf16), step, steps)
         mine = mine[:half] + got.astype(f32)
-    pieces = [(mine * norm_scale).astype(bf16)]
+    piece = (mine * norm_scale).astype(bf16)
 
     returned = []
     for step in range(levels):
         got = swap_tensor(mixed_sent, step, levels)
-        mixed, mixed_sent = add(mixed, got)
-        part = backward(device, step, slopes, held, bf16)
-        returned.append(swap_tensor(part, step, levels))
-    token_sum = backward(device, None, slopes, held, f32)
-
-    rows_parts = [mixed_sent]
-    for step in reversed(range(steps)):
-        sent = jnp.concatenate(pieces) if len(pieces) > 1 else pieces[0]
-        pieces.append(swap_chips(sent, step, steps))
-        sent = jnp.concatenate(rows_parts) if len(rows_parts) > 1 else mixed_sent
-        rows_parts.append(swap_chips(sent, step, steps))
-    left_total, left_sent = left_partial(turned, rows_parts, norm_scale)
-    left_grad = (left_total + swap_core(left_sent).astype(f32)).astype(bf16)
+        if step < levels - 1:
+            mixed, mixed_sent = add(mixed, got)
+        else:
+            mixed_rows = add(mixed, got, (bf16,))[0]
+        parts = backward(device, step, slopes, held, bf16, 2)
+        returned += [swap_tensor(part, step, levels) for part in parts]
+    own = backward(device, None, slopes, held, f32, 1)[0]
+
+    pieces = gather_chips(piece, steps)
+    rows_parts = gather_chips(mixed_rows, steps)
+    left_total, left_sent = left_partial(early, late, rows_parts, norm_scale)
+    left_got = swap_core(left_sent)
     pieces += [swap_core(part) for part in pieces]
-    right_grad = join(device, chips, pieces)
-
-    token_sum = token_sum + dot(mixed_sent, left_factor, 1, 1)
-    for part in returned:
-        token_sum = token_sum + part.astype(f32)
-    return activated, token_sum.astype(bf16), left_grad, right_grad
+    right_grad, left_grad = finish(device, chips, left_total, left_got, pieces)
+    token_grad = token_total(own, mixed_rows, left_factor, returned)
+    return activated, token_grad, left_grad, right_grad
 
 
 def solution(mesh):

time: 82.9 us -> 92.7 us (1.12)
  waiting for transfers between devices: 30.3 us -> 39.7 us
  starting transfers between devices: 26.2 us -> 28.1 us
  other arithmetic: 2.17 us -> 0.28 us
    ppermute x21 -> x27, waiting for transfers between devices: 30.3 us -> 39.7 us  [swap(): return lax.ppermute(block, axes, route)]
    ppermute x21 -> x27, starting transfers between devices: 26.2 us -> 28.1 us  [swap(): return lax.ppermute(block, axes, route)]
    convert_element_type x3 -> x1, other arithmetic: 1.8 us -> 0.06 us  [body(): piece = (mine * norm_scale).astype(bf16)]
    pallas_call x13 -> x15, Pallas kernels: 19.4 us -> 19.9 us  [call(): pl.pallas_call(kernel, out_shape=outs, in_specs=in_specs or [VMEM] * len(...]
  transfers between devices with their start and end apart: 21 -> 27, of which waited for: 10 -> 10; matrix products, arithmetic and copies ran while one was open for 3% -> 0% of each run, Pallas kernels for 16% -> 15%
where the time goes in v2:
time: 92.7 us; the launch traced here: 92.4 us
  waiting for transfers between devices  39.7 us (43%)
  starting transfers between devices  28.1 us (30%)
  Pallas kernels  19.9 us (21%)
  local copies, waits for them, and re-layouts  3.49 us (4%)
    ppermute x27, waiting for transfers between devices, swap(): return lax.ppermute(block, axes, route)  39.7 us
    ppermute x27, starting transfers between devices, swap(): return lax.ppermute(block, axes, route)  28.1 us
    pallas_call x15, Pallas kernels, call(): pl.pallas_call(kernel, out_shape=outs, in_specs=in_specs or [VMEM] * len(...  19.9 us
    unnamed x14, local copies, waits for them, and re-layouts  3.42 us
  transfers between devices with their start and end apart: 27, of which 10 were waited for; matrix products, arithmetic and copies ran while one was open for 0% of the time, Pallas kernels for 15%

profile of v2, /device:TPU:0, one launch (start us, length us, event | category | flops | bytes accessed | tf_op | source)
XLA Modules:
  0.0 92.4 jit_solution(2824903430124220623)
XLA Ops:
  0.6 3.1 %collective-permute-start = (bf16[256,768]{1,0:T(8,128)(2,1)}, bf16[256,768]{1,0:T(8,128)(2,1)S(1)}, u32[]{:S(2)}, u32[]{:S(2)}) collective-permute-start(bf16[256,768]{1,0:T(8,128)(2,1)} %refs_0_.1), channel_id=1, source_target_pairs={{0,1},{1,0},{2,3},{3,2},{4,6},{5,7},{6,4},{7,5},{8,9},{9,8},{10,11... | collective-permute-start | bytes 1179656 | tf_op jit(solution)/shard_map/ppermute | solution.py:24
  3.7 2.6 %collective-permute-start.1 = (bf16[256,768]{1,0:T(8,128)(2,1)}, bf16[256,768]{1,0:T(8,128)(2,1)S(1)}, u32[]{:S(2)}, u32[]{:S(2)}) collective-permute-start(bf16[256,768]{1,0:T(8,128)(2,1)} %refs_0_.1), channel_id=1, source_target_pairs={{0,2},{1,3},{2,0},{3,1},{4,5},{5,4},{6,7},{7,6},{8,10},{9,11},{10,... | collective-permute-start | bytes 1179656 | tf_op jit(solution)/shard_map/ppermute | solution.py:24
  6.3 1.0 %copy-done = bf16[256,768]{1,0:T(8,128)(2,1)S(1)} copy-done((bf16[256,768]{1,0:T(8,128)(2,1)S(1)}, bf16[256,768]{1,0:T(8,128)(2,1)}, u32[]{:S(2)}) %copy-start) | copy-done | bytes 393240
  7.4 1.0 %copy-done.5 = bf16[768,256]{1,0:T(8,128)(2,1)S(1)} copy-done((bf16[768,256]{1,0:T(8,128)(2,1)S(1)}, bf16[768,256]{1,0:T(8,128)(2,1)}, u32[]{:S(2)}) %copy-start.5) | copy-done | bytes 393240
  8.4 0.3 shard_map.86
  8.6 0.5 collective-permute-start.2
  9.2 15.7 %collective-permute-done.2.got_ref = bf16[256,256]{1,0:T(8,128)(2,1)S(1)} collective-permute-done((bf16[256,256]{1,0:T(8,128)(2,1)S(1)}, bf16[256,256]{1,0:T(8,128)(2,1)S(1)}, u32[]{:S(2)}, u32[]{:S(2)}) %collective-permute-start.2) | collective-permute-done | bytes 131104 | tf_op jit(solution)/shard_map/ppermute | solution.py:24
  24.9 2.2 %collective-permute-start.3 = (bf16[256,256]{1,0:T(8,128)(2,1)S(1)}, bf16[256,256]{1,0:T(8,128)(2,1)S(1)}, u32[]{:S(2)}, u32[]{:S(2)}) collective-permute-start(bf16[256,256]{1,0:T(8,128)(2,1)S(1)} %get-tuple-element.31), channel_id=1, source_target_pairs={{0,2},{1,3},{2,0},{3,1},{4,5},{5,4},{6,7},{7,6},{8,10},{9,11},{10,... | collective-permute-start | bytes 393224 | tf_op jit(solution)/shard_map/ppermute | solution.py:24
  27.2 1.0 %copy-done.1 = bf16[256,768]{1,0:T(8,128)(2,1)S(1)} copy-done((bf16[256,768]{1,0:T(8,128)(2,1)S(1)}, bf16[256,768]{1,0:T(8,128)(2,1)}, u32[]{:S(2)}) %copy-start.1) | copy-done | bytes 393240
  28.1 5.2 %shard_map.84 = (f32[256,3072]{1,0:T(8,128)S(1)}, bf16[3,768,3072]{2,1,0:T(8,128)(2,1)S(1)}) custom-call(s32[1]{0:T(128)} %bitcast.device_ref, bf16[256,768]{1,0:T(8,128)(2,1)S(1)} %copy-done.1, bf16[3,768,3072]{2,1,0:T(8,128)(2,1)} %b_ref.1), custom_call_target="tpu_custom_call" | custom-call | flops 1207959552 | bytes 3981312 | tf_op jit(solution)/shard_map/pallas_call | solution.py:51
  33.4 1.4 %shard_map.85.pre_ref = f32[256,3072]{1,0:T(8,128)S(1)} custom-call(s32[1]{0:T(128)} %bitcast.device_ref, bf16[3,768,3072]{2,1,0:T(8,128)(2,1)S(1)} %get-tuple-element.26.b_ref, f32[256,3072]{1,0:T(8,128)S(1)} %get-tuple-element.27.running_ref, bf16[256,768]{1,0:T(8,128)(2,1)S(1)} %collective-permute-done.refs_0_), custom_call_target="tpu_custom_call" | custom-call | flops 1207959552 | bytes 2605056 | tf_op jit(solution)/shard_map/pallas_call | solution.py:51
  34.9 0.4 copy-done.4
  35.3 5.1 %shard_map.88 = (bf16[256,3072]{1,0:T(8,128)(2,1)}, bf16[256,3072]{1,0:T(8,128)(2,1)S(1)}, f32[256,256]{1,0:T(8,128)S(1)}, bf16[256,256]{1,0:T(8,128)(2,1)S(1)},...) custom-call(s32[1]{0:T(128)} %bitcast.device_ref, f32[256,3072]{1,0:T(8,128)S(1)} %shard_map.85.pre_ref, ...), custom_call_target="tpu_custom_call" | custom-call | flops 2415919104 | bytes 3391488 | tf_op jit(solution)/shard_map/pallas_call | solution.py:51
  40.4 2.3 %collective-permute-done.17 = bf16[128,3072]{1,0:T(8,128)(2,1)S(1)} collective-permute-done((bf16[128,3072]{1,0:T(8,128)(2,1)S(1)}, bf16[128,3072]{1,0:T(8,128)(2,1)S(1)}, u32[]{:S(2)}, u32[]{:S(2)}) %collective-permute-start.17) | collective-permute-done | bytes 786464 | tf_op jit(solution)/shard_map/ppermute | solution.py:24
  42.7 0.2 convert_add_fusion
  42.9 1.6 %collective-permute-start.18 = (bf16[64,3072]{1,0:T(8,128)(2,1)S(1)}, bf16[64,3072]{1,0:T(8,128)(2,1)S(1)}, u32[]{:S(2)}, u32[]{:S(2)}) collective-permute-start(bf16[64,3072]{1,0:T(8,128)(2,1)S(1)} %slice.30), channel_id=1, source_target_pairs={{0,8},{4,20},{8,0},{12,28},{16,24},{20,4},{24,16},{28,12},{1,9},{5... | collective-permute-start | bytes 1179656 | tf_op jit(solution)/shard_map/ppermute | solution.py:24
  44.4 1.5 %collective-permute-start.10 = (bf16[256,768]{1,0:T(8,128)(2,1)S(1)}, bf16[256,768]{1,0:T(8,128)(2,1)S(1)}, u32[]{:S(2)}, u32[]{:S(2)}) collective-permute-start(bf16[256,768]{1,0:T(8,128)(2,1)S(1)} %copy-done.2), channel_id=1, source_target_pairs={{0,16},{4,12},{8,24},{12,4},{16,0},{20,28},{24,8},{28,20},{1,17},{... | collective-permute-start | bytes 1179656 | tf_op jit(solution)/shard_map/ppermute | solution.py:24
  46.0 0.9 collective-permute-start.4
  46.8 7.7 %collective-permute-done.18 = bf16[64,3072]{1,0:T(8,128)(2,1)S(1)} collective-permute-done((bf16[64,3072]{1,0:T(8,128)(2,1)S(1)}, bf16[64,3072]{1,0:T(8,128)(2,1)S(1)}, u32[]{:S(2)}, u32[]{:S(2)}) %collective-permute-start.18) | collective-permute-done | bytes 393248 | tf_op jit(solution)/shard_map/ppermute | solution.py:24
  54.6 1.9 %collective-permute-start.19 = (bf16[32,3072]{1,0:T(8,128)(2,1)S(1)}, bf16[32,3072]{1,0:T(8,128)(2,1)S(1)}, u32[]{:S(2)}, u32[]{:S(2)}) collective-permute-start(bf16[32,3072]{1,0:T(8,128)(2,1)S(1)} %slice.31), channel_id=1, source_target_pairs={{0,16},{4,12},{8,24},{12,4},{16,0},{20,28},{24,8},{28,20},{1,17},{... | collective-permute-start | bytes 589832 | tf_op jit(solution)/shard_map/ppermute | solution.py:24
  56.5 1.6 %collective-permute-start.5 = (bf16[256,256]{1,0:T(8,128)(2,1)S(1)}, bf16[256,256]{1,0:T(8,128)(2,1)S(1)}, u32[]{:S(2)}, u32[]{:S(2)}) collective-permute-start(bf16[256,256]{1,0:T(8,128)(2,1)S(1)} %get-tuple-element.37), channel_id=1, source_target_pairs={{0,2},{1,3},{2,0},{3,1},{4,5},{5,4},{6,7},{7,6},{8,10},{9,11},{10,... | collective-permute-start | bytes 393224 | tf_op jit(solution)/shard_map/ppermute | solution.py:24
  58.2 1.5 %collective-permute-start.11 = (bf16[256,768]{1,0:T(8,128)(2,1)S(1)}, bf16[256,768]{1,0:T(8,128)(2,1)S(1)}, u32[]{:S(2)}, u32[]{:S(2)}) collective-permute-start(bf16[256,768]{1,0:T(8,128)(2,1)S(1)} %copy-done.2), channel_id=1, source_target_pairs={{0,8},{4,20},{8,0},{12,28},{16,24},{20,4},{24,16},{28,12},{1,9},{5... | collective-permute-start | bytes 1179656 | tf_op jit(solution)/shard_map/ppermute | solution.py:24
  59.7 1.4 %shard_map.93 = (bf16[128,768]{1,0:T(8,128)(2,1)S(1)}, bf16[128,768]{1,0:T(8,128)(2,1)S(1)}) custom-call(s32[1]{0:T(128)} %bitcast.device_ref, bf16[256,3072]{1,0:T(8,128)(2,1)S(1)} %get-tuple-element.33.s_ref, bf16[3,768,3072]{2,1,0:T(8,128)(2,1)S(1)} %get-tuple-element.26.b_ref), custom_call_target="tpu_custom_call" | custom-call | flops 1207959552 | bytes 2015232 | tf_op jit(solution)/shard_map/pallas_call | solution.py:51
  61.1 1.4 %collective-permute-start.8 = (bf16[128,768]{1,0:T(8,128)(2,1)S(1)}, bf16[128,768]{1,0:T(8,128)(2,1)S(1)}, u32[]{:S(2)}, u32[]{:S(2)}) collective-permute-start(bf16[128,768]{1,0:T(8,128)(2,1)S(1)} %get-tuple-element.40), channel_id=1, source_target_pairs={{0,2},{1,3},{2,0},{3,1},{4,5},{5,4},{6,7},{7,6},{8,10},{9,11},{10,... | collective-permute-start | bytes 589832 | tf_op jit(solution)/shard_map/ppermute | solution.py:24
  62.5 1.6 %collective-permute-start.9 = (bf16[128,768]{1,0:T(8,128)(2,1)S(1)}, bf16[128,768]{1,0:T(8,128)(2,1)S(1)}, u32[]{:S(2)}, u32[]{:S(2)}) collective-permute-start(bf16[128,768]{1,0:T(8,128)(2,1)S(1)} %get-tuple-element.41), channel_id=1, source_target_pairs={{0,2},{1,3},{2,0},{3,1},{4,5},{5,4},{6,7},{7,6},{8,10},{9,11},{10,... | collective-permute-start | bytes 589832 | tf_op jit(solution)/shard_map/ppermute | solution.py:24
  64.1 1.0 %collective-permute-start.12 = (bf16[256,768]{1,0:T(8,128)(2,1)S(1)}, bf16[256,768]{1,0:T(8,128)(2,1)S(1)}, u32[]{:S(2)}, u32[]{:S(2)}) collective-permute-start(bf16[256,768]{1,0:T(8,128)(2,1)S(1)} %collective-permute-done.10.refs_1_), channel_id=1, source_target_pairs={{0,8},{4,20},{8,0},{12,28},{16,24},{20,4},{24,16},{28,12},{1,9},{5... | collective-permute-start | bytes 1179656 | tf_op jit(solution)/shard_map/ppermute | solution.py:24
  65.1 0.3 collective-permute-start.13
  65.5 2.9 %collective-permute-done.11.refs_2_ = bf16[256,768]{1,0:T(8,128)(2,1)S(1)} collective-permute-done((bf16[256,768]{1,0:T(8,128)(2,1)S(1)}, bf16[256,768]{1,0:T(8,128)(2,1)S(1)}, u32[]{:S(2)}, u32[]{:S(2)}) %collective-permute-start.11) | collective-permute-done | bytes 393248 | tf_op jit(solution)/shard_map/ppermute | solution.py:24
  68.3 2.3 %collective-permute-done.13.refs_1_ = bf16[256,256]{1,0:T(8,128)(2,1)S(1)} collective-permute-done((bf16[256,256]{1,0:T(8,128)(2,1)S(1)}, bf16[256,256]{1,0:T(8,128)(2,1)S(1)}, u32[]{:S(2)}, u32[]{:S(2)}) %collective-permute-start.13) | collective-permute-done | bytes 131104 | tf_op jit(solution)/shard_map/ppermute | solution.py:24
  70.7 0.8 collective-permute-start.14
  71.5 2.2 %collective-permute-done.12.refs_0_ = bf16[256,768]{1,0:T(8,128)(2,1)S(1)} collective-permute-done((bf16[256,768]{1,0:T(8,128)(2,1)S(1)}, bf16[256,768]{1,0:T(8,128)(2,1)S(1)}, u32[]{:S(2)}, u32[]{:S(2)}) %collective-permute-start.12) | collective-permute-done | bytes 393248 | tf_op jit(solution)/shard_map/ppermute | solution.py:24
  73.7 0.5 collective-permute-start.15
  74.1 0.4 shard_map.95.early_ref
  74.5 1.4 %shard_map.92 = (bf16[128,768]{1,0:T(8,128)(2,1)S(1)}, bf16[128,768]{1,0:T(8,128)(2,1)S(1)}) custom-call(s32[1]{0:T(128)} %bitcast.device_ref, bf16[256,3072]{1,0:T(8,128)(2,1)S(1)} %get-tuple-element.33.s_ref, bf16[3,768,3072]{2,1,0:T(8,128)(2,1)S(1)} %get-tuple-element.26.b_ref), custom_call_target="tpu_custom_call" | custom-call | flops 1207959552 | bytes 2015232 | tf_op jit(solution)/shard_map/pallas_call | solution.py:51
  76.0 0.2 shard_map.96.late_ref
  76.1 1.2 %collective-permute-start.6 = (bf16[128,768]{1,0:T(8,128)(2,1)S(1)}, bf16[128,768]{1,0:T(8,128)(2,1)S(1)}, u32[]{:S(2)}, u32[]{:S(2)}) collective-permute-start(bf16[128,768]{1,0:T(8,128)(2,1)S(1)} %get-tuple-element.38), channel_id=1, source_target_pairs={{0,1},{1,0},{2,3},{3,2},{4,6},{5,7},{6,4},{7,5},{8,9},{9,8},{10,11... | collective-permute-start | bytes 589832 | tf_op jit(solution)/shard_map/ppermute | solution.py:24
  77.3 1.3 %collective-permute-done.15.refs_3_ = bf16[256,256]{1,0:T(8,128)(2,1)S(1)} collective-permute-done((bf16[256,256]{1,0:T(8,128)(2,1)S(1)}, bf16[256,256]{1,0:T(8,128)(2,1)S(1)}, u32[]{:S(2)}, u32[]{:S(2)}) %collective-permute-start.15) | collective-permute-done | bytes 131104 | tf_op jit(solution)/shard_map/ppermute | solution.py:24
  78.6 1.3 %collective-permute-start.7 = (bf16[128,768]{1,0:T(8,128)(2,1)S(1)}, bf16[128,768]{1,0:T(8,128)(2,1)S(1)}, u32[]{:S(2)}, u32[]{:S(2)}) collective-permute-start(bf16[128,768]{1,0:T(8,128)(2,1)S(1)} %get-tuple-element.39), channel_id=1, source_target_pairs={{0,1},{1,0},{2,3},{3,2},{4,6},{5,7},{6,4},{7,5},{8,9},{9,8},{10,11... | collective-permute-start | bytes 589832 | tf_op jit(solution)/shard_map/ppermute | solution.py:24
  79.9 0.6 shard_map.97
  80.6 0.4 collective-permute-start.21
  81.0 1.7 %collective-permute-start.22 = (bf16[32,3072]{1,0:T(8,128)(2,1)S(1)}, bf16[32,3072]{1,0:T(8,128)(2,1)S(1)}, u32[]{:S(2)}, u32[]{:S(2)}) collective-permute-start(bf16[32,3072]{1,0:T(8,128)(2,1)S(1)} %collective-permute-done.20.refs_1_), channel_id=1, source_target_pairs={{0,8},{4,20},{8,0},{12,28},{16,24},{20,4},{24,16},{28,12},{1,9},{5... | collective-permute-start | bytes 589832 | tf_op jit(solution)/shard_map/ppermute | solution.py:24
  82.7 2.6 %collective-permute-done.6.refs_0_ = bf16[128,768]{1,0:T(8,128)(2,1)S(1)} collective-permute-done((bf16[128,768]{1,0:T(8,128)(2,1)S(1)}, bf16[128,768]{1,0:T(8,128)(2,1)S(1)}, u32[]{:S(2)}, u32[]{:S(2)}) %collective-permute-start.6) | collective-permute-done | bytes 196640 | tf_op jit(solution)/shard_map/ppermute | solution.py:24
  85.3 2.1 %collective-permute-done.7.refs_1_ = bf16[128,768]{1,0:T(8,128)(2,1)S(1)} collective-permute-done((bf16[128,768]{1,0:T(8,128)(2,1)S(1)}, bf16[128,768]{1,0:T(8,128)(2,1)S(1)}, u32[]{:S(2)}, u32[]{:S(2)}) %collective-permute-start.7) | collective-permute-done | bytes 196640 | tf_op jit(solution)/shard_map/ppermute | solution.py:24
  87.5 0.5 collective-permute-start.25
  88.0 0.5 collective-permute-done.22.refs_3_
  88.5 1.4 %shard_map.89.own_ref = f32[256,768]{1,0:T(8,128)S(1)} custom-call(s32[1]{0:T(128)} %bitcast.device_ref, bf16[256,3072]{1,0:T(8,128)(2,1)S(1)} %get-tuple-element.33.s_ref, bf16[3,768,3072]{2,1,0:T(8,128)(2,1)S(1)} %get-tuple-element.26.b_ref), custom_call_target="tpu_custom_call" | custom-call | flops 1207959552 | bytes 2064384 | tf_op jit(solution)/shard_map/pallas_call | solution.py:51
  89.9 1.1 %shard_map.94 = bf16[256,768]{1,0:T(8,128)(2,1)} custom-call(f32[256,768]{1,0:T(8,128)S(1)} %shard_map.89.own_ref, bf16[256,256]{1,0:T(8,128)(2,1)S(1)} %shard_map.91.mixed_ref.refs_0_, bf16[768,256]{1,0:T(8,128)(2,1)S(1)} %copy-done.6, bf16[128,768]{1,0:T(8,128)(2,1)S(1)} %collective-permute-done.6.refs_0_, ...), custom_call_target="tpu_custom_call" | custom-call | flops 100663296 | bytes 311296 | tf_op jit(solution)/shard_map/pallas_call | solution.py:51
  91.1 1.4 %shard_map.98 = (bf16[256,3072]{1,0:T(8,128)(2,1)}, bf16[768,256]{1,0:T(8,128)(2,1)}) custom-call(s32[1]{0:T(128)} %bitcast.device_ref, f32[768,256]{1,0:T(8,128)S(1)} %get-tuple-element.42.total_ref, bf16[768,256]{1,0:T(8,128)(2,1)S(1)} %collective-permute-done.16.got_ref, bf16[32,3072]{1,0:T(8,128)(2,1)S(1)} %fusion.1.refs_0_, ...), custom_call_target="tpu_custom_call" | custom-call | bytes 589824 | tf_op jit(solution)/shard_map/pallas_call | solution.py:51
  (40 shorter events, 0.4 us)
Async XLA Ops:
  0.6 32.8 %collective-permute-start = (bf16[256,768]{1,0:T(8,128)(2,1)}, bf16[256,768]{1,0:T(8,128)(2,1)S(1)}, u32[]{:S(2)}, u32[]{:S(2)}) collective-permute-start(bf16[256,768]{1,0:T(8,128)(2,1)} %refs_0_.1), channel_id=1, source_target_pairs={{0,1},{1,0},{2,3},{3,2},{4,6},{5,7},{6,4},{7,5},{8,9},{9,8},{10,11... | collective-permute-start | bytes 1179656 | tf_op jit(solution)/shard_map/ppermute | solution.py:24
  3.7 31.1 %collective-permute-start.1 = (bf16[256,768]{1,0:T(8,128)(2,1)}, bf16[256,768]{1,0:T(8,128)(2,1)S(1)}, u32[]{:S(2)}, u32[]{:S(2)}) collective-permute-start(bf16[256,768]{1,0:T(8,128)(2,1)} %refs_0_.1), channel_id=1, source_target_pairs={{0,2},{1,3},{2,0},{3,1},{4,5},{5,4},{6,7},{7,6},{8,10},{9,11},{10,... | collective-permute-start | bytes 1179656 | tf_op jit(solution)/shard_map/ppermute | solution.py:24
  6.3 1.0 %copy-start = (bf16[256,768]{1,0:T(8,128)(2,1)S(1)}, bf16[256,768]{1,0:T(8,128)(2,1)}, u32[]{:S(2)}) copy-start(bf16[256,768]{1,0:T(8,128)(2,1)} %refs_0_.1) | copy-start | bytes 1179652
  7.4 1.0 %copy-start.5 = (bf16[768,256]{1,0:T(8,128)(2,1)S(1)}, bf16[768,256]{1,0:T(8,128)(2,1)}, u32[]{:S(2)}) copy-start(bf16[768,256]{1,0:T(8,128)(2,1)} %left_ref.3) | copy-start | bytes 1179652
  8.6 16.2 %collective-permute-start.2 = (bf16[256,256]{1,0:T(8,128)(2,1)S(1)}, bf16[256,256]{1,0:T(8,128)(2,1)S(1)}, u32[]{:S(2)}, u32[]{:S(2)}) collective-permute-start(bf16[256,256]{1,0:T(8,128)(2,1)S(1)} %get-tuple-element.29), channel_id=1, source_target_pairs={{0,1},{1,0},{2,3},{3,2},{4,6},{5,7},{6,4},{7,5},{8,9},{9,8},{10,11... | collective-permute-start | bytes 393224 | tf_op jit(solution)/shard_map/ppermute | solution.py:24
  24.9 9.9 %collective-permute-start.3 = (bf16[256,256]{1,0:T(8,128)(2,1)S(1)}, bf16[256,256]{1,0:T(8,128)(2,1)S(1)}, u32[]{:S(2)}, u32[]{:S(2)}) collective-permute-start(bf16[256,256]{1,0:T(8,128)(2,1)S(1)} %get-tuple-element.31), channel_id=1, source_target_pairs={{0,2},{1,3},{2,0},{3,1},{4,5},{5,4},{6,7},{7,6},{8,10},{9,11},{10,... | collective-permute-start | bytes 393224 | tf_op jit(solution)/shard_map/ppermute | solution.py:24
  27.1 1.0 %copy-start.1 = (bf16[256,768]{1,0:T(8,128)(2,1)S(1)}, bf16[256,768]{1,0:T(8,128)(2,1)}, u32[]{:S(2)}) copy-start(bf16[256,768]{1,0:T(8,128)(2,1)} %refs_0_.1) | copy-start | bytes 1179652
  33.4 1.5 %copy-start.3 = (bf16[256,3072]{1,0:T(8,128)(2,1)S(1)}, bf16[256,3072]{1,0:T(8,128)(2,1)}, u32[]{:S(2)}) copy-start(bf16[256,3072]{1,0:T(8,128)(2,1)} %right_ref.1) | copy-start | bytes 4718596
  33.4 1.9 %copy-start.4 = (bf16[256,3072]{1,0:T(8,128)(2,1)S(1)}, bf16[256,3072]{1,0:T(8,128)(2,1)}, u32[]{:S(2)}) copy-start(bf16[256,3072]{1,0:T(8,128)(2,1)} %up_ref.1) | copy-start | bytes 4718596
  40.4 2.3 %collective-permute-start.17 = (bf16[128,3072]{1,0:T(8,128)(2,1)S(1)}, bf16[128,3072]{1,0:T(8,128)(2,1)S(1)}, u32[]{:S(2)}, u32[]{:S(2)}) collective-permute-start(bf16[128,3072]{1,0:T(8,128)(2,1)S(1)} %get-tuple-element.45), channel_id=1, source_target_pairs={{0,4},{4,0},{8,12},{12,8},{16,20},{20,16},{24,28},{28,24},{1,5},{5... | collective-permute-start | bytes 2359304 | tf_op jit(solution)/shard_map/ppermute | solution.py:24
  42.7 1.8 %copy-start.2 = (bf16[256,768]{1,0:T(8,128)(2,1)S(1)}, bf16[256,768]{1,0:T(8,128)(2,1)}, u32[]{:S(2)}) copy-start(bf16[256,768]{1,0:T(8,128)(2,1)} %refs_0_.1) | copy-start | bytes 1179652
  42.9 11.6 %collective-permute-start.18 = (bf16[64,3072]{1,0:T(8,128)(2,1)S(1)}, bf16[64,3072]{1,0:T(8,128)(2,1)S(1)}, u32[]{:S(2)}, u32[]{:S(2)}) collective-permute-start(bf16[64,3072]{1,0:T(8,128)(2,1)S(1)} %slice.30), channel_id=1, source_target_pairs={{0,8},{4,20},{8,0},{12,28},{16,24},{20,4},{24,16},{28,12},{1,9},{5... | collective-permute-start | bytes 1179656 | tf_op jit(solution)/shard_map/ppermute | solution.py:24
  44.4 18.1 %collective-permute-start.10 = (bf16[256,768]{1,0:T(8,128)(2,1)S(1)}, bf16[256,768]{1,0:T(8,128)(2,1)S(1)}, u32[]{:S(2)}, u32[]{:S(2)}) collective-permute-start(bf16[256,768]{1,0:T(8,128)(2,1)S(1)} %copy-done.2), channel_id=1, source_target_pairs={{0,16},{4,12},{8,24},{12,4},{16,0},{20,28},{24,8},{28,20},{1,17},{... | collective-permute-start | bytes 1179656 | tf_op jit(solution)/shard_map/ppermute | solution.py:24
  46.0 10.6 %collective-permute-start.4 = (bf16[256,256]{1,0:T(8,128)(2,1)S(1)}, bf16[256,256]{1,0:T(8,128)(2,1)S(1)}, u32[]{:S(2)}, u32[]{:S(2)}) collective-permute-start(bf16[256,256]{1,0:T(8,128)(2,1)S(1)} %get-tuple-element.35), channel_id=1, source_target_pairs={{0,1},{1,0},{2,3},{3,2},{4,6},{5,7},{6,4},{7,5},{8,9},{9,8},{10,11... | collective-permute-start | bytes 393224 | tf_op jit(solution)/shard_map/ppermute | solution.py:24
  54.6 10.5 %collective-permute-start.19 = (bf16[32,3072]{1,0:T(8,128)(2,1)S(1)}, bf16[32,3072]{1,0:T(8,128)(2,1)S(1)}, u32[]{:S(2)}, u32[]{:S(2)}) collective-permute-start(bf16[32,3072]{1,0:T(8,128)(2,1)S(1)} %slice.31), channel_id=1, source_target_pairs={{0,16},{4,12},{8,24},{12,4},{16,0},{20,28},{24,8},{28,20},{1,17},{... | collective-permute-start | bytes 589832 | tf_op jit(solution)/shard_map/ppermute | solution.py:24
  56.5 7.5 %collective-permute-start.5 = (bf16[256,256]{1,0:T(8,128)(2,1)S(1)}, bf16[256,256]{1,0:T(8,128)(2,1)S(1)}, u32[]{:S(2)}, u32[]{:S(2)}) collective-permute-start(bf16[256,256]{1,0:T(8,128)(2,1)S(1)} %get-tuple-element.37), channel_id=1, source_target_pairs={{0,2},{1,3},{2,0},{3,1},{4,5},{5,4},{6,7},{7,6},{8,10},{9,11},{10,... | collective-permute-start | bytes 393224 | tf_op jit(solution)/shard_map/ppermute | solution.py:24
  58.2 10.2 %collective-permute-start.11 = (bf16[256,768]{1,0:T(8,128)(2,1)S(1)}, bf16[256,768]{1,0:T(8,128)(2,1)S(1)}, u32[]{:S(2)}, u32[]{:S(2)}) collective-permute-start(bf16[256,768]{1,0:T(8,128)(2,1)S(1)} %copy-done.2), channel_id=1, source_target_pairs={{0,8},{4,20},{8,0},{12,28},{16,24},{20,4},{24,16},{28,12},{1,9},{5... | collective-permute-start | bytes 1179656 | tf_op jit(solution)/shard_map/ppermute | solution.py:24
  61.1 19.4 %collective-permute-start.8 = (bf16[128,768]{1,0:T(8,128)(2,1)S(1)}, bf16[128,768]{1,0:T(8,128)(2,1)S(1)}, u32[]{:S(2)}, u32[]{:S(2)}) collective-permute-start(bf16[128,768]{1,0:T(8,128)(2,1)S(1)} %get-tuple-element.40), channel_id=1, source_target_pairs={{0,2},{1,3},{2,0},{3,1},{4,5},{5,4},{6,7},{7,6},{8,10},{9,11},{10,... | collective-permute-start | bytes 589832 | tf_op jit(solution)/shard_map/ppermute | solution.py:24
  62.5 18.1 %collective-permute-start.9 = (bf16[128,768]{1,0:T(8,128)(2,1)S(1)}, bf16[128,768]{1,0:T(8,128)(2,1)S(1)}, u32[]{:S(2)}, u32[]{:S(2)}) collective-permute-start(bf16[128,768]{1,0:T(8,128)(2,1)S(1)} %get-tuple-element.41), channel_id=1, source_target_pairs={{0,2},{1,3},{2,0},{3,1},{4,5},{5,4},{6,7},{7,6},{8,10},{9,11},{10,... | collective-permute-start | bytes 589832 | tf_op jit(solution)/shard_map/ppermute | solution.py:24
  64.1 9.6 %collective-permute-start.12 = (bf16[256,768]{1,0:T(8,128)(2,1)S(1)}, bf16[256,768]{1,0:T(8,128)(2,1)S(1)}, u32[]{:S(2)}, u32[]{:S(2)}) collective-permute-start(bf16[256,768]{1,0:T(8,128)(2,1)S(1)} %collective-permute-done.10.refs_1_), channel_id=1, source_target_pairs={{0,8},{4,20},{8,0},{12,28},{16,24},{20,4},{24,16},{28,12},{1,9},{5... | collective-permute-start | bytes 1179656 | tf_op jit(solution)/shard_map/ppermute | solution.py:24
  65.1 5.5 %collective-permute-start.13 = (bf16[256,256]{1,0:T(8,128)(2,1)S(1)}, bf16[256,256]{1,0:T(8,128)(2,1)S(1)}, u32[]{:S(2)}, u32[]{:S(2)}) collective-permute-start(bf16[256,256]{1,0:T(8,128)(2,1)S(1)} %shard_map.91.mixed_ref.refs_0_), channel_id=1, source_target_pairs={{0,16},{4,12},{8,24},{12,4},{16,0},{20,28},{24,8},{28,20},{1,17},{... | collective-permute-start | bytes 393224 | tf_op jit(solution)/shard_map/ppermute | solution.py:24
  68.3 12.7 %collective-permute-start.20 = (bf16[32,3072]{1,0:T(8,128)(2,1)S(1)}, bf16[32,3072]{1,0:T(8,128)(2,1)S(1)}, u32[]{:S(2)}, u32[]{:S(2)}) collective-permute-start(bf16[32,3072]{1,0:T(8,128)(2,1)S(1)} %fusion.1.refs_0_), channel_id=1, source_target_pairs={{0,16},{4,12},{8,24},{12,4},{16,0},{20,28},{24,8},{28,20},{1,17},{... | collective-permute-start | bytes 589832 | tf_op jit(solution)/shard_map/ppermute | solution.py:24
  70.7 5.5 %collective-permute-start.14 = (bf16[256,256]{1,0:T(8,128)(2,1)S(1)}, bf16[256,256]{1,0:T(8,128)(2,1)S(1)}, u32[]{:S(2)}, u32[]{:S(2)}) collective-permute-start(bf16[256,256]{1,0:T(8,128)(2,1)S(1)} %shard_map.91.mixed_ref.refs_0_), channel_id=1, source_target_pairs={{0,8},{4,20},{8,0},{12,28},{16,24},{20,4},{24,16},{28,12},{1,9},{5... | collective-permute-start | bytes 393224 | tf_op jit(solution)/shard_map/ppermute | solution.py:24
  73.7 5.0 %collective-permute-start.15 = (bf16[256,256]{1,0:T(8,128)(2,1)S(1)}, bf16[256,256]{1,0:T(8,128)(2,1)S(1)}, u32[]{:S(2)}, u32[]{:S(2)}) collective-permute-start(bf16[256,256]{1,0:T(8,128)(2,1)S(1)} %collective-permute-done.13.refs_1_), channel_id=1, source_target_pairs={{0,8},{4,20},{8,0},{12,28},{16,24},{20,4},{24,16},{28,12},{1,9},{5... | collective-permute-start | bytes 393224 | tf_op jit(solution)/shard_map/ppermute | solution.py:24
  76.1 9.2 %collective-permute-start.6 = (bf16[128,768]{1,0:T(8,128)(2,1)S(1)}, bf16[128,768]{1,0:T(8,128)(2,1)S(1)}, u32[]{:S(2)}, u32[]{:S(2)}) collective-permute-start(bf16[128,768]{1,0:T(8,128)(2,1)S(1)} %get-tuple-element.38), channel_id=1, source_target_pairs={{0,1},{1,0},{2,3},{3,2},{4,6},{5,7},{6,4},{7,5},{8,9},{9,8},{10,11... | collective-permute-start | bytes 589832 | tf_op jit(solution)/shard_map/ppermute | solution.py:24
  78.6 8.8 %collective-permute-start.7 = (bf16[128,768]{1,0:T(8,128)(2,1)S(1)}, bf16[128,768]{1,0:T(8,128)(2,1)S(1)}, u32[]{:S(2)}, u32[]{:S(2)}) collective-permute-start(bf16[128,768]{1,0:T(8,128)(2,1)S(1)} %get-tuple-element.39), channel_id=1, source_target_pairs={{0,1},{1,0},{2,3},{3,2},{4,6},{5,7},{6,4},{7,5},{8,9},{9,8},{10,11... | collective-permute-start | bytes 589832 | tf_op jit(solution)/shard_map/ppermute | solution.py:24
  80.5 9.4 %copy-start.6 = (bf16[768,256]{1,0:T(8,128)(2,1)S(1)}, bf16[768,256]{1,0:T(8,128)(2,1)}, u32[]{:S(2)}) copy-start(bf16[768,256]{1,0:T(8,128)(2,1)} %left_ref.3) | copy-start | bytes 1179652
  80.5 10.5 %collective-permute-start.16 = (bf16[768,256]{1,0:T(8,128)(2,1)S(1)}, bf16[768,256]{1,0:T(8,128)(2,1)S(1)}, u32[]{:S(2)}, u32[]{:S(2)}) collective-permute-start(bf16[768,256]{1,0:T(8,128)(2,1)S(1)} %get-tuple-element.43), channel_id=1, source_target_pairs={{0,4},{4,0},{8,12},{12,8},{16,20},{20,16},{24,28},{28,24},{1,5},{5... | collective-permute-start | bytes 1179656 | tf_op jit(solution)/shard_map/ppermute | solution.py:24
  80.6 6.8 %collective-permute-start.21 = (bf16[32,3072]{1,0:T(8,128)(2,1)S(1)}, bf16[32,3072]{1,0:T(8,128)(2,1)S(1)}, u32[]{:S(2)}, u32[]{:S(2)}) collective-permute-start(bf16[32,3072]{1,0:T(8,128)(2,1)S(1)} %fusion.1.refs_0_), channel_id=1, source_target_pairs={{0,8},{4,20},{8,0},{12,28},{16,24},{20,4},{24,16},{28,12},{1,9},{5... | collective-permute-start | bytes 589832 | tf_op jit(solution)/shard_map/ppermute | solution.py:24
  81.0 7.5 %collective-permute-start.22 = (bf16[32,3072]{1,0:T(8,128)(2,1)S(1)}, bf16[32,3072]{1,0:T(8,128)(2,1)S(1)}, u32[]{:S(2)}, u32[]{:S(2)}) collective-permute-start(bf16[32,3072]{1,0:T(8,128)(2,1)S(1)} %collective-permute-done.20.refs_1_), channel_id=1, source_target_pairs={{0,8},{4,20},{8,0},{12,28},{16,24},{20,4},{24,16},{28,12},{1,9},{5... | collective-permute-start | bytes 589832 | tf_op jit(solution)/shard_map/ppermute | solution.py:24
  85.3 5.7 %collective-permute-start.23 = (bf16[32,3072]{1,0:T(8,128)(2,1)S(1)}, bf16[32,3072]{1,0:T(8,128)(2,1)S(1)}, u32[]{:S(2)}, u32[]{:S(2)}) collective-permute-start(bf16[32,3072]{1,0:T(8,128)(2,1)S(1)} %fusion.1.refs_0_), channel_id=1, source_target_pairs={{0,4},{4,0},{8,12},{12,8},{16,20},{20,16},{24,28},{28,24},{1,5},{5... | collective-permute-start | bytes 589832 | tf_op jit(solution)/shard_map/ppermute | solution.py:24
  87.4 3.6 %collective-permute-start.24 = (bf16[32,3072]{1,0:T(8,128)(2,1)S(1)}, bf16[32,3072]{1,0:T(8,128)(2,1)S(1)}, u32[]{:S(2)}, u32[]{:S(2)}) collective-permute-start(bf16[32,3072]{1,0:T(8,128)(2,1)S(1)} %collective-permute-done.20.refs_1_), channel_id=1, source_target_pairs={{0,4},{4,0},{8,12},{12,8},{16,20},{20,16},{24,28},{28,24},{1,5},{5... | collective-permute-start | bytes 589832 | tf_op jit(solution)/shard_map/ppermute | solution.py:24
  87.5 3.6 %collective-permute-start.25 = (bf16[32,3072]{1,0:T(8,128)(2,1)S(1)}, bf16[32,3072]{1,0:T(8,128)(2,1)S(1)}, u32[]{:S(2)}, u32[]{:S(2)}) collective-permute-start(bf16[32,3072]{1,0:T(8,128)(2,1)S(1)} %collective-permute-done.21.refs_2_), channel_id=1, source_target_pairs={{0,4},{4,0},{8,12},{12,8},{16,20},{20,16},{24,28},{28,24},{1,5},{5... | collective-permute-start | bytes 589832 | tf_op jit(solution)/shard_map/ppermute | solution.py:24
  88.5 2.6 %collective-permute-start.26 = (bf16[32,3072]{1,0:T(8,128)(2,1)S(1)}, bf16[32,3072]{1,0:T(8,128)(2,1)S(1)}, u32[]{:S(2)}, u32[]{:S(2)}) collective-permute-start(bf16[32,3072]{1,0:T(8,128)(2,1)S(1)} %collective-permute-done.22.refs_3_), channel_id=1, source_target_pairs={{0,4},{4,0},{8,12},{12,8},{16,20},{20,16},{24,28},{28,24},{1,5},{5... | collective-permute-start | bytes 589832 | tf_op jit(solution)/shard_map/ppermute | solution.py:24

commit v3 on v2

--- a/solution.py
+++ b/solution.py
@@ -191,7 +191,7 @@
 
 
 def middle_kernel(
-    step, chips, device_ref, pre_ref, x_ref, b_ref, low_ref, got_ref, right_ref, up_ref,
+    chips, device_ref, pre_ref, low_ref, got_ref, right_ref, up_ref,
     act_ref, slope_ref, mixed_ref, mixed_sent_ref, keep_ref, send_ref, turned_ref, order_ref,
 ):
     rank = low_ref.shape[1]
@@ -208,13 +208,11 @@
             order_ref[target : target + piece, :] = turned_ref[
                 pl.ds(pl.multiple_of(source, piece), piece), :
             ].astype(jnp.bfloat16)
-    section = section_at(device, step, b_ref.shape[0] - 1)
-    x = x_ref[...]
     order = order_ref[...]
     mixed = None
     for at in tiles(up_ref.shape[1], 1024):
         right = right_ref[:, at]
-        value = pre_ref[:, at] + dot(x, b_ref[section, :, at], 1, 0) + dot(low, right, 1, 0)
+        value = pre_ref[:, at] + dot(low, right, 1, 0)
         act, slope = gelu_and_slope(value, up_ref[:, at].astype(jnp.float32))
         act_ref[:, at] = act.astype(jnp.bfloat16)
         slope = slope.astype(jnp.bfloat16)
@@ -228,7 +226,7 @@
     mixed_sent_ref[...] = mixed.astype(jnp.bfloat16)
 
 
-def middle(device, step, chips, running, x, blocks, low, got, right_factor, upstream):
+def middle(device, chips, running, low, got, right_factor, upstream):
     rows, cols = upstream.shape
     rank = low.shape[1]
     bf16, f32 = jnp.bfloat16, jnp.float32
@@ -240,10 +238,10 @@
         jax.ShapeDtypeStruct((rank // 2, cols), f32),
         jax.ShapeDtypeStruct((rank // 2, cols), bf16),
     ]
-    args = (device, running, x, blocks, low, got, right_factor, upstream)
-    flops = 2 * rows * cols * (x.shape[1] + 3 * rank)
+    args = (device, running, low, got, right_factor, upstream)
+    flops = 2 * rows * cols * 3 * rank
     scratch = [pltpu.VMEM((rank, rows), f32), pltpu.VMEM((rank, rows), bf16)]
-    kernel = functools.partial(middle_kernel, step, chips)
+    kernel = functools.partial(middle_kernel, chips)
     specs = [SMEM] + [VMEM] * (len(args) - 1)
     return call(kernel, outs, args, flops, 16, scratch, specs)
 
@@ -289,11 +287,12 @@
     return call(kernel, outs, (early, late, *mixed), flops, 6)
 
 
-def token_kernel(own_ref, mixed_ref, left_ref, *refs):
+def token_kernel(counts, own_ref, mixed_ref, left_ref, *refs):
     returned, out_ref, held_ref, sem = refs[:-3], refs[-3], refs[-2], refs[-1]
     total = own_ref[...] + dot(mixed_ref[...], left_ref[...], 1, 1)
-    for index in range(0, len(returned), 2):
-        total = total + rows_joined(returned[index : index + 2]).astype(jnp.float32)
+    for count in counts:
+        total = total + rows_joined(returned[:count]).astype(jnp.float32)
+        returned = returned[count:]
     held_ref[...] = total.astype(jnp.bfloat16)
     copy = pltpu.make_async_copy(held_ref, out_ref, sem)
     copy.start()
@@ -302,10 +301,11 @@
 
 def token_total(own, mixed, left_factor, returned):
     out = jax.ShapeDtypeStruct(own.shape, jnp.bfloat16)
-    args = (own, mixed, left_factor, *returned)
+    args = (own, mixed, left_factor, *(part for parts in returned for part in parts))
+    kernel = functools.partial(token_kernel, [len(parts) for parts in returned])
     scratch = [pltpu.VMEM(own.shape, jnp.bfloat16), pltpu.SemaphoreType.DMA]
     flops = 2 * own.size * mixed.shape[1]
-    return call(token_kernel, [out], args, flops, 4, scratch, None, [HBM])[0]
+    return call(kernel, [out], args, flops, 4, scratch, None, [HBM])[0]
 
 
 def finish_kernel(chips, device_ref, total_ref, got_ref, *refs):
@@ -364,10 +364,10 @@
             low, low_sent = add(low, got)
     running, held = first(device, tokens, blocks)
     token_parts = gather_chips(tokens, steps)
-    for step in range(levels - 1):
+    for step in range(levels):
         running = forward(device, step, [partners[step]], held, running)
     activated, slopes, mixed, mixed_sent, keep, send = middle(
-        device, levels - 1, chips, running, partners[-1], held, low, got, right_factor, upstream
+        device, chips, running, low, got, right_factor, upstream
     )
     early, late = turn(token_parts[:-1]), turn(token_parts[-1:])
 
@@ -385,8 +385,9 @@
             mixed, mixed_sent = add(mixed, got)
         else:
             mixed_rows = add(mixed, got, (bf16,))[0]
-        parts = backward(device, step, slopes, held, bf16, 2)
-        returned += [swap_tensor(part, step, levels) for part in parts]
+        count = 1 if step == levels - 1 else 2
+        parts = backward(device, step, slopes, held, bf16, count)
+        returned.append([swap_tensor(part, step, levels) for part in parts])
     own = backward(device, None, slopes, held, f32, 1)[0]
 
     pieces = gather_chips(piece, steps)

time: 92.7 us -> 85.3 us (0.920)
  waiting for transfers between devices: 39.7 us -> 28.5 us
  starting transfers between devices: 28.1 us -> 32.2 us
    ppermute x27 -> x26, waiting for transfers between devices: 39.7 us -> 28.5 us  [swap(): return lax.ppermute(block, axes, route)]
    ppermute x27 -> x26, starting transfers between devices: 28.1 us -> 32.2 us  [swap(): return lax.ppermute(block, axes, route)]
    unnamed x14 -> x12, local copies, waits for them, and re-layouts: 3.42 us -> 3.04 us
    pallas_call x15 -> x16, Pallas kernels: 19.9 us -> 20.1 us  [call(): pl.pallas_call(kernel, out_shape=outs, in_specs=in_specs or [VMEM] * len(...]
  transfers between devices with their start and end apart: 27 -> 26, of which waited for: 10 -> 11; matrix products, arithmetic and copies ran while one was open for 0% -> 0% of each run, Pallas kernels for 15% -> 18%
where the time goes in v3:
time: 85.3 us; the launch traced here: 85.1 us
  starting transfers between devices  32.2 us (38%)
  waiting for transfers between devices  28.5 us (33%)
  Pallas kernels  20.1 us (24%)
  local copies, waits for them, and re-layouts  3.1 us (4%)
  between operations  0.9 us (1%)
    ppermute x26, starting transfers between devices, swap(): return lax.ppermute(block, axes, route)  32.2 us
    ppermute x26, waiting for transfers between devices, swap(): return lax.ppermute(block, axes, route)  28.5 us
    pallas_call x16, Pallas kernels, call(): pl.pallas_call(kernel, out_shape=outs, in_specs=in_specs or [VMEM] * len(...  20.1 us
    unnamed x12, local copies, waits for them, and re-layouts  3.04 us
  transfers between devices with their start and end apart: 26, of which 11 were waited for; matrix products, arithmetic and copies ran while one was open for 0% of the time, Pallas kernels for 18%

profile of v3, /device:TPU:0, one launch (start us, length us, event | category | flops | bytes accessed | tf_op | source)
XLA Modules:
  0.0 85.1 jit_solution(14860186010229868923)
XLA Ops:
  0.6 3.1 %collective-permute-start = (bf16[256,768]{1,0:T(8,128)(2,1)}, bf16[256,768]{1,0:T(8,128)(2,1)S(1)}, u32[]{:S(2)}, u32[]{:S(2)}) collective-permute-start(bf16[256,768]{1,0:T(8,128)(2,1)} %refs_0_.1), channel_id=1, source_target_pairs={{0,1},{1,0},{2,3},{3,2},{4,6},{5,7},{6,4},{7,5},{8,9},{9,8},{10,11... | collective-permute-start | bytes 1179656 | tf_op jit(solution)/shard_map/ppermute | solution.py:24
  3.7 2.6 %collective-permute-start.1 = (bf16[256,768]{1,0:T(8,128)(2,1)}, bf16[256,768]{1,0:T(8,128)(2,1)S(1)}, u32[]{:S(2)}, u32[]{:S(2)}) collective-permute-start(bf16[256,768]{1,0:T(8,128)(2,1)} %refs_0_.1), channel_id=1, source_target_pairs={{0,2},{1,3},{2,0},{3,1},{4,5},{5,4},{6,7},{7,6},{8,10},{9,11},{10,... | collective-permute-start | bytes 1179656 | tf_op jit(solution)/shard_map/ppermute | solution.py:24
  6.3 1.0 %copy-done = bf16[256,768]{1,0:T(8,128)(2,1)S(1)} copy-done((bf16[256,768]{1,0:T(8,128)(2,1)S(1)}, bf16[256,768]{1,0:T(8,128)(2,1)}, u32[]{:S(2)}) %copy-start) | copy-done | bytes 393240
  7.4 1.0 %copy-done.2 = bf16[768,256]{1,0:T(8,128)(2,1)S(1)} copy-done((bf16[768,256]{1,0:T(8,128)(2,1)S(1)}, bf16[768,256]{1,0:T(8,128)(2,1)}, u32[]{:S(2)}) %copy-start.2) | copy-done | bytes 393240
  8.4 0.3 shard_map.87
  8.6 0.5 collective-permute-start.2
  9.2 1.0 %copy-done.1 = bf16[256,768]{1,0:T(8,128)(2,1)S(1)} copy-done((bf16[256,768]{1,0:T(8,128)(2,1)S(1)}, bf16[256,768]{1,0:T(8,128)(2,1)}, u32[]{:S(2)}) %copy-start.1) | copy-done | bytes 393240
  10.1 5.2 %shard_map.84 = (f32[256,3072]{1,0:T(8,128)S(1)}, bf16[3,768,3072]{2,1,0:T(8,128)(2,1)S(1)}) custom-call(s32[1]{0:T(128)} %bitcast.device_ref, bf16[256,768]{1,0:T(8,128)(2,1)S(1)} %copy-done.1, bf16[3,768,3072]{2,1,0:T(8,128)(2,1)} %b_ref.1), custom_call_target="tpu_custom_call" | custom-call | flops 1207959552 | bytes 3981312 | tf_op jit(solution)/shard_map/pallas_call | solution.py:51
  15.4 9.5 %collective-permute-done.2.got_ref = bf16[256,256]{1,0:T(8,128)(2,1)S(1)} collective-permute-done((bf16[256,256]{1,0:T(8,128)(2,1)S(1)}, bf16[256,256]{1,0:T(8,128)(2,1)S(1)}, u32[]{:S(2)}, u32[]{:S(2)}) %collective-permute-start.2) | collective-permute-done | bytes 131104 | tf_op jit(solution)/shard_map/ppermute | solution.py:24
  24.9 2.2 %collective-permute-start.3 = (bf16[256,256]{1,0:T(8,128)(2,1)S(1)}, bf16[256,256]{1,0:T(8,128)(2,1)S(1)}, u32[]{:S(2)}, u32[]{:S(2)}) collective-permute-start(bf16[256,256]{1,0:T(8,128)(2,1)S(1)} %get-tuple-element.29), channel_id=1, source_target_pairs={{0,2},{1,3},{2,0},{3,1},{4,5},{5,4},{6,7},{7,6},{8,10},{9,11},{10,... | collective-permute-start | bytes 393224 | tf_op jit(solution)/shard_map/ppermute | solution.py:24
  27.1 1.4 %shard_map.85.running_ref = f32[256,3072]{1,0:T(8,128)S(1)} custom-call(s32[1]{0:T(128)} %bitcast.device_ref, bf16[3,768,3072]{2,1,0:T(8,128)(2,1)S(1)} %get-tuple-element.24.b_ref, f32[256,3072]{1,0:T(8,128)S(1)} %get-tuple-element.25.running_ref, bf16[256,768]{1,0:T(8,128)(2,1)S(1)} %collective-permute-done.refs_0_), custom_call_target="tpu_custom_call" | custom-call | flops 1207959552 | bytes 2605056 | tf_op jit(solution)/shard_map/pallas_call | solution.py:51
  28.6 1.4 %shard_map.86.pre_ref = f32[256,3072]{1,0:T(8,128)S(1)} custom-call(s32[1]{0:T(128)} %bitcast.device_ref, bf16[3,768,3072]{2,1,0:T(8,128)(2,1)S(1)} %get-tuple-element.24.b_ref, f32[256,3072]{1,0:T(8,128)S(1)} %shard_map.85.running_ref, bf16[256,768]{1,0:T(8,128)(2,1)S(1)} %collective-permute-done.1.refs_0_), custom_call_target="tpu_custom_call" | custom-call | flops 1207959552 | bytes 2605056 | tf_op jit(solution)/shard_map/pallas_call | solution.py:51
  30.1 0.8 collective-permute-done.3.got_ref
  30.9 3.8 %shard_map.89 = (bf16[256,3072]{1,0:T(8,128)(2,1)}, bf16[256,3072]{1,0:T(8,128)(2,1)S(1)}, f32[256,256]{1,0:T(8,128)S(1)}, bf16[256,256]{1,0:T(8,128)(2,1)S(1)},...) custom-call(s32[1]{0:T(128)} %bitcast.device_ref, f32[256,3072]{1,0:T(8,128)S(1)} %shard_map.86.pre_ref, ...), custom_call_target="tpu_custom_call" | custom-call | flops 1207959552 | bytes 1572864 | tf_op jit(solution)/shard_map/pallas_call | solution.py:51
  34.7 2.3 %collective-permute-done.16 = bf16[128,3072]{1,0:T(8,128)(2,1)S(1)} collective-permute-done((bf16[128,3072]{1,0:T(8,128)(2,1)S(1)}, bf16[128,3072]{1,0:T(8,128)(2,1)S(1)}, u32[]{:S(2)}, u32[]{:S(2)}) %collective-permute-start.16) | collective-permute-done | bytes 786464 | tf_op jit(solution)/shard_map/ppermute | solution.py:24
  37.0 0.2 convert_add_fusion
  37.2 1.9 %collective-permute-start.17 = (bf16[64,3072]{1,0:T(8,128)(2,1)S(1)}, bf16[64,3072]{1,0:T(8,128)(2,1)S(1)}, u32[]{:S(2)}, u32[]{:S(2)}) collective-permute-start(bf16[64,3072]{1,0:T(8,128)(2,1)S(1)} %slice.30), channel_id=1, source_target_pairs={{0,8},{4,20},{8,0},{12,28},{16,24},{20,4},{24,16},{28,12},{1,9},{5... | collective-permute-start | bytes 1179656 | tf_op jit(solution)/shard_map/ppermute | solution.py:24
  39.1 1.9 %collective-permute-start.4 = (bf16[256,256]{1,0:T(8,128)(2,1)S(1)}, bf16[256,256]{1,0:T(8,128)(2,1)S(1)}, u32[]{:S(2)}, u32[]{:S(2)}) collective-permute-start(bf16[256,256]{1,0:T(8,128)(2,1)S(1)} %get-tuple-element.33), channel_id=1, source_target_pairs={{0,1},{1,0},{2,3},{3,2},{4,6},{5,7},{6,4},{7,5},{8,9},{9,8},{10,11... | collective-permute-start | bytes 393224 | tf_op jit(solution)/shard_map/ppermute | solution.py:24
  41.0 1.5 %collective-permute-start.9 = (bf16[256,768]{1,0:T(8,128)(2,1)S(1)}, bf16[256,768]{1,0:T(8,128)(2,1)S(1)}, u32[]{:S(2)}, u32[]{:S(2)}) collective-permute-start(bf16[256,768]{1,0:T(8,128)(2,1)S(1)} %copy-done.1), channel_id=1, source_target_pairs={{0,16},{4,12},{8,24},{12,4},{16,0},{20,28},{24,8},{28,20},{1,17},{... | collective-permute-start | bytes 1179656 | tf_op jit(solution)/shard_map/ppermute | solution.py:24
  42.6 0.5 collective-permute-start.10
  43.1 2.2 %collective-permute-done.4.got_ref = bf16[256,256]{1,0:T(8,128)(2,1)S(1)} collective-permute-done((bf16[256,256]{1,0:T(8,128)(2,1)S(1)}, bf16[256,256]{1,0:T(8,128)(2,1)S(1)}, u32[]{:S(2)}, u32[]{:S(2)}) %collective-permute-start.4) | collective-permute-done | bytes 131104 | tf_op jit(solution)/shard_map/ppermute | solution.py:24
  45.3 2.0 %collective-permute-start.5 = (bf16[256,256]{1,0:T(8,128)(2,1)S(1)}, bf16[256,256]{1,0:T(8,128)(2,1)S(1)}, u32[]{:S(2)}, u32[]{:S(2)}) collective-permute-start(bf16[256,256]{1,0:T(8,128)(2,1)S(1)} %get-tuple-element.35), channel_id=1, source_target_pairs={{0,2},{1,3},{2,0},{3,1},{4,5},{5,4},{6,7},{7,6},{8,10},{9,11},{10,... | collective-permute-start | bytes 393224 | tf_op jit(solution)/shard_map/ppermute | solution.py:24
  47.3 0.1 slice_add_fusion
  47.5 2.9 %collective-permute-start.18 = (bf16[32,3072]{1,0:T(8,128)(2,1)S(1)}, bf16[32,3072]{1,0:T(8,128)(2,1)S(1)}, u32[]{:S(2)}, u32[]{:S(2)}) collective-permute-start(bf16[32,3072]{1,0:T(8,128)(2,1)S(1)} %slice.31), channel_id=1, source_target_pairs={{0,16},{4,12},{8,24},{12,4},{16,0},{20,28},{24,8},{28,20},{1,17},{... | collective-permute-start | bytes 589832 | tf_op jit(solution)/shard_map/ppermute | solution.py:24
  50.3 1.4 %shard_map.94 = bf16[256,768]{1,0:T(8,128)(2,1)S(1)} custom-call(s32[1]{0:T(128)} %bitcast.device_ref, bf16[256,3072]{1,0:T(8,128)(2,1)S(1)} %get-tuple-element.31.s_ref, bf16[3,768,3072]{2,1,0:T(8,128)(2,1)S(1)} %get-tuple-element.24.b_ref), custom_call_target="tpu_custom_call" | custom-call | flops 1207959552 | bytes 2015232 | tf_op jit(solution)/shard_map/pallas_call | solution.py:51
  51.7 2.9 %collective-permute-start.8 = (bf16[256,768]{1,0:T(8,128)(2,1)S(1)}, bf16[256,768]{1,0:T(8,128)(2,1)S(1)}, u32[]{:S(2)}, u32[]{:S(2)}) collective-permute-start(bf16[256,768]{1,0:T(8,128)(2,1)S(1)} %shard_map.94), channel_id=1, source_target_pairs={{0,2},{1,3},{2,0},{3,1},{4,5},{5,4},{6,7},{7,6},{8,10},{9,11},{10,... | collective-permute-start | bytes 1179656 | tf_op jit(solution)/shard_map/ppermute | solution.py:24
  54.7 1.4 %shard_map.93 = (bf16[128,768]{1,0:T(8,128)(2,1)S(1)}, bf16[128,768]{1,0:T(8,128)(2,1)S(1)}) custom-call(s32[1]{0:T(128)} %bitcast.device_ref, bf16[256,3072]{1,0:T(8,128)(2,1)S(1)} %get-tuple-element.31.s_ref, bf16[3,768,3072]{2,1,0:T(8,128)(2,1)S(1)} %get-tuple-element.24.b_ref), custom_call_target="tpu_custom_call" | custom-call | flops 1207959552 | bytes 2015232 | tf_op jit(solution)/shard_map/pallas_call | solution.py:51
  56.1 2.2 %collective-permute-start.6 = (bf16[128,768]{1,0:T(8,128)(2,1)S(1)}, bf16[128,768]{1,0:T(8,128)(2,1)S(1)}, u32[]{:S(2)}, u32[]{:S(2)}) collective-permute-start(bf16[128,768]{1,0:T(8,128)(2,1)S(1)} %get-tuple-element.36), channel_id=1, source_target_pairs={{0,1},{1,0},{2,3},{3,2},{4,6},{5,7},{6,4},{7,5},{8,9},{9,8},{10,11... | collective-permute-start | bytes 589832 | tf_op jit(solution)/shard_map/ppermute | solution.py:24
  58.3 1.5 %collective-permute-start.11 = (bf16[256,768]{1,0:T(8,128)(2,1)S(1)}, bf16[256,768]{1,0:T(8,128)(2,1)S(1)}, u32[]{:S(2)}, u32[]{:S(2)}) collective-permute-start(bf16[256,768]{1,0:T(8,128)(2,1)S(1)} %collective-permute-done.9.refs_1_), channel_id=1, source_target_pairs={{0,8},{4,20},{8,0},{12,28},{16,24},{20,4},{24,16},{28,12},{1,9},{5... | collective-permute-start | bytes 1179656 | tf_op jit(solution)/shard_map/ppermute | solution.py:24
  60.0 2.1 %collective-permute-start.19 = (bf16[32,3072]{1,0:T(8,128)(2,1)S(1)}, bf16[32,3072]{1,0:T(8,128)(2,1)S(1)}, u32[]{:S(2)}, u32[]{:S(2)}) collective-permute-start(bf16[32,3072]{1,0:T(8,128)(2,1)S(1)} %fusion.1.refs_0_), channel_id=1, source_target_pairs={{0,16},{4,12},{8,24},{12,4},{16,0},{20,28},{24,8},{28,20},{1,17},{... | collective-permute-start | bytes 589832 | tf_op jit(solution)/shard_map/ppermute | solution.py:24
  62.0 4.2 %collective-permute-done.12.refs_1_ = bf16[256,256]{1,0:T(8,128)(2,1)S(1)} collective-permute-done((bf16[256,256]{1,0:T(8,128)(2,1)S(1)}, bf16[256,256]{1,0:T(8,128)(2,1)S(1)}, u32[]{:S(2)}, u32[]{:S(2)}) %collective-permute-start.12) | collective-permute-done | bytes 131104 | tf_op jit(solution)/shard_map/ppermute | solution.py:24
  66.2 0.4 collective-permute-start.13
  66.6 0.4 collective-permute-done.11.refs_0_
  67.0 1.2 %collective-permute-start.14 = (bf16[256,256]{1,0:T(8,128)(2,1)S(1)}, bf16[256,256]{1,0:T(8,128)(2,1)S(1)}, u32[]{:S(2)}, u32[]{:S(2)}) collective-permute-start(bf16[256,256]{1,0:T(8,128)(2,1)S(1)} %collective-permute-done.12.refs_1_), channel_id=1, source_target_pairs={{0,8},{4,20},{8,0},{12,28},{16,24},{20,4},{24,16},{28,12},{1,9},{5... | collective-permute-start | bytes 393224 | tf_op jit(solution)/shard_map/ppermute | solution.py:24
  68.3 0.4 shard_map.96.early_ref
  68.6 0.2 shard_map.97.late_ref
  68.8 2.4 %collective-permute-done.13.refs_2_ = bf16[256,256]{1,0:T(8,128)(2,1)S(1)} collective-permute-done((bf16[256,256]{1,0:T(8,128)(2,1)S(1)}, bf16[256,256]{1,0:T(8,128)(2,1)S(1)}, u32[]{:S(2)}, u32[]{:S(2)}) %collective-permute-start.13) | collective-permute-done | bytes 131104 | tf_op jit(solution)/shard_map/ppermute | solution.py:24
  71.2 1.4 %collective-permute-done.14.refs_3_ = bf16[256,256]{1,0:T(8,128)(2,1)S(1)} collective-permute-done((bf16[256,256]{1,0:T(8,128)(2,1)S(1)}, bf16[256,256]{1,0:T(8,128)(2,1)S(1)}, u32[]{:S(2)}, u32[]{:S(2)}) %collective-permute-start.14) | collective-permute-done | bytes 131104 | tf_op jit(solution)/shard_map/ppermute | solution.py:24
  72.6 0.6 shard_map.98
  73.3 0.7 collective-permute-start.20
  74.0 1.4 %collective-permute-start.21 = (bf16[32,3072]{1,0:T(8,128)(2,1)S(1)}, bf16[32,3072]{1,0:T(8,128)(2,1)S(1)}, u32[]{:S(2)}, u32[]{:S(2)}) collective-permute-start(bf16[32,3072]{1,0:T(8,128)(2,1)S(1)} %collective-permute-done.19.refs_1_), channel_id=1, source_target_pairs={{0,8},{4,20},{8,0},{12,28},{16,24},{20,4},{24,16},{28,12},{1,9},{5... | collective-permute-start | bytes 589832 | tf_op jit(solution)/shard_map/ppermute | solution.py:24
  75.4 1.5 %collective-permute-done.7.refs_1_ = bf16[128,768]{1,0:T(8,128)(2,1)S(1)} collective-permute-done((bf16[128,768]{1,0:T(8,128)(2,1)S(1)}, bf16[128,768]{1,0:T(8,128)(2,1)S(1)}, u32[]{:S(2)}, u32[]{:S(2)}) %collective-permute-start.7) | collective-permute-done | bytes 196640 | tf_op jit(solution)/shard_map/ppermute | solution.py:24
  76.9 0.5 collective-permute-start.23
  77.4 1.6 %collective-permute-done.20.refs_2_ = bf16[32,3072]{1,0:T(8,128)(2,1)S(1)} collective-permute-done((bf16[32,3072]{1,0:T(8,128)(2,1)S(1)}, bf16[32,3072]{1,0:T(8,128)(2,1)S(1)}, u32[]{:S(2)}, u32[]{:S(2)}) %collective-permute-start.20) | collective-permute-done | bytes 196640 | tf_op jit(solution)/shard_map/ppermute | solution.py:24
  79.0 2.1 %collective-permute-done.21.refs_3_ = bf16[32,3072]{1,0:T(8,128)(2,1)S(1)} collective-permute-done((bf16[32,3072]{1,0:T(8,128)(2,1)S(1)}, bf16[32,3072]{1,0:T(8,128)(2,1)S(1)}, u32[]{:S(2)}, u32[]{:S(2)}) %collective-permute-start.21) | collective-permute-done | bytes 196640 | tf_op jit(solution)/shard_map/ppermute | solution.py:24
  81.1 1.4 %shard_map.90.own_ref = f32[256,768]{1,0:T(8,128)S(1)} custom-call(s32[1]{0:T(128)} %bitcast.device_ref, bf16[256,3072]{1,0:T(8,128)(2,1)S(1)} %get-tuple-element.31.s_ref, bf16[3,768,3072]{2,1,0:T(8,128)(2,1)S(1)} %get-tuple-element.24.b_ref), custom_call_target="tpu_custom_call" | custom-call | flops 1207959552 | bytes 2064384 | tf_op jit(solution)/shard_map/pallas_call | solution.py:51
  82.6 1.1 %shard_map.95 = bf16[256,768]{1,0:T(8,128)(2,1)} custom-call(f32[256,768]{1,0:T(8,128)S(1)} %shard_map.90.own_ref, bf16[256,256]{1,0:T(8,128)(2,1)S(1)} %shard_map.92.mixed_ref.refs_0_, bf16[768,256]{1,0:T(8,128)(2,1)S(1)} %copy-done.3, bf16[128,768]{1,0:T(8,128)(2,1)S(1)} %collective-permute-done.6.refs_0_, ...), custom_call_target="tpu_custom_call" | custom-call | flops 100663296 | bytes 311296 | tf_op jit(solution)/shard_map/pallas_call | solution.py:51
  83.7 1.4 %shard_map.99 = (bf16[256,3072]{1,0:T(8,128)(2,1)}, bf16[768,256]{1,0:T(8,128)(2,1)}) custom-call(s32[1]{0:T(128)} %bitcast.device_ref, f32[768,256]{1,0:T(8,128)S(1)} %get-tuple-element.38.total_ref, bf16[768,256]{1,0:T(8,128)(2,1)S(1)} %collective-permute-done.15.got_ref, bf16[32,3072]{1,0:T(8,128)(2,1)S(1)} %fusion.1.refs_0_, ...), custom_call_target="tpu_custom_call" | custom-call | bytes 589824 | tf_op jit(solution)/shard_map/pallas_call | solution.py:51
  (37 shorter events, 0.5 us)
Async XLA Ops:
  0.6 26.5 %collective-permute-start = (bf16[256,768]{1,0:T(8,128)(2,1)}, bf16[256,768]{1,0:T(8,128)(2,1)S(1)}, u32[]{:S(2)}, u32[]{:S(2)}) collective-permute-start(bf16[256,768]{1,0:T(8,128)(2,1)} %refs_0_.1), channel_id=1, source_target_pairs={{0,1},{1,0},{2,3},{3,2},{4,6},{5,7},{6,4},{7,5},{8,9},{9,8},{10,11... | collective-permute-start | bytes 1179656 | tf_op jit(solution)/shard_map/ppermute | solution.py:24
  3.7 24.9 %collective-permute-start.1 = (bf16[256,768]{1,0:T(8,128)(2,1)}, bf16[256,768]{1,0:T(8,128)(2,1)S(1)}, u32[]{:S(2)}, u32[]{:S(2)}) collective-permute-start(bf16[256,768]{1,0:T(8,128)(2,1)} %refs_0_.1), channel_id=1, source_target_pairs={{0,2},{1,3},{2,0},{3,1},{4,5},{5,4},{6,7},{7,6},{8,10},{9,11},{10,... | collective-permute-start | bytes 1179656 | tf_op jit(solution)/shard_map/ppermute | solution.py:24
  6.3 1.0 %copy-start = (bf16[256,768]{1,0:T(8,128)(2,1)S(1)}, bf16[256,768]{1,0:T(8,128)(2,1)}, u32[]{:S(2)}) copy-start(bf16[256,768]{1,0:T(8,128)(2,1)} %refs_0_.1) | copy-start | bytes 1179652
  7.4 1.0 %copy-start.2 = (bf16[768,256]{1,0:T(8,128)(2,1)S(1)}, bf16[768,256]{1,0:T(8,128)(2,1)}, u32[]{:S(2)}) copy-start(bf16[768,256]{1,0:T(8,128)(2,1)} %left_ref.3) | copy-start | bytes 1179652
  8.6 16.2 %collective-permute-start.2 = (bf16[256,256]{1,0:T(8,128)(2,1)S(1)}, bf16[256,256]{1,0:T(8,128)(2,1)S(1)}, u32[]{:S(2)}, u32[]{:S(2)}) collective-permute-start(bf16[256,256]{1,0:T(8,128)(2,1)S(1)} %get-tuple-element.27), channel_id=1, source_target_pairs={{0,1},{1,0},{2,3},{3,2},{4,6},{5,7},{6,4},{7,5},{8,9},{9,8},{10,11... | collective-permute-start | bytes 393224 | tf_op jit(solution)/shard_map/ppermute | solution.py:24
  9.2 1.0 %copy-start.1 = (bf16[256,768]{1,0:T(8,128)(2,1)S(1)}, bf16[256,768]{1,0:T(8,128)(2,1)}, u32[]{:S(2)}) copy-start(bf16[256,768]{1,0:T(8,128)(2,1)} %refs_0_.1) | copy-start | bytes 1179652
  24.9 6.0 %collective-permute-start.3 = (bf16[256,256]{1,0:T(8,128)(2,1)S(1)}, bf16[256,256]{1,0:T(8,128)(2,1)S(1)}, u32[]{:S(2)}, u32[]{:S(2)}) collective-permute-start(bf16[256,256]{1,0:T(8,128)(2,1)S(1)} %get-tuple-element.29), channel_id=1, source_target_pairs={{0,2},{1,3},{2,0},{3,1},{4,5},{5,4},{6,7},{7,6},{8,10},{9,11},{10,... | collective-permute-start | bytes 393224 | tf_op jit(solution)/shard_map/ppermute | solution.py:24
  28.6 2.3 %copy-start.4 = (bf16[256,3072]{1,0:T(8,128)(2,1)S(1)}, bf16[256,3072]{1,0:T(8,128)(2,1)}, u32[]{:S(2)}) copy-start(bf16[256,3072]{1,0:T(8,128)(2,1)} %right_ref.1) | copy-start | bytes 4718596
  28.6 2.3 %copy-start.5 = (bf16[256,3072]{1,0:T(8,128)(2,1)S(1)}, bf16[256,3072]{1,0:T(8,128)(2,1)}, u32[]{:S(2)}) copy-start(bf16[256,3072]{1,0:T(8,128)(2,1)} %up_ref.1) | copy-start | bytes 4718596
  34.7 2.3 %collective-permute-start.16 = (bf16[128,3072]{1,0:T(8,128)(2,1)S(1)}, bf16[128,3072]{1,0:T(8,128)(2,1)S(1)}, u32[]{:S(2)}, u32[]{:S(2)}) collective-permute-start(bf16[128,3072]{1,0:T(8,128)(2,1)S(1)} %get-tuple-element.41), channel_id=1, source_target_pairs={{0,4},{4,0},{8,12},{12,8},{16,20},{20,16},{24,28},{28,24},{1,5},{5... | collective-permute-start | bytes 2359304 | tf_op jit(solution)/shard_map/ppermute | solution.py:24
  37.2 10.1 %collective-permute-start.17 = (bf16[64,3072]{1,0:T(8,128)(2,1)S(1)}, bf16[64,3072]{1,0:T(8,128)(2,1)S(1)}, u32[]{:S(2)}, u32[]{:S(2)}) collective-permute-start(bf16[64,3072]{1,0:T(8,128)(2,1)S(1)} %slice.30), channel_id=1, source_target_pairs={{0,8},{4,20},{8,0},{12,28},{16,24},{20,4},{24,16},{28,12},{1,9},{5... | collective-permute-start | bytes 1179656 | tf_op jit(solution)/shard_map/ppermute | solution.py:24
  39.1 6.2 %collective-permute-start.4 = (bf16[256,256]{1,0:T(8,128)(2,1)S(1)}, bf16[256,256]{1,0:T(8,128)(2,1)S(1)}, u32[]{:S(2)}, u32[]{:S(2)}) collective-permute-start(bf16[256,256]{1,0:T(8,128)(2,1)S(1)} %get-tuple-element.33), channel_id=1, source_target_pairs={{0,1},{1,0},{2,3},{3,2},{4,6},{5,7},{6,4},{7,5},{8,9},{9,8},{10,11... | collective-permute-start | bytes 393224 | tf_op jit(solution)/shard_map/ppermute | solution.py:24
  41.0 15.0 %collective-permute-start.9 = (bf16[256,768]{1,0:T(8,128)(2,1)S(1)}, bf16[256,768]{1,0:T(8,128)(2,1)S(1)}, u32[]{:S(2)}, u32[]{:S(2)}) collective-permute-start(bf16[256,768]{1,0:T(8,128)(2,1)S(1)} %copy-done.1), channel_id=1, source_target_pairs={{0,16},{4,12},{8,24},{12,4},{16,0},{20,28},{24,8},{28,20},{1,17},{... | collective-permute-start | bytes 1179656 | tf_op jit(solution)/shard_map/ppermute | solution.py:24
  42.6 17.4 %collective-permute-start.10 = (bf16[256,768]{1,0:T(8,128)(2,1)S(1)}, bf16[256,768]{1,0:T(8,128)(2,1)S(1)}, u32[]{:S(2)}, u32[]{:S(2)}) collective-permute-start(bf16[256,768]{1,0:T(8,128)(2,1)S(1)} %copy-done.1), channel_id=1, source_target_pairs={{0,8},{4,20},{8,0},{12,28},{16,24},{20,4},{24,16},{28,12},{1,9},{5... | collective-permute-start | bytes 1179656 | tf_op jit(solution)/shard_map/ppermute | solution.py:24
  45.3 12.9 %collective-permute-start.5 = (bf16[256,256]{1,0:T(8,128)(2,1)S(1)}, bf16[256,256]{1,0:T(8,128)(2,1)S(1)}, u32[]{:S(2)}, u32[]{:S(2)}) collective-permute-start(bf16[256,256]{1,0:T(8,128)(2,1)S(1)} %get-tuple-element.35), channel_id=1, source_target_pairs={{0,2},{1,3},{2,0},{3,1},{4,5},{5,4},{6,7},{7,6},{8,10},{9,11},{10,... | collective-permute-start | bytes 393224 | tf_op jit(solution)/shard_map/ppermute | solution.py:24
  47.5 12.3 %collective-permute-start.18 = (bf16[32,3072]{1,0:T(8,128)(2,1)S(1)}, bf16[32,3072]{1,0:T(8,128)(2,1)S(1)}, u32[]{:S(2)}, u32[]{:S(2)}) collective-permute-start(bf16[32,3072]{1,0:T(8,128)(2,1)S(1)} %slice.31), channel_id=1, source_target_pairs={{0,16},{4,12},{8,24},{12,4},{16,0},{20,28},{24,8},{28,20},{1,17},{... | collective-permute-start | bytes 589832 | tf_op jit(solution)/shard_map/ppermute | solution.py:24
  51.7 25.1 %collective-permute-start.8 = (bf16[256,768]{1,0:T(8,128)(2,1)S(1)}, bf16[256,768]{1,0:T(8,128)(2,1)S(1)}, u32[]{:S(2)}, u32[]{:S(2)}) collective-permute-start(bf16[256,768]{1,0:T(8,128)(2,1)S(1)} %shard_map.94), channel_id=1, source_target_pairs={{0,2},{1,3},{2,0},{3,1},{4,5},{5,4},{6,7},{7,6},{8,10},{9,11},{10,... | collective-permute-start | bytes 1179656 | tf_op jit(solution)/shard_map/ppermute | solution.py:24
  56.1 17.2 %collective-permute-start.6 = (bf16[128,768]{1,0:T(8,128)(2,1)S(1)}, bf16[128,768]{1,0:T(8,128)(2,1)S(1)}, u32[]{:S(2)}, u32[]{:S(2)}) collective-permute-start(bf16[128,768]{1,0:T(8,128)(2,1)S(1)} %get-tuple-element.36), channel_id=1, source_target_pairs={{0,1},{1,0},{2,3},{3,2},{4,6},{5,7},{6,4},{7,5},{8,9},{9,8},{10,11... | collective-permute-start | bytes 589832 | tf_op jit(solution)/shard_map/ppermute | solution.py:24
  58.3 8.8 %collective-permute-start.11 = (bf16[256,768]{1,0:T(8,128)(2,1)S(1)}, bf16[256,768]{1,0:T(8,128)(2,1)S(1)}, u32[]{:S(2)}, u32[]{:S(2)}) collective-permute-start(bf16[256,768]{1,0:T(8,128)(2,1)S(1)} %collective-permute-done.9.refs_1_), channel_id=1, source_target_pairs={{0,8},{4,20},{8,0},{12,28},{16,24},{20,4},{24,16},{28,12},{1,9},{5... | collective-permute-start | bytes 1179656 | tf_op jit(solution)/shard_map/ppermute | solution.py:24
  59.8 6.4 %collective-permute-start.12 = (bf16[256,256]{1,0:T(8,128)(2,1)S(1)}, bf16[256,256]{1,0:T(8,128)(2,1)S(1)}, u32[]{:S(2)}, u32[]{:S(2)}) collective-permute-start(bf16[256,256]{1,0:T(8,128)(2,1)S(1)} %shard_map.92.mixed_ref.refs_0_), channel_id=1, source_target_pairs={{0,16},{4,12},{8,24},{12,4},{16,0},{20,28},{24,8},{28,20},{1,17},{... | collective-permute-start | bytes 393224 | tf_op jit(solution)/shard_map/ppermute | solution.py:24
  60.0 14.0 %collective-permute-start.19 = (bf16[32,3072]{1,0:T(8,128)(2,1)S(1)}, bf16[32,3072]{1,0:T(8,128)(2,1)S(1)}, u32[]{:S(2)}, u32[]{:S(2)}) collective-permute-start(bf16[32,3072]{1,0:T(8,128)(2,1)S(1)} %fusion.1.refs_0_), channel_id=1, source_target_pairs={{0,16},{4,12},{8,24},{12,4},{16,0},{20,28},{24,8},{28,20},{1,17},{... | collective-permute-start | bytes 589832 | tf_op jit(solution)/shard_map/ppermute | solution.py:24
  66.2 5.0 %collective-permute-start.13 = (bf16[256,256]{1,0:T(8,128)(2,1)S(1)}, bf16[256,256]{1,0:T(8,128)(2,1)S(1)}, u32[]{:S(2)}, u32[]{:S(2)}) collective-permute-start(bf16[256,256]{1,0:T(8,128)(2,1)S(1)} %shard_map.92.mixed_ref.refs_0_), channel_id=1, source_target_pairs={{0,8},{4,20},{8,0},{12,28},{16,24},{20,4},{24,16},{28,12},{1,9},{5... | collective-permute-start | bytes 393224 | tf_op jit(solution)/shard_map/ppermute | solution.py:24
  67.0 5.6 %collective-permute-start.14 = (bf16[256,256]{1,0:T(8,128)(2,1)S(1)}, bf16[256,256]{1,0:T(8,128)(2,1)S(1)}, u32[]{:S(2)}, u32[]{:S(2)}) collective-permute-start(bf16[256,256]{1,0:T(8,128)(2,1)S(1)} %collective-permute-done.12.refs_1_), channel_id=1, source_target_pairs={{0,8},{4,20},{8,0},{12,28},{16,24},{20,4},{24,16},{28,12},{1,9},{5... | collective-permute-start | bytes 393224 | tf_op jit(solution)/shard_map/ppermute | solution.py:24
  71.2 5.7 %collective-permute-start.7 = (bf16[128,768]{1,0:T(8,128)(2,1)S(1)}, bf16[128,768]{1,0:T(8,128)(2,1)S(1)}, u32[]{:S(2)}, u32[]{:S(2)}) collective-permute-start(bf16[128,768]{1,0:T(8,128)(2,1)S(1)} %get-tuple-element.37), channel_id=1, source_target_pairs={{0,1},{1,0},{2,3},{3,2},{4,6},{5,7},{6,4},{7,5},{8,9},{9,8},{10,11... | collective-permute-start | bytes 589832 | tf_op jit(solution)/shard_map/ppermute | solution.py:24
  73.2 9.4 %copy-start.3 = (bf16[768,256]{1,0:T(8,128)(2,1)S(1)}, bf16[768,256]{1,0:T(8,128)(2,1)}, u32[]{:S(2)}) copy-start(bf16[768,256]{1,0:T(8,128)(2,1)} %left_ref.3) | copy-start | bytes 1179652
  73.2 10.5 %collective-permute-start.15 = (bf16[768,256]{1,0:T(8,128)(2,1)S(1)}, bf16[768,256]{1,0:T(8,128)(2,1)S(1)}, u32[]{:S(2)}, u32[]{:S(2)}) collective-permute-start(bf16[768,256]{1,0:T(8,128)(2,1)S(1)} %get-tuple-element.39), channel_id=1, source_target_pairs={{0,4},{4,0},{8,12},{12,8},{16,20},{20,16},{24,28},{28,24},{1,5},{5... | collective-permute-start | bytes 1179656 | tf_op jit(solution)/shard_map/ppermute | solution.py:24
  73.3 5.7 %collective-permute-start.20 = (bf16[32,3072]{1,0:T(8,128)(2,1)S(1)}, bf16[32,3072]{1,0:T(8,128)(2,1)S(1)}, u32[]{:S(2)}, u32[]{:S(2)}) collective-permute-start(bf16[32,3072]{1,0:T(8,128)(2,1)S(1)} %fusion.1.refs_0_), channel_id=1, source_target_pairs={{0,8},{4,20},{8,0},{12,28},{16,24},{20,4},{24,16},{28,12},{1,9},{5... | collective-permute-start | bytes 589832 | tf_op jit(solution)/shard_map/ppermute | solution.py:24
  74.0 7.1 %collective-permute-start.21 = (bf16[32,3072]{1,0:T(8,128)(2,1)S(1)}, bf16[32,3072]{1,0:T(8,128)(2,1)S(1)}, u32[]{:S(2)}, u32[]{:S(2)}) collective-permute-start(bf16[32,3072]{1,0:T(8,128)(2,1)S(1)} %collective-permute-done.19.refs_1_), channel_id=1, source_target_pairs={{0,8},{4,20},{8,0},{12,28},{16,24},{20,4},{24,16},{28,12},{1,9},{5... | collective-permute-start | bytes 589832 | tf_op jit(solution)/shard_map/ppermute | solution.py:24
  76.9 6.8 %collective-permute-start.22 = (bf16[32,3072]{1,0:T(8,128)(2,1)S(1)}, bf16[32,3072]{1,0:T(8,128)(2,1)S(1)}, u32[]{:S(2)}, u32[]{:S(2)}) collective-permute-start(bf16[32,3072]{1,0:T(8,128)(2,1)S(1)} %fusion.1.refs_0_), channel_id=1, source_target_pairs={{0,4},{4,0},{8,12},{12,8},{16,20},{20,16},{24,28},{28,24},{1,5},{5... | collective-permute-start | bytes 589832 | tf_op jit(solution)/shard_map/ppermute | solution.py:24
  76.9 6.8 %collective-permute-start.23 = (bf16[32,3072]{1,0:T(8,128)(2,1)S(1)}, bf16[32,3072]{1,0:T(8,128)(2,1)S(1)}, u32[]{:S(2)}, u32[]{:S(2)}) collective-permute-start(bf16[32,3072]{1,0:T(8,128)(2,1)S(1)} %collective-permute-done.19.refs_1_), channel_id=1, source_target_pairs={{0,4},{4,0},{8,12},{12,8},{16,20},{20,16},{24,28},{28,24},{1,5},{5... | collective-permute-start | bytes 589832 | tf_op jit(solution)/shard_map/ppermute | solution.py:24
  79.0 4.7 %collective-permute-start.24 = (bf16[32,3072]{1,0:T(8,128)(2,1)S(1)}, bf16[32,3072]{1,0:T(8,128)(2,1)S(1)}, u32[]{:S(2)}, u32[]{:S(2)}) collective-permute-start(bf16[32,3072]{1,0:T(8,128)(2,1)S(1)} %collective-permute-done.20.refs_2_), channel_id=1, source_target_pairs={{0,4},{4,0},{8,12},{12,8},{16,20},{20,16},{24,28},{28,24},{1,5},{5... | collective-permute-start | bytes 589832 | tf_op jit(solution)/shard_map/ppermute | solution.py:24
  81.1 2.6 %collective-permute-start.25 = (bf16[32,3072]{1,0:T(8,128)(2,1)S(1)}, bf16[32,3072]{1,0:T(8,128)(2,1)S(1)}, u32[]{:S(2)}, u32[]{:S(2)}) collective-permute-start(bf16[32,3072]{1,0:T(8,128)(2,1)S(1)} %collective-permute-done.21.refs_3_), channel_id=1, source_target_pairs={{0,4},{4,0},{8,12},{12,8},{16,20},{20,16},{24,28},{28,24},{1,5},{5... | collective-permute-start | bytes 589832 | tf_op jit(solution)/shard_map/ppermute | solution.py:24

commit v4 on v3

--- a/solution.py
+++ b/solution.py
@@ -46,7 +46,7 @@
     return [slice(at, min(at + width, extent)) for at in range(0, extent, width)]
 
 
-def call(kernel, outs, args, flops, mib, scratch=(), in_specs=None, out_specs=None):
+def call(kernel, outs, args, flops, mib, scratch=(), in_specs=None, out_specs=None, aliases=None):
     nbytes = sum(a.size * a.dtype.itemsize for a in (*args, *outs))
     return pl.pallas_call(
         kernel,
@@ -54,6 +54,7 @@
         in_specs=in_specs or [VMEM] * len(args),
         out_specs=out_specs or [VMEM] * len(outs),
         scratch_shapes=list(scratch),
+        input_output_aliases=aliases or {},
         compiler_params=pltpu.CompilerParams(vmem_limit_bytes=mib * MIB),
         cost_estimate=pl.CostEstimate(flops=flops, bytes_accessed=nbytes // 8, transcendentals=0),
     )(*args)
@@ -210,7 +211,7 @@
             ].astype(jnp.bfloat16)
     order = order_ref[...]
     mixed = None
-    for at in tiles(up_ref.shape[1], 1024):
+    for at in tiles(up_ref.shape[1], 1536):
         right = right_ref[:, at]
         value = pre_ref[:, at] + dot(low, right, 1, 0)
         act, slope = gelu_and_slope(value, up_ref[:, at].astype(jnp.float32))
@@ -308,22 +309,37 @@
     return call(kernel, [out], args, flops, 4, scratch, None, [HBM])[0]
 
 
-def finish_kernel(chips, device_ref, total_ref, got_ref, *refs):
+def place_copies(device, chips, parts, positions, out_ref, sem):
+    height = out_ref.shape[0] // (2 * chips)
+    copies = []
+    for ref, (side, position) in zip(parts, positions):
+        row = ((device & 1) ^ side) * chips + chip_at(device, side, chips, position)
+        target = out_ref.at[pl.ds(pl.multiple_of(row * height, height), height), :]
+        copies.append(pltpu.make_async_copy(ref, target, sem.at[len(copies)]))
+    for copy in copies:
+        copy.start()
+    return copies
+
+
+def place_kernel(chips, positions, device_ref, *refs):
+    parts, out_ref, sem = refs[:-2], refs[-2], refs[-1]
+    for copy in place_copies(device_ref[0], chips, parts, positions, out_ref, sem):
+        copy.wait()
+
+
+def place(device, chips, parts, positions):
+    height, cols = parts[0].shape
+    out = jax.ShapeDtypeStruct((2 * chips * height, cols), jnp.bfloat16)
+    specs = [SMEM] + [VMEM] * len(parts)
+    scratch = [pltpu.SemaphoreType.DMA((len(parts),))]
+    kernel = functools.partial(place_kernel, chips, positions)
+    return call(kernel, [out], (device, *parts), 0, 2, scratch, specs, [HBM])[0]
+
+
+def finish_kernel(chips, positions, device_ref, placed_ref, total_ref, got_ref, *refs):
     parts = refs[:-4]
     right_ref, left_ref, held_ref, sem = refs[-4:]
-    height = right_ref.shape[0] // (2 * chips)
-    device = device_ref[0]
-    copies = []
-    for side in range(2):
-        other = 0
-        for ref in parts[side * len(parts) // 2 : (side + 1) * len(parts) // 2]:
-            for at in tiles(ref.shape[0], height):
-                row = ((device & 1) ^ side) * chips + chip_at(device, side, chips, other)
-                target = right_ref.at[pl.ds(pl.multiple_of(row * height, height), height), :]
-                copies.append(pltpu.make_async_copy(ref.at[at, :], target, sem.at[len(copies)]))
-                other += 1
-    for copy in copies:
-        copy.start()
+    copies = place_copies(device_ref[0], chips, parts, positions, right_ref, sem)
     held_ref[...] = (total_ref[...] + got_ref[...].astype(jnp.float32)).astype(jnp.bfloat16)
     copies.append(pltpu.make_async_copy(held_ref, left_ref, sem.at[len(copies)]))
     copies[-1].start()
@@ -331,20 +347,19 @@
         copy.wait()
 
 
-def finish(device, chips, left_total, left_got, parts):
-    rows = sum(part.shape[0] for part in parts)
+def finish(device, chips, placed, left_total, left_got, parts, positions):
     outs = [
-        jax.ShapeDtypeStruct((rows, parts[0].shape[1]), jnp.bfloat16),
+        jax.ShapeDtypeStruct(placed.shape, placed.dtype),
         jax.ShapeDtypeStruct(left_total.shape, jnp.bfloat16),
     ]
-    specs = [SMEM] + [VMEM] * (len(parts) + 2)
+    specs = [SMEM, HBM] + [VMEM] * (len(parts) + 2)
     scratch = [
         pltpu.VMEM(left_total.shape, jnp.bfloat16),
-        pltpu.SemaphoreType.DMA((2 * chips + 1,)),
+        pltpu.SemaphoreType.DMA((len(parts) + 1,)),
     ]
-    kernel = functools.partial(finish_kernel, chips)
-    args = (device, left_total, left_got, *parts)
-    return call(kernel, outs, args, 0, 2, scratch, specs, [HBM, HBM])
+    kernel = functools.partial(finish_kernel, chips, positions)
+    args = (device, placed, left_total, left_got, *parts)
+    return call(kernel, outs, args, 0, 2, scratch, specs, [HBM, HBM], {1: 0})
 
 
 def body(tokens, blocks, left_factor, right_factor, upstream):
@@ -394,8 +409,13 @@
     rows_parts = gather_chips(mixed_rows, steps)
     left_total, left_sent = left_partial(early, late, rows_parts, norm_scale)
     left_got = swap_core(left_sent)
-    pieces += [swap_core(part) for part in pieces]
-    right_grad, left_grad = finish(device, chips, left_total, left_got, pieces)
+    pieces = [pieces, [swap_core(part) for part in pieces]]
+    soon = [(side, position) for side in range(2) for position in range(chips - 1)]
+    last = [(side, chips - 1) for side in range(2)]
+    placed = place(device, chips, [pieces[side][position] for side, position in soon], soon)
+    right_grad, left_grad = finish(
+        device, chips, placed, left_total, left_got, [pieces[side][-1] for side, _ in last], last
+    )
     token_grad = token_total(own, mixed_rows, left_factor, returned)
     return activated, token_grad, left_grad, right_grad
 

time: 85.3 us -> 85.9 us (level)
    pallas_call x16 -> x17, Pallas kernels: 20.1 us -> 20.7 us  [call(): pl.pallas_call(kernel, out_shape=outs, in_specs=in_specs or [VMEM] * len(...]
  transfers between devices with their start and end apart: 26 -> 26, of which waited for: 11 -> 11; matrix products, arithmetic and copies ran while one was open for 0% -> 0% of each run, Pallas kernels for 18% -> 19%
where the time goes in v4:
time: 85.9 us; the launch traced here: 85.6 us
  starting transfers between devices  32.2 us (37%)
  waiting for transfers between devices  28.4 us (33%)
  Pallas kernels  20.7 us (24%)
  local copies, waits for them, and re-layouts  3.1 us (4%)
  between operations  0.89 us (1%)
    ppermute x26, starting transfers between devices, swap(): return lax.ppermute(block, axes, route)  32.2 us
    ppermute x26, waiting for transfers between devices, swap(): return lax.ppermute(block, axes, route)  28.4 us
    pallas_call x17, Pallas kernels, call(): pl.pallas_call(kernel, out_shape=outs, in_specs=in_specs or [VMEM] * len(...  20.7 us
    unnamed x12, local copies, waits for them, and re-layouts  3.04 us
  transfers between devices with their start and end apart: 26, of which 11 were waited for; matrix products, arithmetic and copies ran while one was open for 0% of the time, Pallas kernels for 19%

profile of v4, /device:TPU:0, one launch (start us, length us, event | category | flops | bytes accessed | tf_op | source)
XLA Modules:
  0.0 85.6 jit_solution(5053048223235649230)
XLA Ops:
  0.6 3.1 %collective-permute-start = (bf16[256,768]{1,0:T(8,128)(2,1)}, bf16[256,768]{1,0:T(8,128)(2,1)S(1)}, u32[]{:S(2)}, u32[]{:S(2)}) collective-permute-start(bf16[256,768]{1,0:T(8,128)(2,1)} %refs_0_.1), channel_id=1, source_target_pairs={{0,1},{1,0},{2,3},{3,2},{4,6},{5,7},{6,4},{7,5},{8,9},{9,8},{10,11... | collective-permute-start | bytes 1179656 | tf_op jit(solution)/shard_map/ppermute | solution.py:24
  3.7 2.6 %collective-permute-start.1 = (bf16[256,768]{1,0:T(8,128)(2,1)}, bf16[256,768]{1,0:T(8,128)(2,1)S(1)}, u32[]{:S(2)}, u32[]{:S(2)}) collective-permute-start(bf16[256,768]{1,0:T(8,128)(2,1)} %refs_0_.1), channel_id=1, source_target_pairs={{0,2},{1,3},{2,0},{3,1},{4,5},{5,4},{6,7},{7,6},{8,10},{9,11},{10,... | collective-permute-start | bytes 1179656 | tf_op jit(solution)/shard_map/ppermute | solution.py:24
  6.3 1.0 %copy-done = bf16[256,768]{1,0:T(8,128)(2,1)S(1)} copy-done((bf16[256,768]{1,0:T(8,128)(2,1)S(1)}, bf16[256,768]{1,0:T(8,128)(2,1)}, u32[]{:S(2)}) %copy-start) | copy-done | bytes 393240
  7.4 1.0 %copy-done.2 = bf16[768,256]{1,0:T(8,128)(2,1)S(1)} copy-done((bf16[768,256]{1,0:T(8,128)(2,1)S(1)}, bf16[768,256]{1,0:T(8,128)(2,1)}, u32[]{:S(2)}) %copy-start.2) | copy-done | bytes 393240
  8.4 0.3 shard_map.87
  8.6 0.5 collective-permute-start.2
  9.2 1.0 %copy-done.1 = bf16[256,768]{1,0:T(8,128)(2,1)S(1)} copy-done((bf16[256,768]{1,0:T(8,128)(2,1)S(1)}, bf16[256,768]{1,0:T(8,128)(2,1)}, u32[]{:S(2)}) %copy-start.1) | copy-done | bytes 393240
  10.1 5.2 %shard_map.84 = (f32[256,3072]{1,0:T(8,128)S(1)}, bf16[3,768,3072]{2,1,0:T(8,128)(2,1)S(1)}) custom-call(s32[1]{0:T(128)} %bitcast.device_ref, bf16[256,768]{1,0:T(8,128)(2,1)S(1)} %copy-done.1, bf16[3,768,3072]{2,1,0:T(8,128)(2,1)} %b_ref.1), custom_call_target="tpu_custom_call" | custom-call | flops 1207959552 | bytes 3981312 | tf_op jit(solution)/shard_map/pallas_call | solution.py:51
  15.4 9.5 %collective-permute-done.2.got_ref = bf16[256,256]{1,0:T(8,128)(2,1)S(1)} collective-permute-done((bf16[256,256]{1,0:T(8,128)(2,1)S(1)}, bf16[256,256]{1,0:T(8,128)(2,1)S(1)}, u32[]{:S(2)}, u32[]{:S(2)}) %collective-permute-start.2) | collective-permute-done | bytes 131104 | tf_op jit(solution)/shard_map/ppermute | solution.py:24
  24.9 2.2 %collective-permute-start.3 = (bf16[256,256]{1,0:T(8,128)(2,1)S(1)}, bf16[256,256]{1,0:T(8,128)(2,1)S(1)}, u32[]{:S(2)}, u32[]{:S(2)}) collective-permute-start(bf16[256,256]{1,0:T(8,128)(2,1)S(1)} %get-tuple-element.29), channel_id=1, source_target_pairs={{0,2},{1,3},{2,0},{3,1},{4,5},{5,4},{6,7},{7,6},{8,10},{9,11},{10,... | collective-permute-start | bytes 393224 | tf_op jit(solution)/shard_map/ppermute | solution.py:24
  27.1 1.4 %shard_map.85.running_ref = f32[256,3072]{1,0:T(8,128)S(1)} custom-call(s32[1]{0:T(128)} %bitcast.device_ref, bf16[3,768,3072]{2,1,0:T(8,128)(2,1)S(1)} %get-tuple-element.24.b_ref, f32[256,3072]{1,0:T(8,128)S(1)} %get-tuple-element.25.running_ref, bf16[256,768]{1,0:T(8,128)(2,1)S(1)} %collective-permute-done.refs_0_), custom_call_target="tpu_custom_call" | custom-call | flops 1207959552 | bytes 2605056 | tf_op jit(solution)/shard_map/pallas_call | solution.py:51
  28.6 1.4 %shard_map.86.pre_ref = f32[256,3072]{1,0:T(8,128)S(1)} custom-call(s32[1]{0:T(128)} %bitcast.device_ref, bf16[3,768,3072]{2,1,0:T(8,128)(2,1)S(1)} %get-tuple-element.24.b_ref, f32[256,3072]{1,0:T(8,128)S(1)} %shard_map.85.running_ref, bf16[256,768]{1,0:T(8,128)(2,1)S(1)} %collective-permute-done.1.refs_0_), custom_call_target="tpu_custom_call" | custom-call | flops 1207959552 | bytes 2605056 | tf_op jit(solution)/shard_map/pallas_call | solution.py:51
  30.1 0.8 collective-permute-done.3.got_ref
  30.9 3.8 %shard_map.89 = (bf16[256,3072]{1,0:T(8,128)(2,1)}, bf16[256,3072]{1,0:T(8,128)(2,1)S(1)}, f32[256,256]{1,0:T(8,128)S(1)}, bf16[256,256]{1,0:T(8,128)(2,1)S(1)},...) custom-call(s32[1]{0:T(128)} %bitcast.device_ref, f32[256,3072]{1,0:T(8,128)S(1)} %shard_map.86.pre_ref, ...), custom_call_target="tpu_custom_call" | custom-call | flops 1207959552 | bytes 1572864 | tf_op jit(solution)/shard_map/pallas_call | solution.py:51
  34.8 2.3 %collective-permute-done.9 = bf16[128,3072]{1,0:T(8,128)(2,1)S(1)} collective-permute-done((bf16[128,3072]{1,0:T(8,128)(2,1)S(1)}, bf16[128,3072]{1,0:T(8,128)(2,1)S(1)}, u32[]{:S(2)}, u32[]{:S(2)}) %collective-permute-start.9) | collective-permute-done | bytes 786464 | tf_op jit(solution)/shard_map/ppermute | solution.py:24
  37.0 0.2 convert_add_fusion
  37.2 1.9 %collective-permute-start.10 = (bf16[64,3072]{1,0:T(8,128)(2,1)S(1)}, bf16[64,3072]{1,0:T(8,128)(2,1)S(1)}, u32[]{:S(2)}, u32[]{:S(2)}) collective-permute-start(bf16[64,3072]{1,0:T(8,128)(2,1)S(1)} %slice.30), channel_id=1, source_target_pairs={{0,8},{4,20},{8,0},{12,28},{16,24},{20,4},{24,16},{28,12},{1,9},{5... | collective-permute-start | bytes 1179656 | tf_op jit(solution)/shard_map/ppermute | solution.py:24
  39.1 1.9 %collective-permute-start.4 = (bf16[256,256]{1,0:T(8,128)(2,1)S(1)}, bf16[256,256]{1,0:T(8,128)(2,1)S(1)}, u32[]{:S(2)}, u32[]{:S(2)}) collective-permute-start(bf16[256,256]{1,0:T(8,128)(2,1)S(1)} %get-tuple-element.33), channel_id=1, source_target_pairs={{0,1},{1,0},{2,3},{3,2},{4,6},{5,7},{6,4},{7,5},{8,9},{9,8},{10,11... | collective-permute-start | bytes 393224 | tf_op jit(solution)/shard_map/ppermute | solution.py:24
  41.1 1.5 %collective-permute-start.17 = (bf16[256,768]{1,0:T(8,128)(2,1)S(1)}, bf16[256,768]{1,0:T(8,128)(2,1)S(1)}, u32[]{:S(2)}, u32[]{:S(2)}) collective-permute-start(bf16[256,768]{1,0:T(8,128)(2,1)S(1)} %copy-done.1), channel_id=1, source_target_pairs={{0,16},{4,12},{8,24},{12,4},{16,0},{20,28},{24,8},{28,20},{1,17},{... | collective-permute-start | bytes 1179656 | tf_op jit(solution)/shard_map/ppermute | solution.py:24
  42.6 0.5 collective-permute-start.18
  43.1 2.2 %collective-permute-done.4.got_ref = bf16[256,256]{1,0:T(8,128)(2,1)S(1)} collective-permute-done((bf16[256,256]{1,0:T(8,128)(2,1)S(1)}, bf16[256,256]{1,0:T(8,128)(2,1)S(1)}, u32[]{:S(2)}, u32[]{:S(2)}) %collective-permute-start.4) | collective-permute-done | bytes 131104 | tf_op jit(solution)/shard_map/ppermute | solution.py:24
  45.4 2.0 %collective-permute-start.5 = (bf16[256,256]{1,0:T(8,128)(2,1)S(1)}, bf16[256,256]{1,0:T(8,128)(2,1)S(1)}, u32[]{:S(2)}, u32[]{:S(2)}) collective-permute-start(bf16[256,256]{1,0:T(8,128)(2,1)S(1)} %get-tuple-element.35), channel_id=1, source_target_pairs={{0,2},{1,3},{2,0},{3,1},{4,5},{5,4},{6,7},{7,6},{8,10},{9,11},{10,... | collective-permute-start | bytes 393224 | tf_op jit(solution)/shard_map/ppermute | solution.py:24
  47.5 2.9 %collective-permute-start.11 = (bf16[32,3072]{1,0:T(8,128)(2,1)S(1)}, bf16[32,3072]{1,0:T(8,128)(2,1)S(1)}, u32[]{:S(2)}, u32[]{:S(2)}) collective-permute-start(bf16[32,3072]{1,0:T(8,128)(2,1)S(1)} %slice.31), channel_id=1, source_target_pairs={{0,16},{4,12},{8,24},{12,4},{16,0},{20,28},{24,8},{28,20},{1,17},{... | collective-permute-start | bytes 589832 | tf_op jit(solution)/shard_map/ppermute | solution.py:24
  50.3 1.4 %shard_map.94 = bf16[256,768]{1,0:T(8,128)(2,1)S(1)} custom-call(s32[1]{0:T(128)} %bitcast.device_ref, bf16[256,3072]{1,0:T(8,128)(2,1)S(1)} %get-tuple-element.31.s_ref, bf16[3,768,3072]{2,1,0:T(8,128)(2,1)S(1)} %get-tuple-element.24.b_ref), custom_call_target="tpu_custom_call" | custom-call | flops 1207959552 | bytes 2015232 | tf_op jit(solution)/shard_map/pallas_call | solution.py:51
  51.8 2.9 %collective-permute-start.8 = (bf16[256,768]{1,0:T(8,128)(2,1)S(1)}, bf16[256,768]{1,0:T(8,128)(2,1)S(1)}, u32[]{:S(2)}, u32[]{:S(2)}) collective-permute-start(bf16[256,768]{1,0:T(8,128)(2,1)S(1)} %shard_map.94), channel_id=1, source_target_pairs={{0,2},{1,3},{2,0},{3,1},{4,5},{5,4},{6,7},{7,6},{8,10},{9,11},{10,... | collective-permute-start | bytes 1179656 | tf_op jit(solution)/shard_map/ppermute | solution.py:24
  54.7 1.4 %shard_map.93 = (bf16[128,768]{1,0:T(8,128)(2,1)S(1)}, bf16[128,768]{1,0:T(8,128)(2,1)S(1)}) custom-call(s32[1]{0:T(128)} %bitcast.device_ref, bf16[256,3072]{1,0:T(8,128)(2,1)S(1)} %get-tuple-element.31.s_ref, bf16[3,768,3072]{2,1,0:T(8,128)(2,1)S(1)} %get-tuple-element.24.b_ref), custom_call_target="tpu_custom_call" | custom-call | flops 1207959552 | bytes 2015232 | tf_op jit(solution)/shard_map/pallas_call | solution.py:51
  56.1 2.2 %collective-permute-start.6 = (bf16[128,768]{1,0:T(8,128)(2,1)S(1)}, bf16[128,768]{1,0:T(8,128)(2,1)S(1)}, u32[]{:S(2)}, u32[]{:S(2)}) collective-permute-start(bf16[128,768]{1,0:T(8,128)(2,1)S(1)} %get-tuple-element.36), channel_id=1, source_target_pairs={{0,1},{1,0},{2,3},{3,2},{4,6},{5,7},{6,4},{7,5},{8,9},{9,8},{10,11... | collective-permute-start | bytes 589832 | tf_op jit(solution)/shard_map/ppermute | solution.py:24
  58.3 1.5 %collective-permute-start.19 = (bf16[256,768]{1,0:T(8,128)(2,1)S(1)}, bf16[256,768]{1,0:T(8,128)(2,1)S(1)}, u32[]{:S(2)}, u32[]{:S(2)}) collective-permute-start(bf16[256,768]{1,0:T(8,128)(2,1)S(1)} %collective-permute-done.17.refs_1_), channel_id=1, source_target_pairs={{0,8},{4,20},{8,0},{12,28},{16,24},{20,4},{24,16},{28,12},{1,9},{5... | collective-permute-start | bytes 1179656 | tf_op jit(solution)/shard_map/ppermute | solution.py:24
  60.0 2.1 %collective-permute-start.12 = (bf16[32,3072]{1,0:T(8,128)(2,1)S(1)}, bf16[32,3072]{1,0:T(8,128)(2,1)S(1)}, u32[]{:S(2)}, u32[]{:S(2)}) collective-permute-start(bf16[32,3072]{1,0:T(8,128)(2,1)S(1)} %fusion.1.refs_0_), channel_id=1, source_target_pairs={{0,16},{4,12},{8,24},{12,4},{16,0},{20,28},{24,8},{28,20},{1,17},{... | collective-permute-start | bytes 589832 | tf_op jit(solution)/shard_map/ppermute | solution.py:24
  62.0 4.2 %collective-permute-done.20.refs_1_ = bf16[256,256]{1,0:T(8,128)(2,1)S(1)} collective-permute-done((bf16[256,256]{1,0:T(8,128)(2,1)S(1)}, bf16[256,256]{1,0:T(8,128)(2,1)S(1)}, u32[]{:S(2)}, u32[]{:S(2)}) %collective-permute-start.20) | collective-permute-done | bytes 131104 | tf_op jit(solution)/shard_map/ppermute | solution.py:24
  66.3 0.4 collective-permute-start.21
  66.6 0.4 collective-permute-done.19.refs_0_
  67.1 1.2 %collective-permute-start.22 = (bf16[256,256]{1,0:T(8,128)(2,1)S(1)}, bf16[256,256]{1,0:T(8,128)(2,1)S(1)}, u32[]{:S(2)}, u32[]{:S(2)}) collective-permute-start(bf16[256,256]{1,0:T(8,128)(2,1)S(1)} %collective-permute-done.20.refs_1_), channel_id=1, source_target_pairs={{0,8},{4,20},{8,0},{12,28},{16,24},{20,4},{24,16},{28,12},{1,9},{5... | collective-permute-start | bytes 393224 | tf_op jit(solution)/shard_map/ppermute | solution.py:24
  68.3 0.4 shard_map.97.early_ref
  68.7 0.2 shard_map.98.late_ref
  68.8 2.4 %collective-permute-done.21.refs_2_ = bf16[256,256]{1,0:T(8,128)(2,1)S(1)} collective-permute-done((bf16[256,256]{1,0:T(8,128)(2,1)S(1)}, bf16[256,256]{1,0:T(8,128)(2,1)S(1)}, u32[]{:S(2)}, u32[]{:S(2)}) %collective-permute-start.21) | collective-permute-done | bytes 131104 | tf_op jit(solution)/shard_map/ppermute | solution.py:24
  71.2 1.4 %collective-permute-done.22.refs_3_ = bf16[256,256]{1,0:T(8,128)(2,1)S(1)} collective-permute-done((bf16[256,256]{1,0:T(8,128)(2,1)S(1)}, bf16[256,256]{1,0:T(8,128)(2,1)S(1)}, u32[]{:S(2)}, u32[]{:S(2)}) %collective-permute-start.22) | collective-permute-done | bytes 131104 | tf_op jit(solution)/shard_map/ppermute | solution.py:24
  72.6 0.6 shard_map.99
  73.2 0.7 collective-permute-start.13
  73.9 1.5 %collective-permute-start.24 = (bf16[32,3072]{1,0:T(8,128)(2,1)S(1)}, bf16[32,3072]{1,0:T(8,128)(2,1)S(1)}, u32[]{:S(2)}, u32[]{:S(2)}) collective-permute-start(bf16[32,3072]{1,0:T(8,128)(2,1)S(1)} %collective-permute-done.12.refs_1_), channel_id=1, source_target_pairs={{0,8},{4,20},{8,0},{12,28},{16,24},{20,4},{24,16},{28,12},{1,9},{5... | collective-permute-start | bytes 589832 | tf_op jit(solution)/shard_map/ppermute | solution.py:24
  75.4 1.5 %collective-permute-done.7.refs_1_ = bf16[128,768]{1,0:T(8,128)(2,1)S(1)} collective-permute-done((bf16[128,768]{1,0:T(8,128)(2,1)S(1)}, bf16[128,768]{1,0:T(8,128)(2,1)S(1)}, u32[]{:S(2)}, u32[]{:S(2)}) %collective-permute-start.7) | collective-permute-done | bytes 196640 | tf_op jit(solution)/shard_map/ppermute | solution.py:24
  76.9 0.5 collective-permute-start.15
  77.4 1.5 %collective-permute-done.13.refs_2_ = bf16[32,3072]{1,0:T(8,128)(2,1)S(1)} collective-permute-done((bf16[32,3072]{1,0:T(8,128)(2,1)S(1)}, bf16[32,3072]{1,0:T(8,128)(2,1)S(1)}, u32[]{:S(2)}, u32[]{:S(2)}) %collective-permute-start.13) | collective-permute-done | bytes 196640 | tf_op jit(solution)/shard_map/ppermute | solution.py:24
  78.9 2.1 %collective-permute-done.24.refs_0_ = bf16[32,3072]{1,0:T(8,128)(2,1)S(1)} collective-permute-done((bf16[32,3072]{1,0:T(8,128)(2,1)S(1)}, bf16[32,3072]{1,0:T(8,128)(2,1)S(1)}, u32[]{:S(2)}, u32[]{:S(2)}) %collective-permute-start.24) | collective-permute-done | bytes 196640 | tf_op jit(solution)/shard_map/ppermute | solution.py:24
  81.1 1.4 %shard_map.90.own_ref = f32[256,768]{1,0:T(8,128)S(1)} custom-call(s32[1]{0:T(128)} %bitcast.device_ref, bf16[256,3072]{1,0:T(8,128)(2,1)S(1)} %get-tuple-element.31.s_ref, bf16[3,768,3072]{2,1,0:T(8,128)(2,1)S(1)} %get-tuple-element.24.b_ref), custom_call_target="tpu_custom_call" | custom-call | flops 1207959552 | bytes 2064384 | tf_op jit(solution)/shard_map/pallas_call | solution.py:51
  82.5 1.1 %shard_map.95 = bf16[256,768]{1,0:T(8,128)(2,1)} custom-call(f32[256,768]{1,0:T(8,128)S(1)} %shard_map.90.own_ref, bf16[256,256]{1,0:T(8,128)(2,1)S(1)} %shard_map.92.mixed_ref.refs_0_, bf16[768,256]{1,0:T(8,128)(2,1)S(1)} %copy-done.3, bf16[128,768]{1,0:T(8,128)(2,1)S(1)} %collective-permute-done.6.refs_0_, ...), custom_call_target="tpu_custom_call" | custom-call | flops 100663296 | bytes 311296 | tf_op jit(solution)/shard_map/pallas_call | solution.py:51
  83.6 1.1 %shard_map.96.placed_ref = bf16[256,3072]{1,0:T(8,128)(2,1)} custom-call(s32[1]{0:T(128)} %bitcast.device_ref, bf16[32,3072]{1,0:T(8,128)(2,1)S(1)} %fusion.1.refs_0_, bf16[32,3072]{1,0:T(8,128)(2,1)S(1)} %collective-permute-done.12.refs_1_, bf16[32,3072]{1,0:T(8,128)(2,1)S(1)} %collective-permute-done.13.refs_2_, ...), custom_call_target="tpu_custom_call" | custom-call | bytes 344064 | tf_op jit(solution)/shard_map/pallas_call | solution.py:51
  84.7 0.9 %shard_map.100 = (bf16[256,3072]{1,0:T(8,128)(2,1)}, bf16[768,256]{1,0:T(8,128)(2,1)}) custom-call(s32[1]{0:T(128)} %bitcast.device_ref, bf16[256,3072]{1,0:T(8,128)(2,1)} %shard_map.96.placed_ref, f32[768,256]{1,0:T(8,128)S(1)} %get-tuple-element.40.total_ref, ...), custom_call_target="tpu_custom_call", output_to_operand_aliasing={{0}: (1, {})} | custom-call | bytes 638976 | tf_op jit(solution)/shard_map/pallas_call | solution.py:51
  (38 shorter events, 0.5 us)
Async XLA Ops:
  0.6 26.5 %collective-permute-start = (bf16[256,768]{1,0:T(8,128)(2,1)}, bf16[256,768]{1,0:T(8,128)(2,1)S(1)}, u32[]{:S(2)}, u32[]{:S(2)}) collective-permute-start(bf16[256,768]{1,0:T(8,128)(2,1)} %refs_0_.1), channel_id=1, source_target_pairs={{0,1},{1,0},{2,3},{3,2},{4,6},{5,7},{6,4},{7,5},{8,9},{9,8},{10,11... | collective-permute-start | bytes 1179656 | tf_op jit(solution)/shard_map/ppermute | solution.py:24
  3.7 24.9 %collective-permute-start.1 = (bf16[256,768]{1,0:T(8,128)(2,1)}, bf16[256,768]{1,0:T(8,128)(2,1)S(1)}, u32[]{:S(2)}, u32[]{:S(2)}) collective-permute-start(bf16[256,768]{1,0:T(8,128)(2,1)} %refs_0_.1), channel_id=1, source_target_pairs={{0,2},{1,3},{2,0},{3,1},{4,5},{5,4},{6,7},{7,6},{8,10},{9,11},{10,... | collective-permute-start | bytes 1179656 | tf_op jit(solution)/shard_map/ppermute | solution.py:24
  6.3 1.0 %copy-start = (bf16[256,768]{1,0:T(8,128)(2,1)S(1)}, bf16[256,768]{1,0:T(8,128)(2,1)}, u32[]{:S(2)}) copy-start(bf16[256,768]{1,0:T(8,128)(2,1)} %refs_0_.1) | copy-start | bytes 1179652
  7.4 1.0 %copy-start.2 = (bf16[768,256]{1,0:T(8,128)(2,1)S(1)}, bf16[768,256]{1,0:T(8,128)(2,1)}, u32[]{:S(2)}) copy-start(bf16[768,256]{1,0:T(8,128)(2,1)} %left_ref.3) | copy-start | bytes 1179652
  8.6 16.2 %collective-permute-start.2 = (bf16[256,256]{1,0:T(8,128)(2,1)S(1)}, bf16[256,256]{1,0:T(8,128)(2,1)S(1)}, u32[]{:S(2)}, u32[]{:S(2)}) collective-permute-start(bf16[256,256]{1,0:T(8,128)(2,1)S(1)} %get-tuple-element.27), channel_id=1, source_target_pairs={{0,1},{1,0},{2,3},{3,2},{4,6},{5,7},{6,4},{7,5},{8,9},{9,8},{10,11... | collective-permute-start | bytes 393224 | tf_op jit(solution)/shard_map/ppermute | solution.py:24
  9.2 1.0 %copy-start.1 = (bf16[256,768]{1,0:T(8,128)(2,1)S(1)}, bf16[256,768]{1,0:T(8,128)(2,1)}, u32[]{:S(2)}) copy-start(bf16[256,768]{1,0:T(8,128)(2,1)} %refs_0_.1) | copy-start | bytes 1179652
  24.9 6.0 %collective-permute-start.3 = (bf16[256,256]{1,0:T(8,128)(2,1)S(1)}, bf16[256,256]{1,0:T(8,128)(2,1)S(1)}, u32[]{:S(2)}, u32[]{:S(2)}) collective-permute-start(bf16[256,256]{1,0:T(8,128)(2,1)S(1)} %get-tuple-element.29), channel_id=1, source_target_pairs={{0,2},{1,3},{2,0},{3,1},{4,5},{5,4},{6,7},{7,6},{8,10},{9,11},{10,... | collective-permute-start | bytes 393224 | tf_op jit(solution)/shard_map/ppermute | solution.py:24
  28.6 2.3 %copy-start.4 = (bf16[256,3072]{1,0:T(8,128)(2,1)S(1)}, bf16[256,3072]{1,0:T(8,128)(2,1)}, u32[]{:S(2)}) copy-start(bf16[256,3072]{1,0:T(8,128)(2,1)} %right_ref.1) | copy-start | bytes 4718596
  28.6 2.3 %copy-start.5 = (bf16[256,3072]{1,0:T(8,128)(2,1)S(1)}, bf16[256,3072]{1,0:T(8,128)(2,1)}, u32[]{:S(2)}) copy-start(bf16[256,3072]{1,0:T(8,128)(2,1)} %up_ref.1) | copy-start | bytes 4718596
  34.7 2.3 %collective-permute-start.9 = (bf16[128,3072]{1,0:T(8,128)(2,1)S(1)}, bf16[128,3072]{1,0:T(8,128)(2,1)S(1)}, u32[]{:S(2)}, u32[]{:S(2)}) collective-permute-start(bf16[128,3072]{1,0:T(8,128)(2,1)S(1)} %get-tuple-element.39), channel_id=1, source_target_pairs={{0,4},{4,0},{8,12},{12,8},{16,20},{20,16},{24,28},{28,24},{1,5},{5... | collective-permute-start | bytes 2359304 | tf_op jit(solution)/shard_map/ppermute | solution.py:24
  37.2 10.1 %collective-permute-start.10 = (bf16[64,3072]{1,0:T(8,128)(2,1)S(1)}, bf16[64,3072]{1,0:T(8,128)(2,1)S(1)}, u32[]{:S(2)}, u32[]{:S(2)}) collective-permute-start(bf16[64,3072]{1,0:T(8,128)(2,1)S(1)} %slice.30), channel_id=1, source_target_pairs={{0,8},{4,20},{8,0},{12,28},{16,24},{20,4},{24,16},{28,12},{1,9},{5... | collective-permute-start | bytes 1179656 | tf_op jit(solution)/shard_map/ppermute | solution.py:24
  39.1 6.2 %collective-permute-start.4 = (bf16[256,256]{1,0:T(8,128)(2,1)S(1)}, bf16[256,256]{1,0:T(8,128)(2,1)S(1)}, u32[]{:S(2)}, u32[]{:S(2)}) collective-permute-start(bf16[256,256]{1,0:T(8,128)(2,1)S(1)} %get-tuple-element.33), channel_id=1, source_target_pairs={{0,1},{1,0},{2,3},{3,2},{4,6},{5,7},{6,4},{7,5},{8,9},{9,8},{10,11... | collective-permute-start | bytes 393224 | tf_op jit(solution)/shard_map/ppermute | solution.py:24
  41.1 15.1 %collective-permute-start.17 = (bf16[256,768]{1,0:T(8,128)(2,1)S(1)}, bf16[256,768]{1,0:T(8,128)(2,1)S(1)}, u32[]{:S(2)}, u32[]{:S(2)}) collective-permute-start(bf16[256,768]{1,0:T(8,128)(2,1)S(1)} %copy-done.1), channel_id=1, source_target_pairs={{0,16},{4,12},{8,24},{12,4},{16,0},{20,28},{24,8},{28,20},{1,17},{... | collective-permute-start | bytes 1179656 | tf_op jit(solution)/shard_map/ppermute | solution.py:24
  42.6 17.4 %collective-permute-start.18 = (bf16[256,768]{1,0:T(8,128)(2,1)S(1)}, bf16[256,768]{1,0:T(8,128)(2,1)S(1)}, u32[]{:S(2)}, u32[]{:S(2)}) collective-permute-start(bf16[256,768]{1,0:T(8,128)(2,1)S(1)} %copy-done.1), channel_id=1, source_target_pairs={{0,8},{4,20},{8,0},{12,28},{16,24},{20,4},{24,16},{28,12},{1,9},{5... | collective-permute-start | bytes 1179656 | tf_op jit(solution)/shard_map/ppermute | solution.py:24
  45.4 12.9 %collective-permute-start.5 = (bf16[256,256]{1,0:T(8,128)(2,1)S(1)}, bf16[256,256]{1,0:T(8,128)(2,1)S(1)}, u32[]{:S(2)}, u32[]{:S(2)}) collective-permute-start(bf16[256,256]{1,0:T(8,128)(2,1)S(1)} %get-tuple-element.35), channel_id=1, source_target_pairs={{0,2},{1,3},{2,0},{3,1},{4,5},{5,4},{6,7},{7,6},{8,10},{9,11},{10,... | collective-permute-start | bytes 393224 | tf_op jit(solution)/shard_map/ppermute | solution.py:24
  47.5 12.3 %collective-permute-start.11 = (bf16[32,3072]{1,0:T(8,128)(2,1)S(1)}, bf16[32,3072]{1,0:T(8,128)(2,1)S(1)}, u32[]{:S(2)}, u32[]{:S(2)}) collective-permute-start(bf16[32,3072]{1,0:T(8,128)(2,1)S(1)} %slice.31), channel_id=1, source_target_pairs={{0,16},{4,12},{8,24},{12,4},{16,0},{20,28},{24,8},{28,20},{1,17},{... | collective-permute-start | bytes 589832 | tf_op jit(solution)/shard_map/ppermute | solution.py:24
  51.8 25.1 %collective-permute-start.8 = (bf16[256,768]{1,0:T(8,128)(2,1)S(1)}, bf16[256,768]{1,0:T(8,128)(2,1)S(1)}, u32[]{:S(2)}, u32[]{:S(2)}) collective-permute-start(bf16[256,768]{1,0:T(8,128)(2,1)S(1)} %shard_map.94), channel_id=1, source_target_pairs={{0,2},{1,3},{2,0},{3,1},{4,5},{5,4},{6,7},{7,6},{8,10},{9,11},{10,... | collective-permute-start | bytes 1179656 | tf_op jit(solution)/shard_map/ppermute | solution.py:24
  56.1 17.8 %collective-permute-start.6 = (bf16[128,768]{1,0:T(8,128)(2,1)S(1)}, bf16[128,768]{1,0:T(8,128)(2,1)S(1)}, u32[]{:S(2)}, u32[]{:S(2)}) collective-permute-start(bf16[128,768]{1,0:T(8,128)(2,1)S(1)} %get-tuple-element.36), channel_id=1, source_target_pairs={{0,1},{1,0},{2,3},{3,2},{4,6},{5,7},{6,4},{7,5},{8,9},{9,8},{10,11... | collective-permute-start | bytes 589832 | tf_op jit(solution)/shard_map/ppermute | solution.py:24
  58.3 8.8 %collective-permute-start.19 = (bf16[256,768]{1,0:T(8,128)(2,1)S(1)}, bf16[256,768]{1,0:T(8,128)(2,1)S(1)}, u32[]{:S(2)}, u32[]{:S(2)}) collective-permute-start(bf16[256,768]{1,0:T(8,128)(2,1)S(1)} %collective-permute-done.17.refs_1_), channel_id=1, source_target_pairs={{0,8},{4,20},{8,0},{12,28},{16,24},{20,4},{24,16},{28,12},{1,9},{5... | collective-permute-start | bytes 1179656 | tf_op jit(solution)/shard_map/ppermute | solution.py:24
  59.8 6.4 %collective-permute-start.20 = (bf16[256,256]{1,0:T(8,128)(2,1)S(1)}, bf16[256,256]{1,0:T(8,128)(2,1)S(1)}, u32[]{:S(2)}, u32[]{:S(2)}) collective-permute-start(bf16[256,256]{1,0:T(8,128)(2,1)S(1)} %shard_map.92.mixed_ref.refs_0_), channel_id=1, source_target_pairs={{0,16},{4,12},{8,24},{12,4},{16,0},{20,28},{24,8},{28,20},{1,17},{... | collective-permute-start | bytes 393224 | tf_op jit(solution)/shard_map/ppermute | solution.py:24
  60.0 13.9 %collective-permute-start.12 = (bf16[32,3072]{1,0:T(8,128)(2,1)S(1)}, bf16[32,3072]{1,0:T(8,128)(2,1)S(1)}, u32[]{:S(2)}, u32[]{:S(2)}) collective-permute-start(bf16[32,3072]{1,0:T(8,128)(2,1)S(1)} %fusion.1.refs_0_), channel_id=1, source_target_pairs={{0,16},{4,12},{8,24},{12,4},{16,0},{20,28},{24,8},{28,20},{1,17},{... | collective-permute-start | bytes 589832 | tf_op jit(solution)/shard_map/ppermute | solution.py:24
  66.3 5.0 %collective-permute-start.21 = (bf16[256,256]{1,0:T(8,128)(2,1)S(1)}, bf16[256,256]{1,0:T(8,128)(2,1)S(1)}, u32[]{:S(2)}, u32[]{:S(2)}) collective-permute-start(bf16[256,256]{1,0:T(8,128)(2,1)S(1)} %shard_map.92.mixed_ref.refs_0_), channel_id=1, source_target_pairs={{0,8},{4,20},{8,0},{12,28},{16,24},{20,4},{24,16},{28,12},{1,9},{5... | collective-permute-start | bytes 393224 | tf_op jit(solution)/shard_map/ppermute | solution.py:24
  67.1 5.6 %collective-permute-start.22 = (bf16[256,256]{1,0:T(8,128)(2,1)S(1)}, bf16[256,256]{1,0:T(8,128)(2,1)S(1)}, u32[]{:S(2)}, u32[]{:S(2)}) collective-permute-start(bf16[256,256]{1,0:T(8,128)(2,1)S(1)} %collective-permute-done.20.refs_1_), channel_id=1, source_target_pairs={{0,8},{4,20},{8,0},{12,28},{16,24},{20,4},{24,16},{28,12},{1,9},{5... | collective-permute-start | bytes 393224 | tf_op jit(solution)/shard_map/ppermute | solution.py:24
  71.2 5.7 %collective-permute-start.7 = (bf16[128,768]{1,0:T(8,128)(2,1)S(1)}, bf16[128,768]{1,0:T(8,128)(2,1)S(1)}, u32[]{:S(2)}, u32[]{:S(2)}) collective-permute-start(bf16[128,768]{1,0:T(8,128)(2,1)S(1)} %get-tuple-element.37), channel_id=1, source_target_pairs={{0,1},{1,0},{2,3},{3,2},{4,6},{5,7},{6,4},{7,5},{8,9},{9,8},{10,11... | collective-permute-start | bytes 589832 | tf_op jit(solution)/shard_map/ppermute | solution.py:24
  73.2 5.7 %collective-permute-start.13 = (bf16[32,3072]{1,0:T(8,128)(2,1)S(1)}, bf16[32,3072]{1,0:T(8,128)(2,1)S(1)}, u32[]{:S(2)}, u32[]{:S(2)}) collective-permute-start(bf16[32,3072]{1,0:T(8,128)(2,1)S(1)} %fusion.1.refs_0_), channel_id=1, source_target_pairs={{0,8},{4,20},{8,0},{12,28},{16,24},{20,4},{24,16},{28,12},{1,9},{5... | collective-permute-start | bytes 589832 | tf_op jit(solution)/shard_map/ppermute | solution.py:24
  73.9 8.6 %copy-start.3 = (bf16[768,256]{1,0:T(8,128)(2,1)S(1)}, bf16[768,256]{1,0:T(8,128)(2,1)}, u32[]{:S(2)}) copy-start(bf16[768,256]{1,0:T(8,128)(2,1)} %left_ref.3) | copy-start | bytes 1179652
  73.9 10.8 %collective-permute-start.23 = (bf16[768,256]{1,0:T(8,128)(2,1)S(1)}, bf16[768,256]{1,0:T(8,128)(2,1)S(1)}, u32[]{:S(2)}, u32[]{:S(2)}) collective-permute-start(bf16[768,256]{1,0:T(8,128)(2,1)S(1)} %get-tuple-element.41), channel_id=1, source_target_pairs={{0,4},{4,0},{8,12},{12,8},{16,20},{20,16},{24,28},{28,24},{1,5},{5... | collective-permute-start | bytes 1179656 | tf_op jit(solution)/shard_map/ppermute | solution.py:24
  73.9 7.1 %collective-permute-start.24 = (bf16[32,3072]{1,0:T(8,128)(2,1)S(1)}, bf16[32,3072]{1,0:T(8,128)(2,1)S(1)}, u32[]{:S(2)}, u32[]{:S(2)}) collective-permute-start(bf16[32,3072]{1,0:T(8,128)(2,1)S(1)} %collective-permute-done.12.refs_1_), channel_id=1, source_target_pairs={{0,8},{4,20},{8,0},{12,28},{16,24},{20,4},{24,16},{28,12},{1,9},{5... | collective-permute-start | bytes 589832 | tf_op jit(solution)/shard_map/ppermute | solution.py:24
  76.9 6.7 %collective-permute-start.14 = (bf16[32,3072]{1,0:T(8,128)(2,1)S(1)}, bf16[32,3072]{1,0:T(8,128)(2,1)S(1)}, u32[]{:S(2)}, u32[]{:S(2)}) collective-permute-start(bf16[32,3072]{1,0:T(8,128)(2,1)S(1)} %fusion.1.refs_0_), channel_id=1, source_target_pairs={{0,4},{4,0},{8,12},{12,8},{16,20},{20,16},{24,28},{28,24},{1,5},{5... | collective-permute-start | bytes 589832 | tf_op jit(solution)/shard_map/ppermute | solution.py:24
  76.9 6.7 %collective-permute-start.15 = (bf16[32,3072]{1,0:T(8,128)(2,1)S(1)}, bf16[32,3072]{1,0:T(8,128)(2,1)S(1)}, u32[]{:S(2)}, u32[]{:S(2)}) collective-permute-start(bf16[32,3072]{1,0:T(8,128)(2,1)S(1)} %collective-permute-done.12.refs_1_), channel_id=1, source_target_pairs={{0,4},{4,0},{8,12},{12,8},{16,20},{20,16},{24,28},{28,24},{1,5},{5... | collective-permute-start | bytes 589832 | tf_op jit(solution)/shard_map/ppermute | solution.py:24
  78.9 4.7 %collective-permute-start.16 = (bf16[32,3072]{1,0:T(8,128)(2,1)S(1)}, bf16[32,3072]{1,0:T(8,128)(2,1)S(1)}, u32[]{:S(2)}, u32[]{:S(2)}) collective-permute-start(bf16[32,3072]{1,0:T(8,128)(2,1)S(1)} %collective-permute-done.13.refs_2_), channel_id=1, source_target_pairs={{0,4},{4,0},{8,12},{12,8},{16,20},{20,16},{24,28},{28,24},{1,5},{5... | collective-permute-start | bytes 589832 | tf_op jit(solution)/shard_map/ppermute | solution.py:24
  81.1 3.6 %collective-permute-start.25 = (bf16[32,3072]{1,0:T(8,128)(2,1)S(1)}, bf16[32,3072]{1,0:T(8,128)(2,1)S(1)}, u32[]{:S(2)}, u32[]{:S(2)}) collective-permute-start(bf16[32,3072]{1,0:T(8,128)(2,1)S(1)} %collective-permute-done.24.refs_0_), channel_id=1, source_target_pairs={{0,4},{4,0},{8,12},{12,8},{16,20},{20,16},{24,28},{28,24},{1,5},{5... | collective-permute-start | bytes 589832 | tf_op jit(solution)/shard_map/ppermute | solution.py:24
